TPU v7x, 32 devices: a whole 2x2x4 slice. The times are simulated.
32 devices in a mesh: expert: 8 (over y, x, core), tensor: 4 (over z).
Axes of the slice: x: 2, y: 2, z: 4, core: 2. Of those that a mesh axis runs over, the one named last changes fastest.
Arguments:
- tokens_in: bfloat16 [2048, 2048], P(('expert', 'tensor')), may hold values from -6 to 6
- out_grad: bfloat16 [2048, 2048], P(('expert', 'tensor')), may hold values from -6 to 6
- routes: int32 [2048, 6], P('expert'), may hold values from 0 to 63, all different within a row; in each aligned block of 256 rows (0 to 255, 256 to 511, ...) at most 30 rows name the same one
- attn_gain: float32 [2048], replicated, may hold values from 0.5 to 1.5
- kv_gain: float32 [512], replicated, may hold values from 0.5 to 1.5
- ffn_gain: float32 [2048], replicated, may hold values from 0.5 to 1.5
- w_query: bfloat16 [2048, 3072], P('expert', 'tensor'), may hold values from -0.125 to 0.125
- w_latent: bfloat16 [2048, 576], replicated, may hold values from -0.125 to 0.125
- w_keyval: bfloat16 [512, 4096], P('expert', 'tensor'), may hold values from -0.25 to 0.25
- w_output: bfloat16 [2048, 2048], P('tensor', 'expert'), may hold values from -0.5 to 0.5
- w_router: bfloat16 [2048, 64], replicated, may hold values from -0.125 to 0.125
- w_shared_in: bfloat16 [2, 2048, 2816], P(None, 'expert', 'tensor'), may hold values from -0.125 to 0.125
- w_shared_out: bfloat16 [2816, 2048], P('tensor', 'expert'), may hold values from -0.109375 to 0.109375
- w_expert_in: bfloat16 [64, 2, 2048, 1408], P('expert', None, None, 'tensor'), may hold values from -0.125 to 0.125
- w_expert_out: bfloat16 [64, 1408, 2048], P('expert', 'tensor'), may hold values from -0.15625 to 0.15625
Outputs:
- block_out: bfloat16 [2048, 2048], P(('expert', 'tensor'))
- grad_in: float32 [2048, 2048], P(('expert', 'tensor'))
- grad_attn_gain: float32 [2048], replicated
- grad_kv_gain: float32 [512], replicated
- grad_ffn_gain: float32 [2048], replicated
- grad_w_query: float32 [2048, 3072], P('expert', 'tensor')
- grad_w_latent: float32 [2048, 576], replicated
- grad_w_keyval: float32 [512, 4096], P('expert', 'tensor')
- grad_w_output: float32 [2048, 2048], P('tensor', 'expert')
- grad_w_router: float32 [2048, 64], replicated
- grad_w_shared_in: float32 [2, 2048, 2816], P(None, 'expert', 'tensor')
- grad_w_shared_out: float32 [2816, 2048], P('tensor', 'expert')
- grad_w_expert_in: float32 [64, 2, 2048, 1408], P('expert', None, None, 'tensor')
- grad_w_expert_out: float32 [64, 1408, 2048], P('expert', 'tensor')
Inputs may be any that keep to these rules, and one draw needn't show every extreme that they name: `routes`: each row names 6 different experts; within each sequence no expert is named by more than 30 rows, a bound that some block reaches.
All inputs are finite; a program needn't handle non-finite values.
Results may differ from a plain program's by a relative error of at most 0.024.
Values may be sent and summed in bfloat16 or wider, within the bound.
No kernel may reach another device: no remote copies, remote signals or barrier semaphores. Data moves between devices by JAX's collectives and lax.ppermute only.
A program may use at most 384 MiB of HBM per device.

v0:
```python
import jax
import jax.numpy as jnp
from jax import lax
from jax.sharding import PartitionSpec as P

NOPE = 128
ROPE = 64
VD = 128
KVR = 512
EXPERTS = 64
TOP = 6


EPSILON = 1e-06
ROUTE_SCALE = 2.446
ROPE_BASE = 50000.0
BLOCK_LIMIT = 512


def mix_dot(left_side, right_side):
    return jnp.dot(left_side, right_side, preferred_element_type=jnp.float32)


def contract(pattern, left_side, right_side):
    return jnp.einsum(pattern, left_side, right_side, preferred_element_type=jnp.float32)


def exact_dot(left_side, right_side):
    return jnp.dot(left_side, right_side, precision=lax.Precision.HIGHEST)


def rms_forward(values, gain_vec):
    inverse = lax.rsqrt(jnp.mean(values * values, axis=-1, keepdims=True) + EPSILON)
    return (values * inverse * gain_vec, inverse)


def rms_backward(values, inverse, gain_vec, grad_normed):
    weighted = grad_normed * gain_vec
    grad_values = inverse * weighted - values * (inverse * inverse * inverse) * jnp.mean(
        values * weighted, axis=-1, keepdims=True
    )
    grad_gain = jnp.sum(grad_normed * values * inverse, axis=0)
    return (grad_values, grad_gain)


def rope_tables(row_count):
    half_rope = ROPE // 2
    position = jnp.arange(row_count).astype(jnp.float32)[:, None]
    frequency = jnp.exp(-jnp.log(ROPE_BASE) * jnp.arange(half_rope).astype(jnp.float32) / half_rope)
    angles = position * frequency[None, :]
    return (jnp.cos(angles), jnp.sin(angles))


def rotate(columns, cosine, sine_table):
    half_rope = columns.shape[-1] // 2
    first_half = columns[..., :half_rope]
    second_half = columns[..., half_rope:]
    return jnp.concatenate(
        [
            first_half * cosine - second_half * sine_table,
            first_half * sine_table + second_half * cosine,
        ],
        axis=-1,
    )


def unrotate(columns, cosine, sine_table):
    half_rope = columns.shape[-1] // 2
    first_half = columns[..., :half_rope]
    second_half = columns[..., half_rope:]
    return jnp.concatenate(
        [
            first_half * cosine + second_half * sine_table,
            second_half * cosine - first_half * sine_table,
        ],
        axis=-1,
    )


def swiglu(gate_part, up_part):
    return jax.nn.silu(gate_part) * up_part


def swiglu_backward(gate_part, up_part, grad_hidden):
    gate_sigmoid = jax.nn.sigmoid(gate_part)
    activation = gate_part * gate_sigmoid
    slope = gate_sigmoid * (1.0 + gate_part * (1.0 - gate_sigmoid))
    return jnp.stack([grad_hidden * up_part * slope, grad_hidden * activation], axis=-2).astype(
        jnp.bfloat16
    )


def score_block(query_rows, key_nope, key_rope, first_row):
    block_rows = query_rows.shape[0]
    key_count = key_nope.shape[0]
    softmax_scale = (NOPE + ROPE) ** (-0.5)
    scores = contract("qhd,khd->hqk", query_rows[..., :NOPE], key_nope) + contract(
        "qhr,kr->hqk", query_rows[..., NOPE:], key_rope
    )
    scores = scores * softmax_scale
    row_ids = first_row + jnp.arange(block_rows, dtype=jnp.int32)
    col_ids = jnp.arange(key_count, dtype=jnp.int32)
    allowed = col_ids[None, :] <= row_ids[:, None]
    return jnp.where(allowed[None], scores, -1e30)


def attend_forward(queries, key_nope, key_rope, values):
    row_count = queries.shape[0]
    block_rows = min(BLOCK_LIMIT, row_count)

    def one_block(block_index):
        first_row = block_index * block_rows
        scores = score_block(queries, key_nope, key_rope, first_row)
        top_score = jnp.max(scores, axis=-1, keepdims=True)
        log_total = top_score + jnp.log(
            jnp.sum(jnp.exp(scores - top_score), axis=-1, keepdims=True)
        )
        soft_low = jnp.exp(scores - log_total).astype(jnp.bfloat16)
        attended = contract("hqk,khv->qhv", soft_low, values).astype(jnp.bfloat16)
        return (attended, log_total[..., 0])

    attended, log_total = lax.map(one_block, jnp.arange(row_count // block_rows, dtype=jnp.int32))
    return (attended.reshape(row_count, queries.shape[1], values.shape[-1]), log_total)


def attend_backward(queries, key_nope, key_rope, values, attended, log_total, grad_attended):
    row_count = queries.shape[0]
    block_rows = min(BLOCK_LIMIT, row_count)
    softmax_scale = (NOPE + ROPE) ** (-0.5)
    start_sums = (
        jnp.zeros(key_nope.shape, jnp.float32),
        jnp.zeros(key_rope.shape, jnp.float32),
        jnp.zeros(values.shape, jnp.float32),
    )

    def one_block(carried, block_index):
        sum_nope, sum_rope, sum_values = carried
        first_row = block_index * block_rows
        scores = score_block(queries, key_nope, key_rope, first_row)
        soft_full = jnp.exp(scores - log_total[block_index][..., None])
        soft_low = soft_full.astype(jnp.bfloat16)
        grad_soft = contract("qhv,khv->hqk", grad_attended, values)
        row_delta = jnp.sum(
            grad_attended.astype(jnp.float32) * attended.astype(jnp.float32), axis=-1
        ).T
        grad_scores = (soft_full * (grad_soft - row_delta[..., None]) * softmax_scale).astype(
            jnp.bfloat16
        )
        grad_query_rows = jnp.concatenate(
            [
                contract("hqk,khd->qhd", grad_scores, key_nope),
                contract("hqk,kr->qhr", grad_scores, key_rope),
            ],
            axis=-1,
        )
        sum_nope = sum_nope + contract("hqk,qhd->khd", grad_scores, queries[..., :NOPE])
        sum_rope = sum_rope + contract("hqk,qhr->kr", grad_scores, queries[..., NOPE:])
        sum_values = sum_values + contract("hqk,qhv->khv", soft_low, grad_attended)
        return ((sum_nope, sum_rope, sum_values), grad_query_rows)

    carried, grad_queries = lax.scan(
        one_block, start_sums, jnp.arange(row_count // block_rows, dtype=jnp.int32)
    )
    return (grad_queries.reshape(row_count, queries.shape[1], queries.shape[2]), carried)


def gate_values(logits, route_rows):
    chosen = route_rows[..., None] == jnp.arange(EXPERTS, dtype=jnp.int32)
    picked = jnp.sum(jnp.where(chosen, logits[:, None, :], 0.0), axis=-1)
    gate_sigmoid = jax.nn.sigmoid(picked)
    gate_total = jnp.sum(gate_sigmoid, axis=-1, keepdims=True)
    return (ROUTE_SCALE * gate_sigmoid / gate_total, gate_sigmoid, gate_total, chosen)


def gate_backward(grad_gate, gate_sigmoid, gate_total, chosen):
    grad_sigmoid = ROUTE_SCALE * (
        grad_gate / gate_total
        - jnp.sum(grad_gate * gate_sigmoid, axis=-1, keepdims=True) / (gate_total * gate_total)
    )
    grad_pick = grad_sigmoid * gate_sigmoid * (1.0 - gate_sigmoid)
    return jnp.sum(jnp.where(chosen, grad_pick[..., None], 0.0), axis=1)


def route_targets(route_rows, capacity):
    flat_routes = route_rows.reshape(-1)
    onehot = (flat_routes[:, None] == jnp.arange(EXPERTS, dtype=jnp.int32)[None, :]).astype(
        jnp.int32
    )
    before = jnp.cumsum(onehot, axis=0) - onehot
    target = flat_routes * capacity + jnp.sum(before * onehot, axis=1)
    pair_count = flat_routes.shape[0]
    slot_owner = (
        jnp.full((EXPERTS * capacity,), pair_count, jnp.int32)
        .at[target]
        .set(jnp.arange(pair_count, dtype=jnp.int32))
    )
    return (target, slot_owner)


def per_device(
    tokens_in,
    out_grad,
    routes,
    attn_gain,
    kv_gain,
    ffn_gain,
    w_query,
    w_latent,
    w_keyval,
    w_output,
    w_router,
    w_shared_in,
    w_shared_out,
    w_expert_in,
    w_expert_out,
):
    group_tokens, group_grad = (
        lax.all_gather(tokens_in, "tensor", axis=0, tiled=True),
        lax.all_gather(out_grad, "tensor", axis=0, tiled=True),
    )
    full_query, full_keyval, full_output, full_shared_in, full_shared_out = (
        lax.all_gather(w_query, "expert", axis=0, tiled=True),
        lax.all_gather(w_keyval, "expert", axis=0, tiled=True),
        lax.all_gather(w_output, "expert", axis=1, tiled=True),
        lax.all_gather(w_shared_in, "expert", axis=1, tiled=True),
        lax.all_gather(w_shared_out, "expert", axis=1, tiled=True),
    )
    row_count = group_tokens.shape[0]
    width = group_tokens.shape[1]
    local_heads = full_query.shape[1] // (NOPE + ROPE)
    cosine, sine_table = rope_tables(row_count)
    stream = group_tokens.astype(jnp.float32)
    normed_one, inverse_one = rms_forward(stream, attn_gain)
    normed_one = normed_one.astype(jnp.bfloat16)
    queries = mix_dot(normed_one, full_query).reshape(row_count, local_heads, NOPE + ROPE)
    queries = jnp.concatenate(
        [
            queries[..., :NOPE],
            rotate(queries[..., NOPE:], cosine[:, None, :], sine_table[:, None, :]),
        ],
        axis=-1,
    ).astype(jnp.bfloat16)
    latent = mix_dot(normed_one, w_latent)
    compressed = latent[:, :KVR]
    comp_normed, comp_inverse = rms_forward(compressed, kv_gain)
    comp_normed = comp_normed.astype(jnp.bfloat16)
    key_rope = rotate(latent[:, KVR:], cosine, sine_table).astype(jnp.bfloat16)
    keyval = (
        mix_dot(comp_normed, full_keyval)
        .reshape(row_count, local_heads, NOPE + VD)
        .astype(jnp.bfloat16)
    )
    key_nope = keyval[..., :NOPE]
    values = keyval[..., NOPE:]
    attended, log_total = attend_forward(queries, key_nope, key_rope, values)
    attended_flat = attended.reshape(row_count, local_heads * VD)
    residual = stream + lax.psum(
        mix_dot(attended_flat, full_output).astype(jnp.bfloat16), "tensor"
    ).astype(jnp.float32)
    normed_two, inverse_two = rms_forward(residual, ffn_gain)
    normed_two = normed_two.astype(jnp.bfloat16)
    logits = mix_dot(normed_two, w_router)
    gate_weights, gate_sigmoid, gate_total, chosen = gate_values(logits, routes)
    capacity = 5 * row_count * TOP // (4 * EXPERTS)
    target, slot_owner = route_targets(routes, capacity)
    padded_normed = jnp.concatenate([normed_two, jnp.zeros((1, width), jnp.bfloat16)], axis=0)
    send_rows = padded_normed[slot_owner // TOP]
    sources = lax.axis_size("expert")
    local_experts = w_expert_in.shape[0]
    received = lax.all_to_all(send_rows, "expert", split_axis=0, concat_axis=0, tiled=True)
    rows_four = received.reshape(sources, local_experts, capacity, width)
    gates_up = contract("sjcd,jgdf->sjcgf", rows_four, w_expert_in)
    hidden = swiglu(gates_up[..., 0, :], gates_up[..., 1, :]).astype(jnp.bfloat16)
    expert_out = contract("sjcf,jfd->sjcd", hidden, w_expert_out).astype(jnp.bfloat16)
    returned = lax.all_to_all(
        expert_out.reshape(sources * local_experts * capacity, width),
        "expert",
        split_axis=0,
        concat_axis=0,
        tiled=True,
    )
    pair_out = returned[target].astype(jnp.float32).reshape(row_count, TOP, width)
    routed = jnp.sum(gate_weights[..., None] * pair_out, axis=1)
    shared_gate = mix_dot(normed_two, full_shared_in[0])
    shared_up = mix_dot(normed_two, full_shared_in[1])
    shared_hidden = swiglu(shared_gate, shared_up).astype(jnp.bfloat16)
    ffn_part = routed + mix_dot(shared_hidden, full_shared_out)
    own_rows = tokens_in.shape[0]
    first_row = lax.axis_index("tensor") * own_rows
    ffn_total = lax.psum_scatter(
        ffn_part.astype(jnp.bfloat16), "tensor", scatter_dimension=0, tiled=True
    ).astype(jnp.float32)
    block_out = (lax.dynamic_slice_in_dim(residual, first_row, own_rows, 0) + ffn_total).astype(
        jnp.bfloat16
    )
    grad_float = group_grad.astype(jnp.float32)
    grad_gate = jnp.sum(pair_out * grad_float[:, None, :], axis=-1)
    grad_pair = (
        (gate_weights[..., None] * grad_float[:, None, :])
        .astype(jnp.bfloat16)
        .reshape(row_count * TOP, width)
    )
    padded_grad = jnp.concatenate([grad_pair, jnp.zeros((1, width), jnp.bfloat16)], axis=0)
    grad_send = padded_grad[slot_owner]
    grad_received, rows_again = (
        lax.all_to_all(grad_send, "expert", split_axis=0, concat_axis=0, tiled=True),
        lax.all_to_all(
            padded_normed[slot_owner // TOP], "expert", split_axis=0, concat_axis=0, tiled=True
        ),
    )
    again_four = rows_again.reshape(sources, local_experts, capacity, width)
    again_gates = contract("sjcd,jgdf->sjcgf", again_four, w_expert_in)
    again_hidden = swiglu(again_gates[..., 0, :], again_gates[..., 1, :]).astype(jnp.bfloat16)
    grad_four = grad_received.reshape(sources, local_experts, capacity, width)
    grad_hidden = contract("sjcd,jfd->sjcf", grad_four, w_expert_out)
    grad_gate_up = swiglu_backward(again_gates[..., 0, :], again_gates[..., 1, :], grad_hidden)
    grad_expert_out = contract("sjcf,sjcd->jfd", again_hidden, grad_four)
    grad_expert_in = contract("sjcd,sjcgf->jgdf", again_four, grad_gate_up)
    grad_rows_out = contract("sjcgf,jgdf->sjcd", grad_gate_up, w_expert_in).astype(jnp.bfloat16)
    grad_back = lax.all_to_all(
        grad_rows_out.reshape(sources * local_experts * capacity, width),
        "expert",
        split_axis=0,
        concat_axis=0,
        tiled=True,
    )
    grad_normed = jnp.sum(
        grad_back[target].astype(jnp.float32).reshape(row_count, TOP, width), axis=1
    )
    grad_logits = gate_backward(grad_gate, gate_sigmoid, gate_total, chosen)
    grad_router = exact_dot(normed_two.astype(jnp.float32).T, grad_logits)
    grad_normed = grad_normed + exact_dot(grad_logits, w_router.astype(jnp.float32).T)
    grad_shared_hidden = contract("td,fd->tf", group_grad, full_shared_out)
    grad_shared = swiglu_backward(shared_gate, shared_up, grad_shared_hidden)
    grad_shared_out = contract("tf,td->fd", shared_hidden, group_grad)
    grad_shared_in = contract("td,tgf->gdf", normed_two, grad_shared)
    grad_normed = grad_normed + contract("tgf,gdf->td", grad_shared, full_shared_in)
    grad_res_part, grad_ffn_gain = rms_backward(residual, inverse_two, ffn_gain, grad_normed)
    grad_residual = grad_float + lax.psum(grad_res_part.astype(jnp.bfloat16), "tensor").astype(
        jnp.float32
    )
    grad_res_low = grad_residual.astype(jnp.bfloat16)
    grad_output = contract("tv,td->vd", attended_flat, grad_res_low)
    grad_attended = (
        contract("td,vd->tv", grad_res_low, full_output)
        .astype(jnp.bfloat16)
        .reshape(row_count, local_heads, VD)
    )
    grad_queries, key_grads = attend_backward(
        queries, key_nope, key_rope, values, attended, log_total, grad_attended
    )
    grad_key_nope, grad_key_rope, grad_values = key_grads
    grad_query_raw = (
        jnp.concatenate(
            [
                grad_queries[..., :NOPE],
                unrotate(grad_queries[..., NOPE:], cosine[:, None, :], sine_table[:, None, :]),
            ],
            axis=-1,
        )
        .reshape(row_count, local_heads * (NOPE + ROPE))
        .astype(jnp.bfloat16)
    )
    grad_query_weight = contract("td,tq->dq", normed_one, grad_query_raw)
    grad_normed_one = contract("tq,dq->td", grad_query_raw, full_query)
    grad_keyval = (
        jnp.concatenate([grad_key_nope, grad_values], axis=-1)
        .reshape(row_count, local_heads * (NOPE + VD))
        .astype(jnp.bfloat16)
    )
    grad_keyval_weight = contract("tc,tk->ck", comp_normed, grad_keyval)
    grad_comp_normed = contract("tk,ck->tc", grad_keyval, full_keyval)
    grad_compressed, grad_kv_gain = rms_backward(
        compressed, comp_inverse, kv_gain, grad_comp_normed
    )
    grad_latent_out = jnp.concatenate(
        [grad_compressed, unrotate(grad_key_rope, cosine, sine_table)], axis=-1
    )
    grad_latent = exact_dot(normed_one.astype(jnp.float32).T, grad_latent_out)
    grad_normed_one = grad_normed_one + exact_dot(grad_latent_out, w_latent.astype(jnp.float32).T)
    grad_x_part, grad_attn_gain = rms_backward(stream, inverse_one, attn_gain, grad_normed_one)
    grad_in = lax.dynamic_slice_in_dim(grad_residual, first_row, own_rows, 0) + lax.psum_scatter(
        grad_x_part.astype(jnp.bfloat16), "tensor", scatter_dimension=0, tiled=True
    ).astype(jnp.float32)
    sum_query, sum_keyval, sum_output, sum_shared_in, sum_shared_out = (
        lax.psum_scatter(
            grad_query_weight.astype(jnp.bfloat16), "expert", scatter_dimension=0, tiled=True
        ).astype(jnp.float32),
        lax.psum_scatter(
            grad_keyval_weight.astype(jnp.bfloat16), "expert", scatter_dimension=0, tiled=True
        ).astype(jnp.float32),
        lax.psum_scatter(
            grad_output.astype(jnp.bfloat16), "expert", scatter_dimension=1, tiled=True
        ).astype(jnp.float32),
        lax.psum_scatter(
            grad_shared_in.astype(jnp.bfloat16), "expert", scatter_dimension=1, tiled=True
        ).astype(jnp.float32),
        lax.psum_scatter(
            grad_shared_out.astype(jnp.bfloat16), "expert", scatter_dimension=1, tiled=True
        ).astype(jnp.float32),
    )
    sum_router, sum_latent, sum_attn_gain, sum_kv_gain, sum_ffn_gain = lax.psum(
        (grad_router, grad_latent, grad_attn_gain, grad_kv_gain, grad_ffn_gain),
        ("expert", "tensor"),
    )
    return (
        block_out,
        grad_in,
        sum_attn_gain,
        sum_kv_gain,
        sum_ffn_gain,
        sum_query,
        sum_latent,
        sum_keyval,
        sum_output,
        sum_router,
        sum_shared_in,
        sum_shared_out,
        grad_expert_in,
        grad_expert_out,
    )


def solution(mesh):
    placed = (
        P(("expert", "tensor"), None),
        P(("expert", "tensor"), None),
        P("expert", None),
        P(),
        P(),
        P(),
        P("expert", "tensor"),
        P(),
        P("expert", "tensor"),
        P("tensor", "expert"),
        P(),
        P(None, "expert", "tensor"),
        P("tensor", "expert"),
        P("expert", None, None, "tensor"),
        P("expert", "tensor", None),
    )
    return jax.shard_map(
        per_device,
        mesh=mesh,
        in_specs=placed,
        out_specs=(
            P(("expert", "tensor"), None),
            P(("expert", "tensor"), None),
            P(),
            P(),
            P(),
            P("expert", "tensor"),
            P(),
            P("expert", "tensor"),
            P("tensor", "expert"),
            P(),
            P(None, "expert", "tensor"),
            P("tensor", "expert"),
            P("expert", None, None, "tensor"),
            P("expert", "tensor", None),
        ),
        check_vma=False,
    )
```

profile of v0, /device:TPU:0, one launch (start us, length us, event | category | flops | bytes accessed | tf_op | source)
XLA Modules:
  0.0 1256.0 jit_solution(3145893994662896462)
XLA Ops:
  15.1 25.2 %all-gather.8.cloned.1.call-done = bf16[256,2048]{1,0:T(8,128)(2,1)} async-done(((bf16[64,2048]{1,0:T(8,128)(2,1)}), bf16[256,2048]{1,0:T(8,128)(2,1)}) %all-gather.8.cloned.1.call-update) | async-done | bytes 1048592 | tf_op jit(solution)/shard_map/all_gather | solution.py:218
  46.2 18.8 %all-gather.10.cloned.1.call-done = bf16[512,1024]{1,0:T(8,128)(2,1)} async-done(((bf16[64,1024]{1,0:T(8,128)(2,1)}), bf16[512,1024]{1,0:T(8,128)(2,1)}) %all-gather.10.cloned.1.call-update) | async-done | bytes 1048592 | tf_op jit(solution)/shard_map/all_gather | solution.py:223
  73.8 25.3 %all-gather.12.cloned.1.call-done = bf16[2048,768]{1,0:T(8,128)(2,1)} async-done(((bf16[256,768]{1,0:T(8,128)(2,1)}), bf16[2048,768]{1,0:T(8,128)(2,1)}) %all-gather.12.cloned.1.call-update) | async-done | bytes 3145744 | tf_op jit(solution)/shard_map/all_gather | solution.py:222
  105.9 23.0 %all-gather.14.cloned.1.call-done = bf16[512,2048]{1,0:T(8,128)(2,1)} async-done(((bf16[512,256]{1,0:T(8,128)(2,1)}), bf16[512,2048]{1,0:T(8,128)(2,1)}) %all-gather.14.cloned.1.call-update) | async-done | bytes 2097168 | tf_op jit(solution)/shard_map/all_gather | solution.py:224
  133.2 34.6 %reduce-window.6 = s32[64,12,128]{2,1,0:T(8,128)} reduce-window(s32[64,12,128]{2,1,0:T(8,128)} %fusion.58, s32[]{:T(128)} %constant.66.clone.1), window={size=1x1x128 pad=0_0x0_0x127_0}, to_apply=%region_8.9 | reduce-window | flops 12484608 | bytes 786436 | tf_op jit(solution)/shard_map/reduce-window
  204.4 29.1 %all-gather.20.cloned.1.call-done = bf16[256,2048]{1,0:T(8,128)(2,1)} async-done(((bf16[64,2048]{1,0:T(8,128)(2,1)}), bf16[256,2048]{1,0:T(8,128)(2,1)}) %all-gather.20.cloned.1.call-update) | async-done | bytes 1048592 | tf_op jit(solution)/shard_map/all_gather | solution.py:219
  243.1 15.8 %mul.638 = f32[1536,2048]{1,0:T(8,128)} reshape(f32[256,6,2048]{2,1,0:T(8,128)} %mul.637) | data formatting | bytes 25165824 | tf_op jit(solution)/shard_map/mul | solution.py:299
  275.8 19.9 %gather_fusion.2 = bf16[1920,2048]{1,0:T(8,128)(2,1)} fusion(bf16[1537,2048]{1,0:T(8,128)(2,1)} %concatenate.31, s32[2048]{0:T(1024)S(1)} %pad_clamp_fusion), kind=kCustom, calls=%fused_computation.2 | custom fusion | bytes 15736320 | tf_op jit(solution)/shard_map/gather | solution.py:304
  312.1 29.5 %fusion.27 = f32[8,8,30,2,352]{4,2,3,0,1:T(8,128)} fusion(bf16[8,2,2048,352]{2,3,1,0:T(8,128)(2,1)} %param.28, bf16[8,8,30,2048,1]{3,0,2,1,4:T(8,128)(2,1)} %bitcast.207), kind=kOutput, calls=%fused_computation.57 | convolution fusion | flops 5536481280 | bytes 36339712 | tf_op jit(solution)/shard_map/sjcd,jgdf->sjcgf/dot_general | solution.py:25
  341.6 70.6 %all-to-all-done.2 = bf16[8,240,2048]{2,1,0:T(8,128)(2,1)} async-done(((bf16[8,240,2048]{2,1,0:T(8,128)(2,1)}), bf16[8,240,2048]{2,1,0:T(8,128)(2,1)}, u32[]{:S(2)}, u32[]{:S(2)}) %all-to-all-start.2) | async-done | bytes 7864352 | tf_op jit(solution)/shard_map/all_to_all | solution.py:306
  527.5 42.9 %all-to-all-done.1 = bf16[8,240,2048]{2,1,0:T(8,128)(2,1)} async-done(((bf16[8,240,2048]{2,1,0:T(8,128)(2,1)}), bf16[8,240,2048]{2,1,0:T(8,128)(2,1)}, u32[]{:S(2)}, u32[]{:S(2)}) %all-to-all-start.1) | async-done | bytes 7864352 | tf_op jit(solution)/shard_map/all_to_all | solution.py:275
  585.6 57.5 %all-gather.18.cloned.1.call-done = bf16[704,2048]{1,0:T(8,128)(2,1)} async-done(((bf16[704,256]{1,0:T(8,128)(2,1)}), bf16[704,2048]{1,0:T(8,128)(2,1)}) %all-gather.18.cloned.1.call-update) | async-done | bytes 2883600 | tf_op jit(solution)/shard_map/all_gather | solution.py:226
  653.2 16.9 %gather_fusion.1 = bf16[1536,2048]{1,0:T(8,128)(2,1)} fusion(bf16[1920,2048]{1,0:T(8,128)(2,1)} %bitcast.19, s32[2048]{0:T(1024)S(1)} %pad_clamp_fusion.1), kind=kCustom, calls=%fused_computation.1 | custom fusion | bytes 12589056 | tf_op jit(solution)/shard_map/gather | solution.py:282
  681.9 17.0 %gather_fusion.3 = bf16[1536,2048]{1,0:T(8,128)(2,1)} fusion(bf16[1920,2048]{1,0:T(8,128)(2,1)} %bitcast.32, s32[2048]{0:T(1024)S(1)} %pad_clamp_fusion.1), kind=kCustom, calls=%fused_computation.3 | custom fusion | bytes 12589056 | tf_op jit(solution)/shard_map/gather | solution.py:328
  755.1 35.0 %all-reduce.10.cloned.1.call-done = bf16[256,2048]{1,0:T(8,128)(2,1)} async-done(((bf16[256,2048]{1,0:T(8,128)(2,1)}), bf16[256,2048]{1,0:T(8,128)(2,1)}) %all-reduce.10.cloned.1.call-update) | async-done | bytes 1048592 | tf_op jit(solution)/shard_map/psum | solution.py:339
  826.3 26.9 %convolution_bitcast_fusion = f32[8,2,2048,352]{2,3,1,0:T(8,128)} fusion(bf16[8,8,30,2048,1]{3,0,2,1,4:T(8,128)(2,1)} %bitcast.208, bf16[8,8,30,1,352]{4,2,0,1,3:T(8,128)(2,1)} %get-tuple-element.85, bf16[8,8,30,1,352]{4,2,0,1,3:T(8,128)(2,1)} %get-tuple-element.84), kind=kOutput, calls=%fused_computation.12 | convolution fusion | flops 5537832960 | bytes 56705024 | tf_op jit(solution)/shard_map/sjcd,sjcgf->jgdf/dot_general | solution.py:25
  861.4 19.0 %fusion.13 = f32[8,352,2048]{2,1,0:T(8,128)} fusion(bf16[8,8,30,352]{3,2,0,1:T(8,128)(2,1)} %copy-done.12, bf16[8,8,30,2048]{3,0,2,1:T(8,128)(2,1)} %bitcast.206), kind=kOutput, calls=%fused_computation.24 | convolution fusion | flops 2768240640 | bytes 32284672 | tf_op jit(solution)/shard_map/sjcf,sjcd->jfd/dot_general | solution.py:25
  882.4 17.3 %reduce-scatter.18.cloned.1.call-done = bf16[2,256,704]{1,2,0:T(8,128)(2,1)} async-done(((bf16[2,2048,704]{1,2,0:T(8,128)(2,1)}), bf16[2,256,704]{1,2,0:T(8,128)(2,1)}) %reduce-scatter.18.cloned.1.call-update) | async-done | bytes 720912 | tf_op jit(solution)/shard_map/reduce_scatter | solution.py:395
  902.1 40.7 %all-reduce.2 = (f32[2048]{0:T(1024)}, f32[512]{0:T(512)}, f32[2048]{0:T(1024)}) all-reduce(f32[2048]{0:T(1024)S(1)} %copy-done.53, f32[512]{0:T(512)S(1)} %copy-done.71, f32[2048]{0:T(1024)S(1)} %copy-done.52), channel_id=1, replica_groups=mesh['expert'=8,'tensor'=4] {'expert','tensor'}, use_global_device_ids=true, to_apply=%region_25.26 | all-reduce | flops 4608 | bytes 36864 | tf_op jit(solution)/shard_map/psum | solution.py:402
  947.6 20.0 %reduce-scatter.14.cloned.1.call-done = bf16[64,1024]{1,0:T(8,128)(2,1)} async-done(((bf16[512,1024]{1,0:T(8,128)(2,1)}), bf16[64,1024]{1,0:T(8,128)(2,1)}) %reduce-scatter.14.cloned.1.call-update) | async-done | bytes 131088 | tf_op jit(solution)/shard_map/reduce_scatter | solution.py:389
  969.2 27.8 %reduce-scatter.10.cloned.1.call-done = bf16[64,2048]{1,0:T(8,128)(2,1)} async-done(((bf16[256,2048]{1,0:T(8,128)(2,1)}), bf16[64,2048]{1,0:T(8,128)(2,1)}) %reduce-scatter.10.cloned.1.call-update) | async-done | bytes 262160 | tf_op jit(solution)/shard_map/reduce_scatter | solution.py:382
  999.0 40.8 %reduce-scatter.16.cloned.1.call-done = bf16[512,256]{1,0:T(8,128)(2,1)} async-done(((bf16[512,2048]{1,0:T(8,128)(2,1)}), bf16[512,256]{1,0:T(8,128)(2,1)}) %reduce-scatter.16.cloned.1.call-update) | async-done | bytes 262160 | tf_op jit(solution)/shard_map/reduce_scatter | solution.py:392
  1041.6 47.6 %reduce-scatter.12.cloned.1.call-done = bf16[256,768]{1,0:T(8,128)(2,1)} async-done(((bf16[2048,768]{1,0:T(8,128)(2,1)}), bf16[256,768]{1,0:T(8,128)(2,1)}) %reduce-scatter.12.cloned.1.call-update) | async-done | bytes 393232 | tf_op jit(solution)/shard_map/reduce_scatter | solution.py:386
  1091.1 152.2 %all-reduce.12.cloned.1.call-done = (f32[2048,576]{0,1:T(8,128)}, f32[2048,64]{0,1:T(8,128)}) async-done(((f32[2048,576]{0,1:T(8,128)}, f32[2048,64]{0,1:T(8,128)}), (f32[2048,576]{0,1:T(8,128)}, f32[2048,64]{0,1:T(8,128)})) %all-reduce.12.cloned.1.call-update) | async-done | bytes 5242896 | tf_op jit(solution)/shard_map/psum | solution.py:402
  (309 shorter events, 387.3 us)
Async XLA Ops:
  7.2 33.1 %all-gather.8.cloned.1.call-start = ((), (), s32[]{:S(2)}) async-start(), calls=%async_computation.11 | async-start | bytes 1310720 | tf_op jit(solution)/shard_map/all_gather | solution.py:218
  7.9 57.0 %all-gather.10.cloned.1.call-start = ((), (), s32[]{:S(2)}) async-start(), calls=%async_computation.12 | async-start | bytes 1179648 | tf_op jit(solution)/shard_map/all_gather | solution.py:223
  8.7 90.4 %all-gather.12.cloned.1.call-start = ((), (), s32[]{:S(2)}) async-start(), calls=%async_computation.13 | async-start | bytes 3538944 | tf_op jit(solution)/shard_map/all_gather | solution.py:222
  9.4 119.5 %all-gather.14.cloned.1.call-start = ((), (), s32[]{:S(2)}) async-start(), calls=%async_computation.14 | async-start | bytes 2359296 | tf_op jit(solution)/shard_map/all_gather | solution.py:224
  10.0 174.5 %all-reduce.8.cloned.1.call-start = ((), (), s32[]{:S(2)}) async-start(), calls=%async_computation.15 | async-start | bytes 2097152 | tf_op jit(solution)/shard_map/psum | solution.py:257
  42.4 56.7 %copy-start.44 = (f32[256]{0:T(256)}, f32[256]{0:T(256)S(1)}, u32[]{:S(2)}) copy-start(f32[256]{0:T(256)S(1)} %get-tuple-element.107) | copy-start | bytes 3076
  46.2 56.3 %copy-start.34 = (f32[256,32]{0,1:T(8,128)}, f32[256,32]{0,1:T(8,128)S(1)}, u32[]{:S(2)}) copy-start(f32[256,32]{0,1:T(8,128)S(1)} %get-tuple-element.105) | copy-start | bytes 98308
  198.9 96.8 %all-to-all-start = ((bf16[8,240,2048]{2,1,0:T(8,128)(2,1)}), bf16[8,240,2048]{2,1,0:T(8,128)(2,1)}, u32[]{:S(2)}, u32[]{:S(2)}) async-start(bf16[8,240,2048]{2,1,0:T(8,128)(2,1)} %bitcast.201), calls=%async_computation | async-start | bytes 15728640 | tf_op jit(solution)/shard_map/all_to_all | solution.py:270
  203.8 29.7 %all-gather.20.cloned.1.call-start = ((), (), s32[]{:S(2)}) async-start(), calls=%async_computation.19 | async-start | bytes 1310720 | tf_op jit(solution)/shard_map/all_gather | solution.py:219
  295.7 116.5 %all-to-all-start.2 = ((bf16[8,240,2048]{2,1,0:T(8,128)(2,1)}), bf16[8,240,2048]{2,1,0:T(8,128)(2,1)}, u32[]{:S(2)}, u32[]{:S(2)}) async-start(bf16[8,240,2048]{2,1,0:T(8,128)(2,1)} %bitcast.202), calls=%async_computation.3 | async-start | bytes 15728640 | tf_op jit(solution)/shard_map/all_to_all | solution.py:306
  300.6 277.3 %all-gather.16.cloned.1.call-start = ((), (), s32[]{:S(2)}) async-start(), calls=%async_computation.16 | async-start | bytes 6488064 | tf_op jit(solution)/shard_map/all_gather | solution.py:225
  477.1 93.4 %all-to-all-start.1 = ((bf16[8,240,2048]{2,1,0:T(8,128)(2,1)}), bf16[8,240,2048]{2,1,0:T(8,128)(2,1)}, u32[]{:S(2)}, u32[]{:S(2)}) async-start(bf16[8,240,2048]{2,1,0:T(8,128)(2,1)} %copy.224), calls=%async_computation.1 | async-start | bytes 15728640 | tf_op jit(solution)/shard_map/all_to_all | solution.py:275
  570.4 111.4 %all-to-all-start.3 = ((bf16[8,240,2048]{2,1,0:T(8,128)(2,1)}), bf16[8,240,2048]{2,1,0:T(8,128)(2,1)}, u32[]{:S(2)}, u32[]{:S(2)}) async-start(bf16[8,240,2048]{2,1,0:T(8,128)(2,1)} %copy.230), calls=%async_computation.4 | async-start | bytes 15728640 | tf_op jit(solution)/shard_map/all_to_all | solution.py:320
  575.3 67.7 %all-gather.18.cloned.1.call-start = ((), (), s32[]{:S(2)}) async-start(), calls=%async_computation.17 | async-start | bytes 3244032 | tf_op jit(solution)/shard_map/all_gather | solution.py:226
  576.1 214.0 %all-reduce.10.cloned.1.call-start = ((), (), s32[]{:S(2)}) async-start(), calls=%async_computation.20 | async-start | bytes 2097152 | tf_op jit(solution)/shard_map/psum | solution.py:339
  740.5 139.9 %reduce-scatter.20.cloned.1.call-start = ((), (), s32[]{:S(2)}) async-start(), calls=%async_computation.26 | async-start | bytes 3244032 | tf_op jit(solution)/shard_map/reduce_scatter | solution.py:398
  744.7 155.0 %reduce-scatter.18.cloned.1.call-start = ((), (), s32[]{:S(2)}) async-start(), calls=%async_computation.25 | async-start | bytes 6488064 | tf_op jit(solution)/shard_map/reduce_scatter | solution.py:395
  750.4 195.4 %reduce-scatter.8.cloned.1.call-start = ((), (), s32[]{:S(2)}) async-start(), calls=%async_computation.18 | async-start | bytes 1310720 | tf_op jit(solution)/shard_map/reduce_scatter | solution.py:290
  755.0 212.6 %reduce-scatter.14.cloned.1.call-start = ((), (), s32[]{:S(2)}) async-start(), calls=%async_computation.23 | async-start | bytes 1179648 | tf_op jit(solution)/shard_map/reduce_scatter | solution.py:389
  807.0 190.1 %reduce-scatter.10.cloned.1.call-start = ((), (), s32[]{:S(2)}) async-start(), calls=%async_computation.21 | async-start | bytes 1310720 | tf_op jit(solution)/shard_map/reduce_scatter | solution.py:382
  818.2 221.7 %reduce-scatter.16.cloned.1.call-start = ((), (), s32[]{:S(2)}) async-start(), calls=%async_computation.24 | async-start | bytes 2359296 | tf_op jit(solution)/shard_map/reduce_scatter | solution.py:392
  822.4 266.8 %reduce-scatter.12.cloned.1.call-start = ((), (), s32[]{:S(2)}) async-start(), calls=%async_computation.22 | async-start | bytes 3538944 | tf_op jit(solution)/shard_map/reduce_scatter | solution.py:386
  826.3 417.1 %all-reduce.12.cloned.1.call-start = ((), (), s32[]{:S(2)}) async-start(), calls=%async_computation.27 | async-start | bytes 10485760 | tf_op jit(solution)/shard_map/psum | solution.py:402
  880.4 62.4 %copy-start.4 = (bf16[256,2048]{1,0:T(8,128)(2,1)S(1)}, bf16[256,2048]{1,0:T(8,128)(2,1)}, u32[]{:S(2)}) copy-start(bf16[256,2048]{1,0:T(8,128)(2,1)} %all-gather.20.cloned.1.call-done) | copy-start | bytes 3145732
  (69 other events, 809.2 us)
Sparse Core Ops, SparseCore 0:
  9.6 30.6 all-gather.7
  42.2 22.7 all-gather.9
  66.9 32.1 all-gather.11
  100.8 28.0 all-gather.13
  132.5 51.9 all-reduce.7
  205.8 27.6 all-gather.19
  303.3 85.0 all-gather.15
  578.0 64.9 all-gather.17
  740.6 49.4 all-reduce.9
  793.4 43.9 reduce-scatter.19
  840.8 58.8 reduce-scatter.17
  901.9 27.9 reduce-scatter.7
  933.1 34.4 reduce-scatter.13
  969.7 27.2 reduce-scatter.9
  1000.2 39.6 reduce-scatter.15
  1043.1 46.0 reduce-scatter.11
  1095.2 148.0 all-reduce.11
where the time goes:
time: 1270 us; the launch traced here: 1260 us
  waiting for transfers between devices  643 us (51%)
  local copies, waits for them, and re-layouts  225 us (18%)
  matrix products  202 us (16%)
  other arithmetic  109 us (9%)
  blocking collectives  40.7 us (3%)
  starting transfers between devices  21.4 us (2%)
  between operations  15.1 us (1%)
    dot_general x25, matrix products, contract(): jnp.einsum(pattern, left_side, right_side, preferred_element_type=jnp.flo...  159 us
    psum x1, waiting for transfers between devices, per_device(): lax.psum((grad_router, grad_latent, grad_attn_gain, grad_kv_gain, grad_ff...  152 us
    all_to_all x1, waiting for transfers between devices, per_device(): lax.all_to_all(grad_send, 'expert', split_axis=0, concat_axis=0, tiled=True)  70.6 us
    all_gather x1, waiting for transfers between devices, per_device(): lax.all_gather(w_shared_out, 'expert', axis=1, tiled=True)  57.5 us
    reduce_scatter x1, waiting for transfers between devices, per_device(): lax.psum_scatter(grad_query_weight.astype(jnp.bfloat16), 'expert', scatte...  47.6 us
    all_to_all x1, waiting for transfers between devices, per_device(): lax.all_to_all(expert_out.reshape(sources * local_experts * capacity, wid...  42.9 us
    reduce_scatter x1, waiting for transfers between devices, per_device(): lax.psum_scatter(grad_output.astype(jnp.bfloat16), 'expert', scatter_dime...  40.8 us
    psum x1, blocking collectives, per_device(): lax.psum((grad_router, grad_latent, grad_attn_gain, grad_kv_gain, grad_ff...  40.7 us
  transfers between devices with their start and end apart: 21, of which 16 were waited for; matrix products, arithmetic and copies ran while one was open for 36% of the time, Pallas kernels for 0%

commit v1 on v0

v1 whole, which is shorter than its diff:
```python
import functools
import math

import jax
import jax.numpy as jnp
from jax import lax
from jax.experimental import pallas as pl
from jax.experimental.pallas import tpu as pltpu
from jax.sharding import PartitionSpec as P

NOPE = 128
ROPE = 64
VD = 128
KVR = 512
EXPERTS = 64
TOP = 6
SLOTS = 32
SLOT_BLOCK = 256
LANES = 128

EPSILON = 1e-06
ROUTE_SCALE = 2.446
ROPE_BASE = 50000.0
BF16 = jnp.bfloat16
F32 = jnp.float32


def mix_dot(left_side, right_side):
    return jnp.dot(left_side, right_side, preferred_element_type=F32)


def contract(pattern, left_side, right_side):
    return jnp.einsum(pattern, left_side, right_side, preferred_element_type=F32)


def rms_forward(values, gain_vec):
    inverse = lax.rsqrt(jnp.mean(values * values, axis=-1, keepdims=True) + EPSILON)
    return (values * inverse * gain_vec, inverse)


def rms_backward(values, inverse, gain_vec, grad_normed):
    weighted = grad_normed * gain_vec
    grad_values = inverse * weighted - values * (inverse * inverse * inverse) * jnp.mean(
        values * weighted, axis=-1, keepdims=True
    )
    grad_gain = jnp.sum(grad_normed * values * inverse, axis=0)
    return (grad_values, grad_gain)


def rope_tables(position):
    half_rope = ROPE // 2
    frequency = jnp.exp(-jnp.log(ROPE_BASE) * jnp.arange(half_rope).astype(F32) / half_rope)
    angles = position.astype(F32)[:, None] * frequency[None, :]
    return (jnp.cos(angles), jnp.sin(angles))


def rotate(columns, cosine, sine_table):
    half_rope = columns.shape[-1] // 2
    first_half = columns[..., :half_rope]
    second_half = columns[..., half_rope:]
    return jnp.concatenate(
        [
            first_half * cosine - second_half * sine_table,
            first_half * sine_table + second_half * cosine,
        ],
        axis=-1,
    )


def low_add(first, second):
    return (first.astype(F32) + second.astype(F32)).astype(BF16)


class Grid:
    def __init__(self):
        self.experts = lax.axis_size("expert")
        self.depth = lax.axis_size("tensor")
        self.side = math.isqrt(self.experts // 2)
        assert self.side * self.side * 2 == self.experts
        self.offsets = [
            (dy, dx, dc)
            for dy in range(self.side)
            for dx in range(self.side)
            for dc in range(2)
        ]

    def neighbour(self, place, offset):
        side = self.side
        y, x, core = place // (2 * side), place // 2 % side, place % 2
        dy, dx, dc = offset
        return (((y + dy) % side) * side + (x + dx) % side) * 2 + (core + dc) % 2

    def place_of(self, offset):
        return self.neighbour(lax.axis_index("expert"), offset)

    def fetch(self, array, offset):
        pairs = [(self.neighbour(place, offset), place) for place in range(self.experts)]
        return lax.ppermute(array, "expert", pairs)

    def send(self, array, offset):
        pairs = [(place, self.neighbour(place, offset)) for place in range(self.experts)]
        return lax.ppermute(array, "expert", pairs)

    def gather(self, shard):
        if self.side != 2:
            return [shard] + [self.fetch(shard, offset) for offset in self.offsets[1:]]
        half = shard.shape[0] // 2
        along_x = self.fetch(shard, (0, 1, 0))
        along_y = self.fetch(shard, (1, 0, 0))
        pair = self.fetch(shard, (0, 0, 1))
        first = self.fetch(along_x[:half], (1, 0, 0))
        second = self.fetch(along_y[half:], (0, 1, 0))
        pair_x = self.fetch(along_x, (0, 0, 1))
        pair_y = self.fetch(along_y, (0, 0, 1))
        pair_first = self.fetch(first, (0, 0, 1))
        pair_second = self.fetch(second, (0, 0, 1))
        return [
            shard,
            pair,
            along_x,
            pair_x,
            along_y,
            pair_y,
            jnp.concatenate([first, second]),
            jnp.concatenate([pair_first, pair_second]),
        ]

    def reduce(self, chunks):
        if self.side != 2:
            total = chunks[0].astype(F32)
            for offset, chunk in zip(self.offsets[1:], chunks[1:]):
                total = total + self.send(chunk, offset).astype(F32)
            return total
        half = chunks[0].shape[0] // 2
        own = {}
        for place in (6, 2, 4, 0):
            own[place] = low_add(chunks[place], self.send(chunks[place + 1], (0, 0, 1)))
        first = self.send(own[6][:half], (0, 1, 0))
        second = self.send(own[6][half:], (1, 0, 0))
        to_y = jnp.concatenate([low_add(own[4][:half], first), own[4][half:]])
        to_x = jnp.concatenate([own[2][:half], low_add(own[2][half:], second)])
        from_x = self.send(to_x, (0, 1, 0))
        from_y = self.send(to_y, (1, 0, 0))
        return own[0].astype(F32) + from_x.astype(F32) + from_y.astype(F32)

    def gather_depth(self, shard):
        depth = self.depth
        return [shard] + [
            lax.ppermute(shard, "tensor", [((i + k) % depth, i) for i in range(depth)])
            for k in range(1, depth)
        ]

    def reduce_depth(self, chunks):
        depth = self.depth
        total = chunks[0].astype(F32)
        for k in range(1, depth):
            total = total + lax.ppermute(
                chunks[k], "tensor", [(i, (i + k) % depth) for i in range(depth)]
            ).astype(F32)
        return total

    def absolute(self, pieces, axis):
        size = pieces[0].shape[axis]
        shape = list(pieces[0].shape)
        shape[axis] = size * self.experts
        whole = jnp.zeros(shape, pieces[0].dtype)
        for offset, piece in zip(self.offsets, pieces):
            whole = lax.dynamic_update_slice_in_dim(
                whole, piece, self.place_of(offset) * size, axis
            )
        return whole

    def relative(self, whole, axis):
        size = whole.shape[axis] // self.experts
        return [
            lax.dynamic_slice_in_dim(whole, self.place_of(offset) * size, size, axis)
            for offset in self.offsets
        ]

    def absolute_depth(self, pieces, axis):
        size = pieces[0].shape[axis]
        shape = list(pieces[0].shape)
        shape[axis] = size * self.depth
        whole = jnp.zeros(shape, pieces[0].dtype)
        own = lax.axis_index("tensor")
        for k, piece in enumerate(pieces):
            whole = lax.dynamic_update_slice_in_dim(
                whole, piece, (own + k) % self.depth * size, axis
            )
        return whole

    def relative_depth(self, whole, axis):
        size = whole.shape[axis] // self.depth
        own = lax.axis_index("tensor")
        return [
            lax.dynamic_slice_in_dim(whole, (own + k) % self.depth * size, size, axis)
            for k in range(self.depth)
        ]


def split_rows(array, count):
    size = array.shape[0] // count
    return [array[i * size : (i + 1) * size] for i in range(count)]


def attention_scores(queries, key_nope, key_rope, position):
    scores = contract("qhd,khd->hqk", queries[..., :NOPE], key_nope) + contract(
        "qhr,kr->hqk", queries[..., NOPE:], key_rope
    )
    scores = scores * ((NOPE + ROPE) ** (-0.5))
    allowed = position[None, :] <= position[:, None]
    return jnp.where(allowed[None], scores, -1e30)


def dot_nn(left, right):
    return lax.dot_general(left, right, (((1,), (0,)), ((), ())), preferred_element_type=F32)


def dot_nt(left, right):
    return lax.dot_general(left, right, (((1,), (1,)), ((), ())), preferred_element_type=F32)


def dot_tn(left, right):
    return lax.dot_general(left, right, (((0,), (0,)), ((), ())), preferred_element_type=F32)


def silu_parts(gate):
    sigmoid = 1.0 / (1.0 + jnp.exp(-gate))
    return sigmoid, gate * sigmoid


def split_high(value):
    high = value.astype(BF16)
    return high, (value - high.astype(F32)).astype(BF16)


def pick_rows(routes, local):
    count = routes.shape[1]
    expert = lax.broadcasted_iota(jnp.int32, (EXPERTS, count), 0)
    chosen = expert == routes[0:1]
    for k in range(1, routes.shape[0]):
        chosen = chosen | (expert == routes[k : k + 1])
    chosen = chosen.astype(F32)
    rows = max(local, 16)
    earlier = lax.broadcasted_iota(jnp.int32, (count, count), 0) < lax.broadcasted_iota(
        jnp.int32, (count, count), 1
    )
    rank = dot_nn(chosen[:rows].astype(BF16), earlier.astype(F32).astype(BF16))
    rank = jnp.where(chosen[:rows] > 0.5, rank, -1.0)
    parts = []
    slot = lax.broadcasted_iota(jnp.int32, (SLOTS, count), 0).astype(F32)
    for j in range(local):
        parts.append((slot == rank[j : j + 1]).astype(F32))
    return jnp.concatenate(parts, axis=0), chosen


def dispatch_grads_kernel(local, routes_ref, grads_ref, shared_ref, *rest):
    slot_ref, raw_ref = rest[-2:]
    pick, _ = pick_rows(routes_ref[...], local)
    grads = grads_ref[...]
    slot_ref[...] = (
        dot_nn(pick.astype(BF16), grads).astype(BF16).reshape(local, SLOTS, grads.shape[1])
    )
    raw_ref[...] = dot_nt(shared_ref[...], grads)


def dispatch_rows_kernel(
    local, units, routes_ref, rows_ref, router_ref, shared_ref, raw_ref, *rest
):
    slot_ref, info_ref, pick_ref, gate_ref, hidden_ref, back_ref = rest[-6:]
    pick, chosen = pick_rows(routes_ref[...], local)
    rows = rows_ref[...]
    low = pick.astype(BF16)
    pick_ref[...] = low
    slot_ref[...] = dot_nn(low, rows).astype(BF16).reshape(local, SLOTS, rows.shape[1])
    sigmoid = chosen / (1.0 + jnp.exp(-dot_nt(router_ref[...], rows)))
    total = jnp.sum(sigmoid, axis=0, keepdims=True)
    gate_ref[0] = sigmoid
    gate_ref[1] = jnp.broadcast_to(total, sigmoid.shape)
    weight = ROUTE_SCALE * sigmoid / total
    scale = jnp.concatenate(
        [
            jnp.sum(pick[j * SLOTS : (j + 1) * SLOTS] * weight[j : j + 1], axis=1, keepdims=True)
            for j in range(local)
        ],
        axis=0,
    )
    high, low_part = split_high(scale)
    lane = lax.broadcasted_iota(jnp.int32, (scale.shape[0], LANES), 1)
    info = jnp.where(lane == 0, high.astype(F32), jnp.where(lane == 1, low_part.astype(F32), 0.0))
    info_ref[...] = info.astype(BF16).reshape(local, SLOTS, LANES)
    shared = dot_nt(shared_ref[...], rows)
    gate, up, raw = shared[:units], shared[units:], raw_ref[...]
    smooth, active = silu_parts(gate)
    hidden_ref[...] = (active * up).astype(BF16)
    back_ref[...] = jnp.concatenate(
        [raw * up * smooth * (1.0 + gate * (1.0 - smooth)), raw * active], axis=0
    ).astype(BF16)


def expert_kernel(
    units, rows_ref, grads_ref, info_ref, in_ref, out_ref, out_rows_ref, back_rows_ref, extra_ref,
    hidden_ref, back_ref,
):
    expert = pl.program_id(0)
    rows, grads = rows_ref[0], grads_ref[0]
    weight_in, weight_out = in_ref[0], out_ref[0]
    gates = dot_nt(weight_in, rows)
    raw = dot_nt(weight_out, grads)
    gate, up = gates[:units], gates[units:]
    lane = lax.broadcasted_iota(jnp.int32, (16, LANES), 1)
    select = (lane < 2).astype(F32).astype(BF16)
    scale = dot_nt(select, info_ref[0])[0:1]
    smooth, active = silu_parts(gate)
    hidden = active * up
    grad_gate = jnp.sum(hidden.astype(BF16).astype(F32) * raw, axis=0, keepdims=True)
    scaled = (hidden * scale).astype(BF16)
    raw = raw * scale
    back = jnp.concatenate(
        [raw * up * smooth * (1.0 + gate * (1.0 - smooth)), raw * active], axis=0
    ).astype(BF16)
    hidden_ref[0] = scaled
    back_ref[0] = back
    out_rows_ref[0] = dot_tn(scaled, weight_out).astype(BF16)
    back_rows_ref[0] = dot_tn(back, weight_in).astype(BF16)
    high, low = split_high(grad_gate)
    row = lax.broadcasted_iota(jnp.int32, (16, grad_gate.shape[1]), 0)
    pair = jnp.where(row == 0, high.astype(F32), jnp.where(row == 1, low.astype(F32), 0.0))
    row = lax.broadcasted_iota(jnp.int32, (16, LANES), 0)
    lane = lax.broadcasted_iota(jnp.int32, (16, LANES), 1)
    place = ((row < 2) & (lane == expert + row * EXPERTS)).astype(F32)
    extra_ref[0] = dot_tn(pair.astype(BF16), place.astype(BF16)).astype(BF16)


def weight_grad_kernel(rows_ref, grads_ref, hidden_ref, back_ref, in_ref, out_ref):
    @pl.when(pl.program_id(1) == 0)
    def _():
        in_ref[0] = dot_nn(back_ref[0], rows_ref[0])
        out_ref[0] = dot_nn(hidden_ref[0], grads_ref[0])

    @pl.when(pl.program_id(1) > 0)
    def _():
        in_ref[0] += dot_nn(back_ref[0], rows_ref[0])
        out_ref[0] += dot_nn(hidden_ref[0], grads_ref[0])


def combine_back_kernel(
    local, pick_ref, slots_ref, extra_ref, gate_ref, router_ref, back_ref, shared_ref,
    tokens_ref, logits_ref,
):
    pick = pick_ref[...]
    flat = local * SLOTS
    merged = dot_tn(extra_ref[...].reshape(flat, LANES), pick)
    grad_gate = merged[:EXPERTS] + merged[EXPERTS:]
    sigmoid, total = gate_ref[0], gate_ref[1]
    mixed = jnp.sum(grad_gate * sigmoid, axis=0, keepdims=True)
    logits = ROUTE_SCALE * (grad_gate / total - mixed / (total * total)) * sigmoid * (1.0 - sigmoid)
    logits = logits.astype(BF16)
    logits_ref[...] = logits
    tokens_ref[...] = (
        dot_tn(pick, slots_ref[...].reshape(flat, slots_ref.shape[2]))
        + dot_tn(back_ref[...], shared_ref[...])
        + dot_tn(logits, router_ref[...])
    ).astype(BF16)


def combine_out_kernel(local, pick_ref, slots_ref, hidden_ref, shared_ref, tokens_ref):
    tokens_ref[...] = (
        dot_tn(pick_ref[...], slots_ref[...].reshape(local * SLOTS, slots_ref.shape[2]))
        + dot_tn(hidden_ref[...], shared_ref[...])
    ).astype(BF16)


def whole(shape):
    return pl.BlockSpec(shape, lambda *_: (0,) * len(shape))


def strip(local, place, width):
    return pl.BlockSpec((local, SLOTS, width), lambda *_: (0, place, 0))


def params(*semantics):
    return pltpu.CompilerParams(
        dimension_semantics=semantics or None, vmem_limit_bytes=56 * 1024 * 1024
    )


def dispatch_grads(place, sequences, local, routes, grads, shared_out, slots):
    count, width = grads.shape
    units = shared_out.shape[0]
    first = slots is None
    operands = [routes, grads, shared_out] + ([] if first else [slots])
    return pl.pallas_call(
        functools.partial(dispatch_grads_kernel, local),
        grid=(1,),
        in_specs=[whole(a.shape) for a in operands[:3]]
        + ([] if first else [pl.BlockSpec(memory_space=pl.ANY)]),
        out_specs=[strip(local, place, width), whole((units, count))],
        out_shape=[
            jax.ShapeDtypeStruct((local, sequences * SLOTS, width), BF16),
            jax.ShapeDtypeStruct((units, count), F32),
        ],
        input_output_aliases={} if first else {3: 0},
        compiler_params=params(),
        name="dispatch_grads",
    )(*operands)


def dispatch_rows(place, sequences, local, routes, rows, router, shared_in, raw, slots, infos):
    count, width = rows.shape
    units = raw.shape[0]
    first = slots is None
    operands = [routes, rows, router, shared_in, raw] + ([] if first else [slots, infos])
    anywhere = pl.BlockSpec(memory_space=pl.ANY)
    return pl.pallas_call(
        functools.partial(dispatch_rows_kernel, local, units),
        grid=(1,),
        in_specs=[whole(a.shape) for a in operands[:5]] + ([] if first else [anywhere, anywhere]),
        out_specs=[
            strip(local, place, width),
            strip(local, place, LANES),
            whole((local * SLOTS, count)),
            whole((2, EXPERTS, count)),
            whole((units, count)),
            whole((2 * units, count)),
        ],
        out_shape=[
            jax.ShapeDtypeStruct((local, sequences * SLOTS, width), BF16),
            jax.ShapeDtypeStruct((local, sequences * SLOTS, LANES), BF16),
            jax.ShapeDtypeStruct((local * SLOTS, count), BF16),
            jax.ShapeDtypeStruct((2, EXPERTS, count), F32),
            jax.ShapeDtypeStruct((units, count), BF16),
            jax.ShapeDtypeStruct((2 * units, count), BF16),
        ],
        input_output_aliases={} if first else {5: 0, 6: 1},
        compiler_params=params(),
        name="dispatch_rows",
    )(*operands)


def tile(*shape):
    return pl.BlockSpec((1,) + shape, lambda j, b: (j, b) + (0,) * (len(shape) - 1))


def lane_tile(*shape):
    return pl.BlockSpec((1,) + shape, lambda j, b: (j, 0, b))


def one(*shape):
    return pl.BlockSpec((1,) + shape, lambda j, b: (j, 0, 0))


def expert_rows(rows, grads, infos, expert_in, expert_out):
    local, slots, width = rows.shape
    units = expert_out.shape[1]
    block = min(slots, SLOT_BLOCK)
    return pl.pallas_call(
        functools.partial(expert_kernel, units),
        grid=(local, slots // block),
        in_specs=[
            tile(block, width),
            tile(block, width),
            tile(block, LANES),
            one(2 * units, width),
            one(units, width),
        ],
        out_specs=[
            tile(block, width),
            tile(block, width),
            tile(block, LANES),
            lane_tile(units, block),
            lane_tile(2 * units, block),
        ],
        out_shape=[
            jax.ShapeDtypeStruct((local, slots, width), BF16),
            jax.ShapeDtypeStruct((local, slots, width), BF16),
            jax.ShapeDtypeStruct((local, slots, LANES), BF16),
            jax.ShapeDtypeStruct((local, units, slots), BF16),
            jax.ShapeDtypeStruct((local, 2 * units, slots), BF16),
        ],
        compiler_params=params("arbitrary", "arbitrary"),
        name="expert_rows",
    )(rows, grads, infos, expert_in, expert_out)


def weight_grads(rows, grads, hidden, back):
    local, slots, width = rows.shape
    units = hidden.shape[1]
    block = min(slots, SLOT_BLOCK)
    return pl.pallas_call(
        weight_grad_kernel,
        grid=(local, slots // block),
        in_specs=[
            tile(block, width),
            tile(block, width),
            lane_tile(units, block),
            lane_tile(2 * units, block),
        ],
        out_specs=[one(2 * units, width), one(units, width)],
        out_shape=[
            jax.ShapeDtypeStruct((local, 2 * units, width), F32),
            jax.ShapeDtypeStruct((local, units, width), F32),
        ],
        compiler_params=params("arbitrary", "arbitrary"),
        name="weight_grads",
    )(rows, grads, hidden, back)


def combine_back(place, local, pick, slots, extra, gates, router, back, shared_in):
    count, width = pick.shape[1], slots.shape[2]
    return pl.pallas_call(
        functools.partial(combine_back_kernel, local),
        grid=(1,),
        in_specs=[
            whole(pick.shape), strip(local, place, width), strip(local, place, LANES),
            whole(gates.shape), whole(router.shape), whole(back.shape), whole(shared_in.shape),
        ],
        out_specs=[whole((count, width)), whole((EXPERTS, count))],
        out_shape=[
            jax.ShapeDtypeStruct((count, width), BF16),
            jax.ShapeDtypeStruct((EXPERTS, count), BF16),
        ],
        compiler_params=params(),
        name="combine_back",
    )(pick, slots, extra, gates, router, back, shared_in)


def combine_out(place, local, pick, slots, hidden, shared_out):
    count, width = pick.shape[1], slots.shape[2]
    return pl.pallas_call(
        functools.partial(combine_out_kernel, local),
        grid=(1,),
        in_specs=[
            whole(pick.shape), strip(local, place, width), whole(hidden.shape),
            whole(shared_out.shape),
        ],
        out_specs=whole((count, width)),
        out_shape=jax.ShapeDtypeStruct((count, width), BF16),
        compiler_params=params(),
        name="combine_out",
    )(pick, slots, hidden, shared_out)


def expert_layer(rows, grads, routes, router, expert_in, expert_out, shared):
    local, units, width = expert_out.shape
    sequences = len(rows)
    shared_units = shared.shape[0] // 3
    shared_in, shared_out = shared[: 2 * shared_units], shared[2 * shared_units :]
    order = list(range(sequences))
    slot_grads, raws = None, [None] * sequences
    for s in order:
        slot_grads, raws[s] = dispatch_grads(
            s, sequences, local, routes[s], grads[s], shared_out, slot_grads
        )
    slot_rows, infos = None, None
    tables = [None] * sequences
    for s in order:
        slot_rows, infos, *tables[s] = dispatch_rows(
            s, sequences, local, routes[s], rows[s], router, shared_in, raws[s], slot_rows, infos
        )
    out_rows, back_rows, extra, hidden, back = expert_rows(
        slot_rows, slot_grads, infos, expert_in.reshape(local, 2 * units, width), expert_out
    )
    back_tokens, logits = [None] * sequences, [None] * sequences
    for s in reversed(order):
        pick, gates, _, shared_back = tables[s]
        back_tokens[s], logits[s] = combine_back(
            s, local, pick, back_rows, extra, gates, router, shared_back, shared_in
        )
    out_tokens = [None] * sequences
    for s in reversed(order):
        pick, _, shared_hidden, _ = tables[s]
        out_tokens[s] = combine_out(s, local, pick, out_rows, shared_hidden, shared_out)
    grad_in, grad_out = weight_grads(slot_rows, slot_grads, hidden, back)
    all_rows = jnp.stack(rows)
    grad_router = contract("set,std->ed", jnp.stack(logits), all_rows)
    grad_shared = jnp.concatenate(
        [
            contract("sft,std->fd", jnp.stack([table[3] for table in tables]), all_rows),
            contract("sft,std->fd", jnp.stack([table[2] for table in tables]), jnp.stack(grads)),
        ]
    )
    return (
        out_tokens,
        back_tokens,
        grad_in.reshape(local, 2, units, width),
        grad_out,
        grad_router,
        grad_shared,
    )


def per_device(
    tokens_in,
    out_grad,
    routes,
    attn_gain,
    kv_gain,
    ffn_gain,
    w_query,
    w_latent,
    w_keyval,
    w_output,
    w_router,
    w_shared_in,
    w_shared_out,
    w_expert_in,
    w_expert_out,
):
    grid = Grid()
    depth = grid.depth
    own_depth = lax.axis_index("tensor")
    own_rows, width = tokens_in.shape
    row_count = own_rows * depth
    local_experts = w_expert_in.shape[0]
    base = lax.axis_index("expert") * local_experts
    stream = jnp.concatenate(grid.gather_depth(tokens_in)).astype(F32)
    full_query = grid.absolute(grid.gather(w_query), 0)
    full_keyval = grid.absolute(grid.gather(w_keyval), 0)
    full_output = grid.absolute(grid.gather(w_output), 1)
    all_grads = grid.gather(jnp.concatenate(grid.gather_depth(out_grad)))
    routes_rel = jnp.concatenate(grid.relative_depth(routes.T, 1), axis=1)
    routes_all = [routes_rel] + [grid.fetch(routes_rel, offset) for offset in grid.offsets[1:]]
    routes_all = [(part - base) % EXPERTS for part in routes_all]
    units = w_shared_out.shape[0] // grid.experts
    padding = ((0, -units % 32), (0, 0))
    padded_units = units + padding[0][1]
    shared_parts = [
        jnp.concatenate([jnp.pad(part, padding) for part in (gate_rows, up_rows, out_rows)])
        for gate_rows, up_rows, out_rows in zip(
            grid.relative(w_shared_in[0].T, 0),
            grid.relative(w_shared_in[1].T, 0),
            grid.relative(w_shared_out, 0),
        )
    ]
    shared = grid.absolute(
        [shared_parts[0]]
        + [
            grid.send(part, offset)
            for offset, part in zip(
                [(-dy, -dx, dc) for dy, dx, dc in grid.offsets[1:]],
                [
                    shared_parts[
                        grid.offsets.index(((-dy) % grid.side, (-dx) % grid.side, dc))
                    ]
                    for dy, dx, dc in grid.offsets[1:]
                ],
            )
        ],
        1,
    )
    position = (
        (own_depth + jnp.arange(row_count) // own_rows) % depth * own_rows
        + jnp.arange(row_count) % own_rows
    )
    local_heads = full_query.shape[1] // (NOPE + ROPE)
    cosine, sine_table = rope_tables(position)
    normed_one, inverse_one = rms_forward(stream, attn_gain)
    normed_one = normed_one.astype(BF16)
    queries = mix_dot(normed_one, full_query).reshape(row_count, local_heads, NOPE + ROPE)
    queries = jnp.concatenate(
        [
            queries[..., :NOPE],
            rotate(queries[..., NOPE:], cosine[:, None, :], sine_table[:, None, :]),
        ],
        axis=-1,
    ).astype(BF16)
    latent = mix_dot(normed_one, w_latent)
    compressed = latent[:, :KVR]
    comp_normed, comp_inverse = rms_forward(compressed, kv_gain)
    comp_normed = comp_normed.astype(BF16)
    key_rope = rotate(latent[:, KVR:], cosine, sine_table).astype(BF16)
    keyval = mix_dot(comp_normed, full_keyval).reshape(row_count, local_heads, NOPE + VD).astype(BF16)
    key_nope = keyval[..., :NOPE]
    values = keyval[..., NOPE:]
    scores = attention_scores(queries, key_nope, key_rope, position)
    top_score = jnp.max(scores, axis=-1, keepdims=True)
    raised = jnp.exp(scores - top_score)
    soft = raised / jnp.sum(raised, axis=-1, keepdims=True)
    soft_low = soft.astype(BF16)
    attended = contract("hqk,khv->qhv", soft_low, values).astype(BF16)
    attended_flat = attended.reshape(row_count, local_heads * VD)
    attention_part = mix_dot(attended_flat, full_output).astype(BF16)
    stream_own = tokens_in.astype(F32)
    residual = stream_own + grid.reduce_depth(split_rows(attention_part, depth))
    normed_two, inverse_two = rms_forward(residual, ffn_gain)
    normed_two = normed_two.astype(BF16)
    all_rows = grid.gather(jnp.concatenate(grid.gather_depth(normed_two)))
    router_rel = jnp.roll(w_router.T, -base, axis=0)
    (
        out_tokens,
        back_tokens,
        grad_expert_in,
        grad_expert_out,
        grad_router_rel,
        grad_shared,
    ) = expert_layer(
        all_rows,
        all_grads,
        routes_all,
        router_rel,
        jnp.swapaxes(w_expert_in, 2, 3),
        w_expert_out,
        shared,
    )
    grad_normed = grid.reduce_depth(
        split_rows(grid.reduce(back_tokens).astype(BF16), depth)
    )
    ffn_total = grid.reduce_depth(split_rows(grid.reduce(out_tokens).astype(BF16), depth))
    block_out = (residual + ffn_total).astype(BF16)
    grad_float = out_grad.astype(F32)
    grad_res_part, grad_ffn_gain = rms_backward(residual, inverse_two, ffn_gain, grad_normed)
    grad_residual = grad_float + grad_res_part
    grad_res_low = jnp.concatenate(grid.gather_depth(grad_residual.astype(BF16)))
    grad_output = contract("tv,td->vd", attended_flat, grad_res_low).astype(BF16)
    sum_output = grid.reduce(grid.relative(grad_output, 1))
    grad_attended = (
        contract("td,vd->tv", grad_res_low, full_output)
        .astype(BF16)
        .reshape(row_count, local_heads, VD)
    )
    softmax_scale = (NOPE + ROPE) ** (-0.5)
    grad_soft = contract("qhv,khv->hqk", grad_attended, values)
    row_delta = jnp.sum(grad_attended.astype(F32) * attended.astype(F32), axis=-1).T
    grad_scores = (soft * (grad_soft - row_delta[..., None]) * softmax_scale).astype(BF16)
    grad_query_nope = contract("hqk,khd->qhd", grad_scores, key_nope)
    grad_query_rope = contract("hqk,kr->qhr", grad_scores, key_rope)
    grad_key_nope = contract("hqk,qhd->khd", grad_scores, queries[..., :NOPE])
    grad_key_rope = contract("hqk,qhr->kr", grad_scores, queries[..., NOPE:])
    grad_values = contract("hqk,qhv->khv", soft_low, grad_attended)
    grad_query_raw = (
        jnp.concatenate(
            [
                grad_query_nope,
                rotate(grad_query_rope, cosine[:, None, :], -sine_table[:, None, :]),
            ],
            axis=-1,
        )
        .reshape(row_count, local_heads * (NOPE + ROPE))
        .astype(BF16)
    )
    grad_query_weight = contract("td,tq->dq", normed_one, grad_query_raw).astype(BF16)
    grad_keyval = (
        jnp.concatenate([grad_key_nope, grad_values], axis=-1)
        .reshape(row_count, local_heads * (NOPE + VD))
        .astype(BF16)
    )
    grad_keyval_weight = contract("tc,tk->ck", comp_normed, grad_keyval).astype(BF16)
    sum_query = grid.reduce(grid.relative(grad_query_weight, 0))
    sum_keyval = grid.reduce(grid.relative(grad_keyval_weight, 0))
    grad_comp_normed = contract("tk,ck->tc", grad_keyval, full_keyval)
    grad_compressed, grad_kv_gain = rms_backward(
        compressed, comp_inverse, kv_gain, grad_comp_normed
    )
    grad_latent_out = jnp.concatenate(
        [grad_compressed, rotate(grad_key_rope, cosine, -sine_table)], axis=-1
    ).astype(BF16)
    grad_latent = contract("tk,td->kd", grad_latent_out, normed_one)
    grad_normed_one = contract("tq,dq->td", grad_query_raw, full_query) + contract(
        "tk,dk->td", grad_latent_out, w_latent
    )
    grad_normed_one = grid.reduce_depth(split_rows(grad_normed_one.astype(BF16), depth))
    inverse_own = inverse_one[:own_rows]
    grad_x_part, grad_attn_gain = rms_backward(stream_own, inverse_own, attn_gain, grad_normed_one)
    grad_in = grad_residual + grad_x_part
    grad_shared_parts = [part.astype(BF16) for part in grid.relative(grad_shared, 1)]
    returned = [grad_shared_parts[0]] + [
        grid.send(part, offset) for offset, part in zip(grid.offsets[1:], grad_shared_parts[1:])
    ]
    returned = [
        returned[grid.offsets.index(((-dy) % grid.side, (-dx) % grid.side, dc))]
        for dy, dx, dc in grid.offsets
    ]
    sum_shared_in = jnp.stack(
        [
            grid.absolute([part[:units] for part in returned], 0).T,
            grid.absolute([part[padded_units : padded_units + units] for part in returned], 0).T,
        ]
    ).astype(F32)
    sum_shared_out = grid.absolute([part[2 * padded_units : 2 * padded_units + units] for part in returned], 0).astype(F32)
    gains = jnp.stack(
        [grad_attn_gain, grad_ffn_gain, jnp.pad(grad_kv_gain, (0, width - KVR))]
    )
    replicated = jnp.concatenate([grad_latent, jnp.roll(grad_router_rel, base, axis=0), gains])
    used = replicated.shape[0]
    padded = -(-used // (16 * grid.experts)) * 16 * grid.experts
    replicated = jnp.pad(replicated, ((0, padded - used), (0, 0))).astype(BF16)
    chunk = grid.reduce(grid.relative(replicated, 0)).astype(BF16)
    part = grid.reduce_depth(grid.relative_depth(chunk, 1)).astype(BF16)
    chunk = grid.absolute_depth(grid.gather_depth(part), 1)
    whole = grid.absolute(grid.gather(chunk), 0).astype(F32)
    sum_latent = whole[: KVR + ROPE].T
    sum_router = whole[KVR + ROPE : KVR + ROPE + EXPERTS].T
    sum_attn_gain = whole[KVR + ROPE + EXPERTS]
    sum_ffn_gain = whole[KVR + ROPE + EXPERTS + 1]
    sum_kv_gain = whole[KVR + ROPE + EXPERTS + 2, :KVR]
    return (
        block_out,
        grad_in,
        sum_attn_gain,
        sum_kv_gain,
        sum_ffn_gain,
        sum_query,
        sum_latent,
        sum_keyval,
        sum_output,
        sum_router,
        sum_shared_in,
        sum_shared_out,
        jnp.swapaxes(grad_expert_in, 2, 3),
        grad_expert_out,
    )


def solution(mesh):
    placed = (
        P(("expert", "tensor"), None),
        P(("expert", "tensor"), None),
        P("expert", None),
        P(),
        P(),
        P(),
        P("expert", "tensor"),
        P(),
        P("expert", "tensor"),
        P("tensor", "expert"),
        P(),
        P(None, "expert", "tensor"),
        P("tensor", "expert"),
        P("expert", None, None, "tensor"),
        P("expert", "tensor", None),
    )
    return jax.shard_map(
        per_device,
        mesh=mesh,
        in_specs=placed,
        out_specs=(
            P(("expert", "tensor"), None),
            P(("expert", "tensor"), None),
            P(),
            P(),
            P(),
            P("expert", "tensor"),
            P(),
            P("expert", "tensor"),
            P("tensor", "expert"),
            P(),
            P(None, "expert", "tensor"),
            P("tensor", "expert"),
            P("expert", None, None, "tensor"),
            P("expert", "tensor", None),
        ),
        check_vma=False,
    )
```

time: 1270 us -> 791 us (0.62)
  waiting for transfers between devices: 643 us -> 276 us
  matrix products: 202 us -> 35.4 us
  Pallas kernels: 0 us -> 150 us
  starting transfers between devices: 21.4 us -> 136 us
  local copies, waits for them, and re-layouts: 225 us -> 134 us
  other arithmetic: 109 us -> 51.4 us
  blocking collectives: 40.7 us -> 0 us
    ppermute x0 -> x153, waiting for transfers between devices: none -> 276 us  [the longest x62 124 us: send(): return lax.ppermute(array, 'expert', pairs)]
    psum x3 -> x0, waiting for transfers between devices: 193 us -> none  [the longest x1 152 us: per_device(): lax.psum((grad_router, grad_latent, grad_attn_gain, grad_kv_gain, grad_ff...]
    all_gather x7 -> x0, waiting for transfers between devices: 179 us -> none  [the longest x1 57.5 us: per_device(): lax.all_gather(w_shared_out, 'expert', axis=1, tiled=True)]
    dot_general x37 -> x24, matrix products: 202 us -> 35.4 us  [the longest x20 29.9 us: contract(): jnp.einsum(pattern, left_side, right_side, preferred_element_type=F32)]
    reduce_scatter x7 -> x0, waiting for transfers between devices: 154 us -> none  [the longest x1 47.6 us: per_device(): lax.psum_scatter(grad_query_weight.astype(jnp.bfloat16), 'expert', scatte...]
    pallas_call x0 -> x27, Pallas kernels: none -> 150 us  [the longest x1 33.5 us: expert_rows(): pl.pallas_call(functools.partial(expert_kernel, units), grid=(local, slot...]
    ppermute x0 -> x153, starting transfers between devices: none -> 136 us  [the longest x61 40.1 us: fetch(): return lax.ppermute(array, 'expert', pairs)]
    all_to_all x4 -> x0, waiting for transfers between devices: 114 us -> none  [the longest x1 70.6 us: per_device(): lax.all_to_all(grad_send, 'expert', split_axis=0, concat_axis=0, tiled=True)]
  transfers between devices with their start and end apart: 21 -> 153, of which waited for: 16 -> 52; matrix products, arithmetic and copies ran while one was open for 36% -> 23% of each run, Pallas kernels for 0% -> 16%
where the time goes in v1:
time: 791 us; the launch traced here: 787 us
  waiting for transfers between devices  276 us (35%)
  Pallas kernels  150 us (19%)
  starting transfers between devices  136 us (17%)
  local copies, waits for them, and re-layouts  134 us (17%)
  other arithmetic  51.4 us (6%)
  matrix products  35.4 us (4%)
    ppermute x62, waiting for transfers between devices, send(): return lax.ppermute(array, 'expert', pairs)  124 us
    ppermute x15, waiting for transfers between devices, reduce_depth(): lax.ppermute(chunks[k], 'tensor', [(i, (i + k) % depth) for i in range(de...  66.7 us
    ppermute x61, waiting for transfers between devices, fetch(): return lax.ppermute(array, 'expert', pairs)  54 us
    unnamed x354, local copies, waits for them, and re-layouts  43 us
    ppermute x61, starting transfers between devices, fetch(): return lax.ppermute(array, 'expert', pairs)  40.1 us
    ppermute x62, starting transfers between devices, send(): return lax.ppermute(array, 'expert', pairs)  36.8 us
    pallas_call x1, Pallas kernels, expert_rows(): pl.pallas_call(functools.partial(expert_kernel, units), grid=(local, slot...  33.5 us
    pallas_call x8, Pallas kernels, dispatch_rows(): pl.pallas_call(functools.partial(dispatch_rows_kernel, local, units), gri...  33 us
  transfers between devices with their start and end apart: 153, of which 52 were waited for; matrix products, arithmetic and copies ran while one was open for 23% of the time, Pallas kernels for 16%

profile of v1, /device:TPU:0, one launch (start us, length us, event | category | flops | bytes accessed | tf_op | source)
XLA Modules:
  0.0 787.1 jit_solution(9414911678700720692)
XLA Ops:
  109.3 13.5 %collective-permute-start.43 = (bf16[64,2048]{1,0:T(8,128)(2,1)}, bf16[64,2048]{1,0:T(8,128)(2,1)}, u32[]{:S(2)}, u32[]{:S(2)}) collective-permute-start(bf16[64,2048]{1,0:T(8,128)(2,1)} %param.16), channel_id=1, source_target_pairs={{1,0},{2,1},{3,2},{0,3},{5,4},{6,5},{7,6},{4,7},{9,8},{10,9},{11,1... | collective-permute-start | bytes 786440 | tf_op jit(solution)/shard_map/ppermute | solution.py:149
  139.8 5.0 collective-permute-done.30
  148.1 11.8 %collective-permute-done.31 = bf16[64,2048]{1,0:T(8,128)(2,1)S(1)} collective-permute-done((bf16[64,2048]{1,0:T(8,128)(2,1)S(1)}, bf16[64,2048]{1,0:T(8,128)(2,1)S(1)}, u32[]{:S(2)}, u32[]{:S(2)}) %collective-permute-start.31) | collective-permute-done | bytes 262176 | tf_op jit(solution)/shard_map/ppermute | solution.py:157
  176.4 5.3 collective-permute-done.34
  206.4 15.3 %collective-permute-done.54 = bf16[128,2048]{1,0:T(8,128)(2,1)} collective-permute-done((bf16[128,2048]{1,0:T(8,128)(2,1)}, bf16[128,2048]{1,0:T(8,128)(2,1)}, u32[]{:S(2)}, u32[]{:S(2)}) %collective-permute-start.54) | collective-permute-done | bytes 524320 | tf_op jit(solution)/shard_map/ppermute | solution.py:98
  229.5 17.0 %collective-permute-done.47.rows_ref = bf16[256,2048]{1,0:T(8,128)(2,1)S(1)} collective-permute-done((bf16[256,2048]{1,0:T(8,128)(2,1)}, bf16[256,2048]{1,0:T(8,128)(2,1)S(1)}, u32[]{:S(2)}, u32[]{:S(2)}) %collective-permute-start.47) | collective-permute-done | bytes 1048608 | tf_op jit(solution)/shard_map/ppermute | solution.py:98
  335.3 33.5 %expert_rows.1 = (bf16[8,256,2048]{2,1,0:T(8,128)(2,1)}, bf16[8,256,2048]{2,1,0:T(8,128)(2,1)}, bf16[8,256,128]{2,1,0:T(8,128)(2,1)}, bf16[8,352,256]{2,1,0:T(8,128)(2,1)}, bf16[8,704,256]{2,1,0:T(8,128)(2,1)}) custom-call(bf16[8,256,2048]{2,1,0:T(8,128)(2,1)} %get-tuple-element.131.rows_ref, bf16[8,256,2048]{2,1,0:T(8,128)(2,1)} %get-tuple-element.132.grads_ref, ...), custom_call_target="tpu_custom_call" | custom-call | tf_op jit(solution)/shard_map/expert_rows/pallas_call | solution.py:457
  419.3 5.3 convolution_bitcast_fusion.2
  425.5 29.5 %weight_grads.1 = (f32[8,704,2048]{2,1,0:T(8,128)}, f32[8,352,2048]{2,1,0:T(8,128)}) custom-call(bf16[8,256,2048]{2,1,0:T(8,128)(2,1)} %get-tuple-element.131.rows_ref, bf16[8,256,2048]{2,1,0:T(8,128)(2,1)} %get-tuple-element.132.grads_ref, bf16[8,352,256]{2,1,0:T(8,128)(2,1)} %get-tuple-element.184.hidden_ref, bf16[8,704,256]{2,1,0:T(8,128)(2,1)} %get-tuple-element.185.back_ref), custom_call_target="tpu_custom_call" | custom-call | tf_op jit(solution)/shard_map/weight_grads/pallas_call | solution.py:490
  461.4 5.4 collective-permute-done.149
  478.3 21.9 %collective-permute-done.88 = bf16[128,2048]{1,0:T(8,128)(2,1)S(1)} collective-permute-done((bf16[128,2048]{1,0:T(8,128)(2,1)S(1)}, bf16[128,2048]{1,0:T(8,128)(2,1)S(1)}, u32[]{:S(2)}, u32[]{:S(2)}) %collective-permute-start.88) | collective-permute-done | bytes 524320 | tf_op jit(solution)/shard_map/ppermute | solution.py:102
  501.9 11.1 %collective-permute-done.85 = bf16[128,2048]{1,0:T(8,128)(2,1)S(1)} collective-permute-done((bf16[128,2048]{1,0:T(8,128)(2,1)S(1)}, bf16[128,2048]{1,0:T(8,128)(2,1)S(1)}, u32[]{:S(2)}, u32[]{:S(2)}) %collective-permute-start.85) | collective-permute-done | bytes 524320 | tf_op jit(solution)/shard_map/ppermute | solution.py:102
  516.8 22.2 %collective-permute-done.89 = bf16[256,2048]{1,0:T(8,128)(2,1)S(1)} collective-permute-done((bf16[256,2048]{1,0:T(8,128)(2,1)S(1)}, bf16[256,2048]{1,0:T(8,128)(2,1)S(1)}, u32[]{:S(2)}, u32[]{:S(2)}) %collective-permute-start.89) | collective-permute-done | bytes 1048608 | tf_op jit(solution)/shard_map/ppermute | solution.py:102
  547.1 11.6 %collective-permute-done.78 = bf16[256,2048]{1,0:T(8,128)(2,1)S(1)} collective-permute-done((bf16[256,2048]{1,0:T(8,128)(2,1)S(1)}, bf16[256,2048]{1,0:T(8,128)(2,1)S(1)}, u32[]{:S(2)}, u32[]{:S(2)}) %collective-permute-start.78) | collective-permute-done | bytes 1048608 | tf_op jit(solution)/shard_map/ppermute | solution.py:102
  567.3 15.5 %collective-permute-done.91 = bf16[64,2048]{1,0:T(8,128)(2,1)S(1)} collective-permute-done((bf16[64,2048]{1,0:T(8,128)(2,1)S(1)}, bf16[64,2048]{1,0:T(8,128)(2,1)S(1)}, u32[]{:S(2)}, u32[]{:S(2)}) %collective-permute-start.91) | collective-permute-done | bytes 262176 | tf_op jit(solution)/shard_map/ppermute | solution.py:157
  583.2 11.0 %collective-permute-done.80 = bf16[64,2048]{1,0:T(8,128)(2,1)S(1)} collective-permute-done((bf16[64,2048]{1,0:T(8,128)(2,1)S(1)}, bf16[64,2048]{1,0:T(8,128)(2,1)S(1)}, u32[]{:S(2)}, u32[]{:S(2)}) %collective-permute-start.80) | collective-permute-done | bytes 262176 | tf_op jit(solution)/shard_map/ppermute | solution.py:157
  607.5 8.6 %collective-permute-done.94 = bf16[64,2048]{1,0:T(8,128)(2,1)S(1)} collective-permute-done((bf16[64,2048]{1,0:T(8,128)(2,1)S(1)}, bf16[64,2048]{1,0:T(8,128)(2,1)S(1)}, u32[]{:S(2)}, u32[]{:S(2)}) %collective-permute-start.94) | collective-permute-done | bytes 262176 | tf_op jit(solution)/shard_map/ppermute | solution.py:149
  639.3 5.4 collective-permute-start.96
  657.0 10.8 %collective-permute-done.97 = bf16[64,2048]{1,0:T(8,128)(2,1)S(1)} collective-permute-done((bf16[64,2048]{1,0:T(8,128)(2,1)S(1)}, bf16[64,2048]{1,0:T(8,128)(2,1)S(1)}, u32[]{:S(2)}, u32[]{:S(2)}) %collective-permute-start.97) | collective-permute-done | bytes 262176 | tf_op jit(solution)/shard_map/ppermute | solution.py:157
  669.3 13.5 %concatenate.181 = bf16[643,2048]{1,0:T(8,128)(2,1)} concatenate(bf16[576,2048]{1,0:T(8,128)(2,1)} %convolution_convert_fusion.1, bf16[64,2048]{1,0:T(8,128)(2,1)} %fusion.23, bf16[1,2048]{1,0:T(2,128)(2,1)} %stack.174, bf16[1,2048]{1,0:T(2,128)(2,1)S(1)} %stack.175, bf16[1,2048]{1,0:T(2,128)(2,1)} %stack.176), dimensions={0} | concatenate | bytes 5267456 | tf_op jit(solution)/shard_map/concatenate | solution.py:784
  709.6 8.2 %collective-permute-done.105 = bf16[48,2048]{1,0:T(8,128)(2,1)S(1)} collective-permute-done((bf16[48,2048]{1,0:T(8,128)(2,1)S(1)}, bf16[48,2048]{1,0:T(8,128)(2,1)S(1)}, u32[]{:S(2)}, u32[]{:S(2)}) %collective-permute-start.105) | collective-permute-done | bytes 196640 | tf_op jit(solution)/shard_map/ppermute | solution.py:102
  718.4 5.5 collective-permute-done.102
  728.4 7.5 collective-permute-done.106
  744.4 5.2 collective-permute-done.108
  (916 shorter events, 483.8 us)
Async XLA Ops:
  92.9 68.3 %collective-permute-start.45 = (bf16[64,2048]{1,0:T(8,128)(2,1)}, bf16[64,2048]{1,0:T(8,128)(2,1)}, u32[]{:S(2)}, u32[]{:S(2)}) collective-permute-start(bf16[64,2048]{1,0:T(8,128)(2,1)} %param.16), channel_id=1, source_target_pairs={{3,0},{0,1},{1,2},{2,3},{7,4},{4,5},{5,6},{6,7},{11,8},{8,9},{9,10... | collective-permute-start | bytes 786440 | tf_op jit(solution)/shard_map/ppermute | solution.py:149
  100.7 38.0 %collective-permute-start.44 = (bf16[64,2048]{1,0:T(8,128)(2,1)}, bf16[64,2048]{1,0:T(8,128)(2,1)}, u32[]{:S(2)}, u32[]{:S(2)}) collective-permute-start(bf16[64,2048]{1,0:T(8,128)(2,1)} %param.16), channel_id=1, source_target_pairs={{2,0},{3,1},{0,2},{1,3},{6,4},{7,5},{4,6},{5,7},{10,8},{11,9},{8,1... | collective-permute-start | bytes 786440 | tf_op jit(solution)/shard_map/ppermute | solution.py:149
  162.2 33.0 %collective-permute-start.67 = (bf16[256,2048]{1,0:T(8,128)(2,1)S(1)}, bf16[256,2048]{1,0:T(8,128)(2,1)S(1)}, u32[]{:S(2)}, u32[]{:S(2)}) collective-permute-start(bf16[256,2048]{1,0:T(8,128)(2,1)S(1)} %constant_dynamic-update-slice_fusion.grads_ref), channel_id=1, source_target_pairs={{4,0},{0,4},{12,8},{8,12},{20,16},{16,20},{28,24},{24,28},{5,1},{1... | collective-permute-start | bytes 3145736 | tf_op jit(solution)/shard_map/ppermute | solution.py:98
  184.0 66.5 %collective-permute-start.70 = (bf16[256,2048]{1,0:T(8,128)(2,1)}, bf16[256,2048]{1,0:T(8,128)(2,1)}, u32[]{:S(2)}, u32[]{:S(2)}) collective-permute-start(bf16[256,2048]{1,0:T(8,128)(2,1)} %pad_maximum_fusion.1.rows_ref), channel_id=1, source_target_pairs={{4,0},{0,4},{12,8},{8,12},{20,16},{16,20},{28,24},{24,28},{5,1},{1... | collective-permute-start | bytes 3145736 | tf_op jit(solution)/shard_map/ppermute | solution.py:98
  184.0 44.3 %collective-permute-start.50 = (bf16[256,2048]{1,0:T(8,128)(2,1)}, bf16[256,2048]{1,0:T(8,128)(2,1)S(1)}, u32[]{:S(2)}, u32[]{:S(2)}) collective-permute-start(bf16[256,2048]{1,0:T(8,128)(2,1)} %pad_maximum_fusion.1.rows_ref), channel_id=1, source_target_pairs={{16,0},{20,4},{24,8},{28,12},{0,16},{4,20},{8,24},{12,28},{17,1},{... | collective-permute-start | bytes 3145736 | tf_op jit(solution)/shard_map/ppermute | solution.py:98
  189.2 34.0 %collective-permute-start.57 = (bf16[128,2048]{1,0:T(8,128)(2,1)}, bf16[128,2048]{1,0:T(8,128)(2,1)}, u32[]{:S(2)}, u32[]{:S(2)}) collective-permute-start(bf16[128,2048]{1,0:T(8,128)(2,1)} %slice.479), channel_id=1, source_target_pairs={{8,0},{12,4},{0,8},{4,12},{24,16},{28,20},{16,24},{20,28},{9,1},{1... | collective-permute-start | bytes 1572872 | tf_op jit(solution)/shard_map/ppermute | solution.py:98
  224.4 55.1 %collective-permute-start.58 = (bf16[128,2048]{1,0:T(8,128)(2,1)}, bf16[128,2048]{1,0:T(8,128)(2,1)}, u32[]{:S(2)}, u32[]{:S(2)}) collective-permute-start(bf16[128,2048]{1,0:T(8,128)(2,1)} %collective-permute-done.57), channel_id=1, source_target_pairs={{4,0},{0,4},{12,8},{8,12},{20,16},{16,20},{28,24},{24,28},{5,1},{1... | collective-permute-start | bytes 1572872 | tf_op jit(solution)/shard_map/ppermute | solution.py:98
  228.4 49.5 %collective-permute-start.55 = (bf16[128,2048]{1,0:T(8,128)(2,1)}, bf16[128,2048]{1,0:T(8,128)(2,1)}, u32[]{:S(2)}, u32[]{:S(2)}) collective-permute-start(bf16[128,2048]{1,0:T(8,128)(2,1)} %collective-permute-done.54), channel_id=1, source_target_pairs={{4,0},{0,4},{12,8},{8,12},{20,16},{16,20},{28,24},{24,28},{5,1},{1... | collective-permute-start | bytes 1572872 | tf_op jit(solution)/shard_map/ppermute | solution.py:98
  246.6 40.5 %collective-permute-start.51 = (bf16[128,2048]{1,0:T(8,128)(2,1)}, bf16[128,2048]{1,0:T(8,128)(2,1)}, u32[]{:S(2)}, u32[]{:S(2)}) collective-permute-start(bf16[128,2048]{1,0:T(8,128)(2,1)} %slice.477), channel_id=1, source_target_pairs={{8,0},{12,4},{0,8},{4,12},{24,16},{28,20},{16,24},{20,28},{9,1},{1... | collective-permute-start | bytes 1572872 | tf_op jit(solution)/shard_map/ppermute | solution.py:98
  247.8 39.2 %collective-permute-start.48 = (bf16[128,2048]{1,0:T(8,128)(2,1)}, bf16[128,2048]{1,0:T(8,128)(2,1)}, u32[]{:S(2)}, u32[]{:S(2)}) collective-permute-start(bf16[128,2048]{1,0:T(8,128)(2,1)} %slice.476), channel_id=1, source_target_pairs={{16,0},{20,4},{24,8},{28,12},{0,16},{4,20},{8,24},{12,28},{17,1},{... | collective-permute-start | bytes 1572872 | tf_op jit(solution)/shard_map/ppermute | solution.py:98
  329.5 138.8 %collective-permute-start.151 = (bf16[288,256]{1,0:T(8,128)(2,1)}, bf16[288,256]{1,0:T(8,128)(2,1)}, u32[]{:S(2)}, u32[]{:S(2)}) collective-permute-start(bf16[288,256]{1,0:T(8,128)(2,1)} %get-tuple-element.259), channel_id=1, source_target_pairs={{0,24},{4,28},{8,16},{12,20},{16,8},{20,12},{24,0},{28,4},{1,25},{... | collective-permute-start | bytes 442376 | tf_op jit(solution)/shard_map/ppermute | solution.py:102
  332.1 134.8 %collective-permute-start.150 = (bf16[288,256]{1,0:T(8,128)(2,1)}, bf16[288,256]{1,0:T(8,128)(2,1)}, u32[]{:S(2)}, u32[]{:S(2)}) collective-permute-start(bf16[288,256]{1,0:T(8,128)(2,1)} %get-tuple-element.260), channel_id=1, source_target_pairs={{0,20},{4,16},{8,28},{12,24},{16,4},{20,0},{24,12},{28,8},{1,21},{... | collective-permute-start | bytes 442376 | tf_op jit(solution)/shard_map/ppermute | solution.py:102
  332.1 268.6 %collective-permute-start.152 = (bf16[288,256]{1,0:T(8,128)(2,1)}, bf16[288,256]{1,0:T(8,128)(2,1)}, u32[]{:S(2)}, u32[]{:S(2)}) collective-permute-start(bf16[288,256]{1,0:T(8,128)(2,1)} %get-tuple-element.253), channel_id=1, source_target_pairs={{0,28},{4,24},{8,20},{12,16},{16,12},{20,8},{24,4},{28,0},{1,29},{... | collective-permute-start | bytes 442376 | tf_op jit(solution)/shard_map/ppermute | solution.py:102
  333.7 121.4 %collective-permute-start.146 = (bf16[288,256]{1,0:T(8,128)(2,1)}, bf16[288,256]{1,0:T(8,128)(2,1)}, u32[]{:S(2)}, u32[]{:S(2)}) collective-permute-start(bf16[288,256]{1,0:T(8,128)(2,1)} %get-tuple-element.255), channel_id=1, source_target_pairs={{0,4},{4,0},{8,12},{12,8},{16,20},{20,16},{24,28},{28,24},{1,5},{5... | collective-permute-start | bytes 442376 | tf_op jit(solution)/shard_map/ppermute | solution.py:102
  333.7 122.8 %collective-permute-start.147 = (bf16[288,256]{1,0:T(8,128)(2,1)}, bf16[288,256]{1,0:T(8,128)(2,1)}, u32[]{:S(2)}, u32[]{:S(2)}) collective-permute-start(bf16[288,256]{1,0:T(8,128)(2,1)} %get-tuple-element.256), channel_id=1, source_target_pairs={{0,8},{4,12},{8,0},{12,4},{16,24},{20,28},{24,16},{28,20},{1,9},{5... | collective-permute-start | bytes 442376 | tf_op jit(solution)/shard_map/ppermute | solution.py:102
  471.4 44.8 %collective-permute-start.82 = (bf16[256,2048]{1,0:T(8,128)(2,1)S(1)}, bf16[256,2048]{1,0:T(8,128)(2,1)S(1)}, u32[]{:S(2)}, u32[]{:S(2)}) collective-permute-start(bf16[256,2048]{1,0:T(8,128)(2,1)S(1)} %copy-done.62), channel_id=1, source_target_pairs={{0,4},{4,0},{8,12},{12,8},{16,20},{20,16},{24,28},{28,24},{1,5},{5... | collective-permute-start | bytes 3145736 | tf_op jit(solution)/shard_map/ppermute | solution.py:102
  474.2 40.6 %collective-permute-start.74 = (bf16[128,2048]{1,0:T(8,128)(2,1)S(1)}, bf16[128,2048]{1,0:T(8,128)(2,1)S(1)}, u32[]{:S(2)}, u32[]{:S(2)}) collective-permute-start(bf16[128,2048]{1,0:T(8,128)(2,1)S(1)} %get-tuple-element.279), channel_id=1, source_target_pairs={{0,16},{4,20},{8,24},{12,28},{16,0},{20,4},{24,8},{28,12},{1,17},{... | collective-permute-start | bytes 1572872 | tf_op jit(solution)/shard_map/ppermute | solution.py:102
  475.2 40.3 %collective-permute-start.77 = (bf16[128,2048]{1,0:T(8,128)(2,1)S(1)}, bf16[128,2048]{1,0:T(8,128)(2,1)S(1)}, u32[]{:S(2)}, u32[]{:S(2)}) collective-permute-start(bf16[128,2048]{1,0:T(8,128)(2,1)S(1)} %get-tuple-element.280), channel_id=1, source_target_pairs={{0,8},{4,12},{8,0},{12,4},{16,24},{20,28},{24,16},{28,20},{1,9},{5... | collective-permute-start | bytes 1572872 | tf_op jit(solution)/shard_map/ppermute | solution.py:102
  516.2 42.5 %collective-permute-start.78 = (bf16[256,2048]{1,0:T(8,128)(2,1)S(1)}, bf16[256,2048]{1,0:T(8,128)(2,1)S(1)}, u32[]{:S(2)}, u32[]{:S(2)}) collective-permute-start(bf16[256,2048]{1,0:T(8,128)(2,1)S(1)} %pad_maximum_fusion.3), channel_id=1, source_target_pairs={{0,16},{4,20},{8,24},{12,28},{16,0},{20,4},{24,8},{28,12},{1,17},{... | collective-permute-start | bytes 3145736 | tf_op jit(solution)/shard_map/ppermute | solution.py:102
  629.0 62.9 %collective-permute-start.130 = (bf16[64,1024]{1,0:T(8,128)(2,1)}, bf16[64,1024]{1,0:T(8,128)(2,1)}, u32[]{:S(2)}, u32[]{:S(2)}) collective-permute-start(bf16[64,1024]{1,0:T(8,128)(2,1)} %get-tuple-element.261), channel_id=1, source_target_pairs={{0,4},{4,0},{8,12},{12,8},{16,20},{20,16},{24,28},{28,24},{1,5},{5... | collective-permute-start | bytes 393224 | tf_op jit(solution)/shard_map/ppermute | solution.py:102
  631.9 55.8 %collective-permute-start.143 = (bf16[512,256]{1,0:T(8,128)(2,1)}, bf16[512,256]{1,0:T(8,128)(2,1)}, u32[]{:S(2)}, u32[]{:S(2)}) collective-permute-start(bf16[512,256]{1,0:T(8,128)(2,1)} %get-tuple-element.247), channel_id=1, source_target_pairs={{0,4},{4,0},{8,12},{12,8},{16,20},{20,16},{24,28},{28,24},{1,5},{5... | collective-permute-start | bytes 786440 | tf_op jit(solution)/shard_map/ppermute | solution.py:102
  655.8 32.6 %collective-permute-start.140 = (bf16[512,256]{1,0:T(8,128)(2,1)}, bf16[512,256]{1,0:T(8,128)(2,1)}, u32[]{:S(2)}, u32[]{:S(2)}) collective-permute-start(bf16[512,256]{1,0:T(8,128)(2,1)} %get-tuple-element.248), channel_id=1, source_target_pairs={{0,4},{4,0},{8,12},{12,8},{16,20},{20,16},{24,28},{28,24},{1,5},{5... | collective-permute-start | bytes 786440 | tf_op jit(solution)/shard_map/ppermute | solution.py:102
  667.9 32.1 %collective-permute-start.127 = (bf16[256,768]{1,0:T(8,128)(2,1)}, bf16[256,768]{1,0:T(8,128)(2,1)}, u32[]{:S(2)}, u32[]{:S(2)}) collective-permute-start(bf16[256,768]{1,0:T(8,128)(2,1)} %get-tuple-element.231), channel_id=1, source_target_pairs={{0,4},{4,0},{8,12},{12,8},{16,20},{20,16},{24,28},{28,24},{1,5},{5... | collective-permute-start | bytes 1179656 | tf_op jit(solution)/shard_map/ppermute | solution.py:102
  694.6 56.6 %collective-permute-start.138 = (bf16[512,256]{1,0:T(8,128)(2,1)S(1)}, bf16[512,256]{1,0:T(8,128)(2,1)S(1)}, u32[]{:S(2)}, u32[]{:S(2)}) collective-permute-start(bf16[512,256]{1,0:T(8,128)(2,1)S(1)} %copy-done.105), channel_id=1, source_target_pairs={{0,4},{4,0},{8,12},{12,8},{16,20},{20,16},{24,28},{28,24},{1,5},{5... | collective-permute-start | bytes 786440 | tf_op jit(solution)/shard_map/ppermute | solution.py:102
  (288 other events, 3312.0 us)

commit v2 on v1

--- a/solution.py
+++ b/solution.py
@@ -17,6 +17,8 @@
 SLOTS = 32
 SLOT_BLOCK = 256
 LANES = 128
+PARTS = 2
+CHUNK_ROWS = 704
 
 EPSILON = 1e-06
 ROUTE_SCALE = 2.446
@@ -143,6 +145,32 @@
         from_y = self.send(to_y, (1, 0, 0))
         return own[0].astype(F32) + from_x.astype(F32) + from_y.astype(F32)
 
+    def gather_small(self, shard):
+        along_x = self.fetch(shard, (0, 1, 0))
+        along_y = self.fetch(shard, (1, 0, 0))
+        near = [shard, along_x, along_y, self.fetch(along_x, (1, 0, 0))]
+        return [piece for held in near for piece in (held, self.fetch(held, (0, 0, 1)))]
+
+    def exchange(self, parts):
+        pieces = [parts[0]]
+        for dy, dx, dc in self.offsets[1:]:
+            back = (-dy % self.side, -dx % self.side, dc)
+            pieces.append(self.send(parts[self.offsets.index(back)], back))
+        return pieces
+
+    def reduce_parts(self, chunks):
+        half = chunks[0].shape[0] // 2
+        own = {}
+        for place in (6, 2, 4, 0):
+            own[place] = low_add(chunks[place], self.send(chunks[place + 1], (0, 0, 1)))
+        first = self.send(own[6][:half], (0, 1, 0))
+        second = self.send(own[6][half:], (1, 0, 0))
+        to_y = jnp.concatenate([low_add(own[4][:half], first), own[4][half:]])
+        to_x = jnp.concatenate([own[2][:half], low_add(own[2][half:], second)])
+        from_x = self.send(to_x, (0, 1, 0))
+        from_y = self.send(to_y, (1, 0, 0))
+        return [own[0], from_x, from_y], own[6], to_x
+
     def gather_depth(self, shard):
         depth = self.depth
         return [shard] + [
@@ -234,9 +262,23 @@
     return high, (value - high.astype(F32)).astype(BF16)
 
 
-def pick_rows(routes, local):
+def whole(shape):
+    return pl.BlockSpec(shape, lambda *_: (0,) * len(shape))
+
+
+def params(*semantics):
+    return pltpu.CompilerParams(
+        dimension_semantics=semantics or None, vmem_limit_bytes=56 * 1024 * 1024
+    )
+
+
+ANYWHERE = pl.BlockSpec(memory_space=pl.ANY)
+
+
+def pick_rows(routes, base, local):
     count = routes.shape[1]
-    expert = lax.broadcasted_iota(jnp.int32, (EXPERTS, count), 0)
+    expert = lax.broadcasted_iota(jnp.int32, (EXPERTS, count), 0) + base
+    expert = jnp.where(expert >= EXPERTS, expert - EXPERTS, expert)
     chosen = expert == routes[0:1]
     for k in range(1, routes.shape[0]):
         chosen = chosen | (expert == routes[k : k + 1])
@@ -247,66 +289,80 @@
     )
     rank = dot_nn(chosen[:rows].astype(BF16), earlier.astype(F32).astype(BF16))
     rank = jnp.where(chosen[:rows] > 0.5, rank, -1.0)
-    parts = []
     slot = lax.broadcasted_iota(jnp.int32, (SLOTS, count), 0).astype(F32)
-    for j in range(local):
-        parts.append((slot == rank[j : j + 1]).astype(F32))
+    parts = [(slot == rank[j : j + 1]).astype(F32) for j in range(local)]
     return jnp.concatenate(parts, axis=0), chosen
 
 
-def dispatch_grads_kernel(local, routes_ref, grads_ref, shared_ref, *rest):
-    slot_ref, raw_ref = rest[-2:]
-    pick, _ = pick_rows(routes_ref[...], local)
-    grads = grads_ref[...]
-    slot_ref[...] = (
-        dot_nn(pick.astype(BF16), grads).astype(BF16).reshape(local, SLOTS, grads.shape[1])
-    )
-    raw_ref[...] = dot_nt(shared_ref[...], grads)
-
-
-def dispatch_rows_kernel(
-    local, units, routes_ref, rows_ref, router_ref, shared_ref, raw_ref, *rest
-):
-    slot_ref, info_ref, pick_ref, gate_ref, hidden_ref, back_ref = rest[-6:]
-    pick, chosen = pick_rows(routes_ref[...], local)
-    rows = rows_ref[...]
-    low = pick.astype(BF16)
-    pick_ref[...] = low
-    slot_ref[...] = dot_nn(low, rows).astype(BF16).reshape(local, SLOTS, rows.shape[1])
-    sigmoid = chosen / (1.0 + jnp.exp(-dot_nt(router_ref[...], rows)))
-    total = jnp.sum(sigmoid, axis=0, keepdims=True)
-    gate_ref[0] = sigmoid
-    gate_ref[1] = jnp.broadcast_to(total, sigmoid.shape)
-    weight = ROUTE_SCALE * sigmoid / total
-    scale = jnp.concatenate(
-        [
-            jnp.sum(pick[j * SLOTS : (j + 1) * SLOTS] * weight[j : j + 1], axis=1, keepdims=True)
-            for j in range(local)
-        ],
-        axis=0,
-    )
-    high, low_part = split_high(scale)
-    lane = lax.broadcasted_iota(jnp.int32, (scale.shape[0], LANES), 1)
-    info = jnp.where(lane == 0, high.astype(F32), jnp.where(lane == 1, low_part.astype(F32), 0.0))
-    info_ref[...] = info.astype(BF16).reshape(local, SLOTS, LANES)
-    shared = dot_nt(shared_ref[...], rows)
-    gate, up, raw = shared[:units], shared[units:], raw_ref[...]
-    smooth, active = silu_parts(gate)
-    hidden_ref[...] = (active * up).astype(BF16)
-    back_ref[...] = jnp.concatenate(
-        [raw * up * smooth * (1.0 + gate * (1.0 - smooth)), raw * active], axis=0
-    ).astype(BF16)
+def dispatch_grads_kernel(local, base_ref, *refs):
+    routes, grads, shared_ref = refs[:2], refs[2:4], refs[4]
+    slot_ref, raw_ref = refs[-2:]
+    for i in range(2):
+
+        @pl.when(pl.program_id(0) == i)
+        def _():
+            pick, _ = pick_rows(routes[i][...], base_ref[0], local)
+            values = grads[i][...]
+            slot_ref[...] = (
+                dot_nn(pick.astype(BF16), values).astype(BF16).reshape(slot_ref.shape)
+            )
+            raw_ref[0] = dot_nt(shared_ref[...], values)
+
+
+def dispatch_rows_kernel(local, units, base_ref, *refs):
+    routes, pieces, side_ref, raw_ref = refs[:2], refs[2:4], refs[4], refs[5]
+    slot_ref, info_ref, pick_ref, gate_ref, hidden_ref, back_ref = refs[-6:]
+    for i in range(2):
+
+        @pl.when(pl.program_id(0) == i)
+        def _():
+            pick, chosen = pick_rows(routes[i][...], base_ref[0], local)
+            rows = pieces[i][...]
+            low = pick.astype(BF16)
+            pick_ref[0] = low
+            slot_ref[...] = dot_nn(low, rows).astype(BF16).reshape(slot_ref.shape)
+            side = dot_nt(side_ref[...], rows)
+            gate, up, raw = side[:units], side[units : 2 * units], raw_ref[0]
+            sigmoid = chosen / (1.0 + jnp.exp(-side[2 * units :]))
+            total = jnp.sum(sigmoid, axis=0, keepdims=True)
+            gate_ref[0, 0] = sigmoid
+            gate_ref[0, 1] = jnp.broadcast_to(total, sigmoid.shape)
+            weight = ROUTE_SCALE * sigmoid / total
+            scale = jnp.concatenate(
+                [
+                    jnp.sum(
+                        pick[j * SLOTS : (j + 1) * SLOTS] * weight[j : j + 1],
+                        axis=1,
+                        keepdims=True,
+                    )
+                    for j in range(local)
+                ],
+                axis=0,
+            )
+            high, low_part = split_high(scale)
+            lane = lax.broadcasted_iota(jnp.int32, (scale.shape[0], LANES), 1)
+            info = jnp.where(
+                lane == 0, high.astype(F32), jnp.where(lane == 1, low_part.astype(F32), 0.0)
+            )
+            info_ref[...] = info.astype(BF16).reshape(info_ref.shape)
+            smooth, active = silu_parts(gate)
+            hidden_ref[0] = (active * up).astype(BF16)
+            back_ref[0] = jnp.concatenate(
+                [raw * up * smooth * (1.0 + gate * (1.0 - smooth)), raw * active], axis=0
+            ).astype(BF16)
+
+
+def expert_raw_kernel(grads_ref, out_ref, raw_ref):
+    raw_ref[0] = dot_nt(out_ref[0], grads_ref[0])
 
 
 def expert_kernel(
-    units, rows_ref, grads_ref, info_ref, in_ref, out_ref, out_rows_ref, back_rows_ref, extra_ref,
-    hidden_ref, back_ref,
+    units, rows_ref, info_ref, in_ref, raw_ref, back_rows_ref, extra_ref, hidden_ref, back_ref
 ):
     expert = pl.program_id(0)
-    rows, grads = rows_ref[0], grads_ref[0]
-    weight_in, weight_out = in_ref[0], out_ref[0]
-    gates = dot_nt(weight_in, rows)
-    raw = dot_nt(weight_out, grads)
+    weight_in = in_ref[0]
+    gates = dot_nt(weight_in, rows_ref[0])
+    raw = raw_ref[0]
     gate, up = gates[:units], gates[units:]
     lane = lax.broadcasted_iota(jnp.int32, (16, LANES), 1)
     select = (lane < 2).astype(F32).astype(BF16)
@@ -314,14 +370,12 @@
     smooth, active = silu_parts(gate)
     hidden = active * up
     grad_gate = jnp.sum(hidden.astype(BF16).astype(F32) * raw, axis=0, keepdims=True)
-    scaled = (hidden * scale).astype(BF16)
+    hidden_ref[0] = (hidden * scale).astype(BF16)
     raw = raw * scale
     back = jnp.concatenate(
         [raw * up * smooth * (1.0 + gate * (1.0 - smooth)), raw * active], axis=0
     ).astype(BF16)
-    hidden_ref[0] = scaled
     back_ref[0] = back
-    out_rows_ref[0] = dot_tn(scaled, weight_out).astype(BF16)
     back_rows_ref[0] = dot_tn(back, weight_in).astype(BF16)
     high, low = split_high(grad_gate)
     row = lax.broadcasted_iota(jnp.int32, (16, grad_gate.shape[1]), 0)
@@ -332,7 +386,13 @@
     extra_ref[0] = dot_tn(pair.astype(BF16), place.astype(BF16)).astype(BF16)
 
 
-def weight_grad_kernel(rows_ref, grads_ref, hidden_ref, back_ref, in_ref, out_ref):
+def expert_out_kernel(hidden_ref, out_ref, rows_ref):
+    rows_ref[0] = dot_tn(hidden_ref[0], out_ref[0]).astype(BF16)
+
+
+def weight_grad_kernel(rows_ref, grads_ref, hidden_ref, back_ref, *rest):
+    in_ref, out_ref = rest[-2:]
+
     @pl.when(pl.program_id(1) == 0)
     def _():
         in_ref[0] = dot_nn(back_ref[0], rows_ref[0])
@@ -345,97 +405,133 @@
 
 
 def combine_back_kernel(
-    local, pick_ref, slots_ref, extra_ref, gate_ref, router_ref, back_ref, shared_ref,
-    tokens_ref, logits_ref,
+    pick_ref, slots_ref, extra_ref, gate_ref, back_ref, side_ref, *rest
 ):
-    pick = pick_ref[...]
-    flat = local * SLOTS
-    merged = dot_tn(extra_ref[...].reshape(flat, LANES), pick)
-    grad_gate = merged[:EXPERTS] + merged[EXPERTS:]
-    sigmoid, total = gate_ref[0], gate_ref[1]
-    mixed = jnp.sum(grad_gate * sigmoid, axis=0, keepdims=True)
-    logits = ROUTE_SCALE * (grad_gate / total - mixed / (total * total)) * sigmoid * (1.0 - sigmoid)
-    logits = logits.astype(BF16)
-    logits_ref[...] = logits
-    tokens_ref[...] = (
-        dot_tn(pick, slots_ref[...].reshape(flat, slots_ref.shape[2]))
-        + dot_tn(back_ref[...], shared_ref[...])
-        + dot_tn(logits, router_ref[...])
+    first_ref, second_ref, logits_ref, left_ref = rest[-4:]
+    piece, part = pl.program_id(0), pl.program_id(1)
+    flat = pick_ref.shape[1]
+    units = back_ref.shape[1]
+
+    @pl.when(part == 0)
+    def _():
+        merged = dot_tn(extra_ref[...].reshape(flat, LANES), pick_ref[0])
+        grad_gate = merged[:EXPERTS] + merged[EXPERTS:]
+        sigmoid, total = gate_ref[0, 0], gate_ref[0, 1]
+        mixed = jnp.sum(grad_gate * sigmoid, axis=0, keepdims=True)
+        logits = (
+            ROUTE_SCALE
+            * (grad_gate / total - mixed / (total * total))
+            * sigmoid
+            * (1.0 - sigmoid)
+        ).astype(BF16)
+        logits_ref[0] = logits
+        left_ref[:units] = back_ref[0]
+        left_ref[units:] = logits
+
+    value = (
+        dot_tn(pick_ref[0], slots_ref[...].reshape(flat, slots_ref.shape[2]))
+        + dot_tn(left_ref[...], side_ref[...])
     ).astype(BF16)
 
-
-def combine_out_kernel(local, pick_ref, slots_ref, hidden_ref, shared_ref, tokens_ref):
-    tokens_ref[...] = (
-        dot_tn(pick_ref[...], slots_ref[...].reshape(local * SLOTS, slots_ref.shape[2]))
-        + dot_tn(hidden_ref[...], shared_ref[...])
+    @pl.when(piece == 0)
+    def _():
+        first_ref[...] = value
+
+    @pl.when(piece == 1)
+    def _():
+        second_ref[...] = value
+
+
+def combine_out_kernel(pick_ref, slots_ref, hidden_ref, shared_ref, first_ref, second_ref):
+    value = (
+        dot_tn(pick_ref[0], slots_ref[...].reshape(pick_ref.shape[1], slots_ref.shape[2]))
+        + dot_tn(hidden_ref[0], shared_ref[...])
     ).astype(BF16)
 
-
-def whole(shape):
-    return pl.BlockSpec(shape, lambda *_: (0,) * len(shape))
-
-
-def strip(local, place, width):
-    return pl.BlockSpec((local, SLOTS, width), lambda *_: (0, place, 0))
-
-
-def params(*semantics):
-    return pltpu.CompilerParams(
-        dimension_semantics=semantics or None, vmem_limit_bytes=56 * 1024 * 1024
-    )
-
-
-def dispatch_grads(place, sequences, local, routes, grads, shared_out, slots):
-    count, width = grads.shape
+    @pl.when(pl.program_id(0) == 0)
+    def _():
+        first_ref[...] = value
+
+    @pl.when(pl.program_id(0) == 1)
+    def _():
+        second_ref[...] = value
+
+
+def chain_call(kernel, name, grid, prefetch, operands, in_specs, held, out_specs, out_shape, scratch=()):
+    chained = [a for a in held if a is not None]
+    at = len(prefetch) + len(operands)
+    return pl.pallas_call(
+        kernel,
+        grid_spec=pltpu.PrefetchScalarGridSpec(
+            num_scalar_prefetch=len(prefetch),
+            grid=grid,
+            in_specs=in_specs + [ANYWHERE] * len(chained),
+            out_specs=out_specs,
+            scratch_shapes=list(scratch),
+        ),
+        out_shape=out_shape,
+        input_output_aliases={at + i: i for i in range(len(chained))},
+        compiler_params=params(*["arbitrary"] * len(grid)),
+        name=name,
+    )(*prefetch, *operands, *chained)
+
+
+def dispatch_grads(pair, sequences, local, base, routes, grads, shared_out, held):
+    count, width = grads[0].shape
     units = shared_out.shape[0]
-    first = slots is None
-    operands = [routes, grads, shared_out] + ([] if first else [slots])
-    return pl.pallas_call(
+    operands = [*routes, *grads, shared_out]
+    return chain_call(
         functools.partial(dispatch_grads_kernel, local),
-        grid=(1,),
-        in_specs=[whole(a.shape) for a in operands[:3]]
-        + ([] if first else [pl.BlockSpec(memory_space=pl.ANY)]),
-        out_specs=[strip(local, place, width), whole((units, count))],
-        out_shape=[
+        "dispatch_grads",
+        (2,),
+        [base],
+        operands,
+        [whole(a.shape) for a in operands],
+        held,
+        [
+            pl.BlockSpec((local, SLOTS, width), lambda i, *_: (0, 2 * pair + i, 0)),
+            pl.BlockSpec((1, units, count), lambda i, *_: (2 * pair + i, 0, 0)),
+        ],
+        [
             jax.ShapeDtypeStruct((local, sequences * SLOTS, width), BF16),
-            jax.ShapeDtypeStruct((units, count), F32),
-        ],
-        input_output_aliases={} if first else {3: 0},
-        compiler_params=params(),
-        name="dispatch_grads",
-    )(*operands)
-
-
-def dispatch_rows(place, sequences, local, routes, rows, router, shared_in, raw, slots, infos):
-    count, width = rows.shape
-    units = raw.shape[0]
-    first = slots is None
-    operands = [routes, rows, router, shared_in, raw] + ([] if first else [slots, infos])
-    anywhere = pl.BlockSpec(memory_space=pl.ANY)
-    return pl.pallas_call(
+            jax.ShapeDtypeStruct((sequences, units, count), F32),
+        ],
+    )
+
+
+def dispatch_rows(pair, sequences, local, base, routes, rows, side, raws, held):
+    count, width = rows[0].shape
+    units = raws.shape[1]
+    operands = [*routes, *rows, side]
+    shapes = [
+        ((local * SLOTS, count), BF16),
+        ((2, EXPERTS, count), F32),
+        ((units, count), BF16),
+        ((2 * units, count), BF16),
+    ]
+
+    def at(shape):
+        return pl.BlockSpec((1,) + shape, lambda i, *_: (2 * pair + i,) + (0,) * len(shape))
+
+    return chain_call(
         functools.partial(dispatch_rows_kernel, local, units),
-        grid=(1,),
-        in_specs=[whole(a.shape) for a in operands[:5]] + ([] if first else [anywhere, anywhere]),
-        out_specs=[
-            strip(local, place, width),
-            strip(local, place, LANES),
-            whole((local * SLOTS, count)),
-            whole((2, EXPERTS, count)),
-            whole((units, count)),
-            whole((2 * units, count)),
-        ],
-        out_shape=[
+        "dispatch_rows",
+        (2,),
+        [base],
+        operands + [raws],
+        [whole(a.shape) for a in operands] + [at((units, count))],
+        held,
+        [
+            pl.BlockSpec((local, SLOTS, width), lambda i, *_: (0, 2 * pair + i, 0)),
+            pl.BlockSpec((local, SLOTS, LANES), lambda i, *_: (0, 2 * pair + i, 0)),
+        ]
+        + [at(shape) for shape, _ in shapes],
+        [
             jax.ShapeDtypeStruct((local, sequences * SLOTS, width), BF16),
             jax.ShapeDtypeStruct((local, sequences * SLOTS, LANES), BF16),
-            jax.ShapeDtypeStruct((local * SLOTS, count), BF16),
-            jax.ShapeDtypeStruct((2, EXPERTS, count), F32),
-            jax.ShapeDtypeStruct((units, count), BF16),
-            jax.ShapeDtypeStruct((2 * units, count), BF16),
-        ],
-        input_output_aliases={} if first else {5: 0, 6: 1},
-        compiler_params=params(),
-        name="dispatch_rows",
-    )(*operands)
+        ]
+        + [jax.ShapeDtypeStruct((sequences,) + shape, dtype) for shape, dtype in shapes],
+    )
 
 
 def tile(*shape):
@@ -450,22 +546,35 @@
     return pl.BlockSpec((1,) + shape, lambda j, b: (j, 0, 0))
 
 
-def expert_rows(rows, grads, infos, expert_in, expert_out):
+def expert_raw(grads, expert_out):
+    local, slots, width = grads.shape
+    units = expert_out.shape[1]
+    block = min(slots, SLOT_BLOCK)
+    return pl.pallas_call(
+        expert_raw_kernel,
+        grid=(local, slots // block),
+        in_specs=[tile(block, width), one(units, width)],
+        out_specs=lane_tile(units, block),
+        out_shape=jax.ShapeDtypeStruct((local, units, slots), F32),
+        compiler_params=params("arbitrary", "arbitrary"),
+        name="expert_raw",
+    )(grads, expert_out)
+
+
+def expert_rows(rows, infos, expert_in, raw):
     local, slots, width = rows.shape
-    units = expert_out.shape[1]
+    units = raw.shape[1]
     block = min(slots, SLOT_BLOCK)
     return pl.pallas_call(
         functools.partial(expert_kernel, units),
         grid=(local, slots // block),
         in_specs=[
             tile(block, width),
-            tile(block, width),
             tile(block, LANES),
             one(2 * units, width),
-            one(units, width),
+            lane_tile(units, block),
         ],
         out_specs=[
-            tile(block, width),
             tile(block, width),
             tile(block, LANES),
             lane_tile(units, block),
@@ -473,111 +582,662 @@
         ],
         out_shape=[
             jax.ShapeDtypeStruct((local, slots, width), BF16),
-            jax.ShapeDtypeStruct((local, slots, width), BF16),
             jax.ShapeDtypeStruct((local, slots, LANES), BF16),
             jax.ShapeDtypeStruct((local, units, slots), BF16),
             jax.ShapeDtypeStruct((local, 2 * units, slots), BF16),
         ],
         compiler_params=params("arbitrary", "arbitrary"),
         name="expert_rows",
-    )(rows, grads, infos, expert_in, expert_out)
-
-
-def weight_grads(rows, grads, hidden, back):
+    )(rows, infos, expert_in, raw)
+
+
+def expert_out_rows(hidden, expert_out):
+    local, units, slots = hidden.shape
+    width = expert_out.shape[2]
+    block = min(slots, SLOT_BLOCK)
+    return pl.pallas_call(
+        expert_out_kernel,
+        grid=(local, slots // block),
+        in_specs=[lane_tile(units, block), one(units, width)],
+        out_specs=tile(block, width),
+        out_shape=jax.ShapeDtypeStruct((local, slots, width), BF16),
+        compiler_params=params("arbitrary", "arbitrary"),
+        name="expert_out_rows",
+    )(hidden, expert_out)
+
+
+def weight_grads(start, stop, rows, grads, hidden, back, held):
     local, slots, width = rows.shape
     units = hidden.shape[1]
     block = min(slots, SLOT_BLOCK)
-    return pl.pallas_call(
+
+    def moved(spec):
+        return pl.BlockSpec(
+            spec.block_shape, lambda j, b: (lambda at: (at[0] + start,) + at[1:])(spec.index_map(j, b))
+        )
+
+    return chain_call(
         weight_grad_kernel,
-        grid=(local, slots // block),
-        in_specs=[
-            tile(block, width),
-            tile(block, width),
-            lane_tile(units, block),
-            lane_tile(2 * units, block),
-        ],
-        out_specs=[one(2 * units, width), one(units, width)],
-        out_shape=[
+        "weight_grads",
+        (stop - start, slots // block),
+        [],
+        [rows, grads, hidden, back],
+        [
+            moved(spec)
+            for spec in (
+                tile(block, width),
+                tile(block, width),
+                lane_tile(units, block),
+                lane_tile(2 * units, block),
+            )
+        ],
+        held,
+        [moved(one(2 * units, width)), moved(one(units, width))],
+        [
             jax.ShapeDtypeStruct((local, 2 * units, width), F32),
             jax.ShapeDtypeStruct((local, units, width), F32),
         ],
+    )
+
+
+def piece_specs(width, part):
+    return [
+        pl.BlockSpec((width[0], part), lambda i, h: (0, jnp.where(i == 0, h, width[1] - 1))),
+        pl.BlockSpec((width[0], part), lambda i, h: (0, jnp.where(i == 0, 0, h))),
+    ]
+
+
+def combine_back(pair, picks, slots, extra, gates, backs, side, held):
+    sequences, flat, count = picks.shape
+    local, _, width = slots.shape
+    part = width // PARTS
+
+    def at(array):
+        shape = array.shape[1:]
+        return pl.BlockSpec((1,) + shape, lambda i, h: (2 * pair + i,) + (0,) * len(shape))
+
+    def strip(size):
+        return pl.BlockSpec((local, SLOTS, size), lambda i, h: (0, 2 * pair + i, 0))
+
+    outs = chain_call(
+        lambda *refs: combine_back_kernel(*refs[:6], *refs[-3:-1], refs[-4], refs[-1]),
+        "combine_back",
+        (2, PARTS),
+        [],
+        [picks, slots, extra, gates, backs, side],
+        [
+            at(picks),
+            pl.BlockSpec((local, SLOTS, part), lambda i, h: (0, 2 * pair + i, h)),
+            strip(LANES),
+            at(gates),
+            at(backs),
+            pl.BlockSpec((side.shape[0], part), lambda i, h: (0, h)),
+        ],
+        held,
+        [pl.BlockSpec((1, EXPERTS, count), lambda i, h: (2 * pair + i, 0, 0))]
+        + piece_specs((count, PARTS), part),
+        [jax.ShapeDtypeStruct((sequences, EXPERTS, count), BF16)]
+        + [jax.ShapeDtypeStruct((count, width), BF16)] * 2,
+        [pltpu.VMEM((side.shape[0], count), BF16)],
+    )
+    return outs[1:], outs[:1]
+
+
+def combine_out(pair, picks, slots, hiddens, shared_out):
+    _, flat, count = picks.shape
+    local, _, width = slots.shape
+    part = width // PARTS
+    units = hiddens.shape[1]
+    return pl.pallas_call(
+        combine_out_kernel,
+        grid=(2, PARTS),
+        in_specs=[
+            pl.BlockSpec((1, flat, count), lambda i, h: (2 * pair + i, 0, 0)),
+            pl.BlockSpec((local, SLOTS, part), lambda i, h: (0, 2 * pair + i, h)),
+            pl.BlockSpec((1, units, count), lambda i, h: (2 * pair + i, 0, 0)),
+            pl.BlockSpec((units, part), lambda i, h: (0, h)),
+        ],
+        out_specs=piece_specs((count, PARTS), part),
+        out_shape=[jax.ShapeDtypeStruct((count, width), BF16)] * 2,
         compiler_params=params("arbitrary", "arbitrary"),
-        name="weight_grads",
-    )(rows, grads, hidden, back)
-
-
-def combine_back(place, local, pick, slots, extra, gates, router, back, shared_in):
-    count, width = pick.shape[1], slots.shape[2]
+        name="combine_out",
+    )(picks, slots, hiddens, shared_out)
+
+
+def side_grads_kernel(sequences, block_ref, *refs):
+    rows, grads, rest = refs[:sequences], refs[sequences : 2 * sequences], refs[2 * sequences :]
+    logits_ref, hidden_ref, back_ref, first_ref, *parts, router_ref, left_ref, in_ref, out_ref = rest
+    units = hidden_ref.shape[1]
+    for s in range(sequences):
+        left_ref[: 2 * units] = back_ref[s]
+        left_ref[2 * units :] = logits_ref[s]
+        value = dot_nn(left_ref[...], rows[s][...])
+        other = dot_nn(hidden_ref[s], grads[s][...])
+        if s == 0:
+            in_ref[...] = value
+            out_ref[...] = other
+        else:
+            in_ref[...] += value
+            out_ref[...] += other
+    shards, columns = len(parts), parts[0].shape[1]
+    for k in range(shards):
+        at = pl.ds(pl.multiple_of(block_ref[k] * columns, columns), columns)
+        parts[k][: 2 * units] = in_ref[: 2 * units, at].astype(BF16)
+        parts[k][2 * units :] = out_ref[:, at].astype(BF16)
+    local = EXPERTS // shards
+    for k in range(shards):
+        start = first_ref[0] + k * local
+        start = jnp.where(start >= EXPERTS, start - EXPERTS, start)
+        router_ref[pl.ds(pl.multiple_of(start, local), local)] = in_ref[
+            2 * units + k * local : 2 * units + (k + 1) * local
+        ]
+
+
+def side_grads(blocks, base, rows, grads, logits, hiddens, backs):
+    sequences = len(rows)
+    count, width = rows[0].shape
+    units = hiddens.shape[1]
+    shards = blocks.shape[0]
+    operands = [*rows, *grads, logits, hiddens, backs]
     return pl.pallas_call(
-        functools.partial(combine_back_kernel, local),
-        grid=(1,),
-        in_specs=[
-            whole(pick.shape), strip(local, place, width), strip(local, place, LANES),
-            whole(gates.shape), whole(router.shape), whole(back.shape), whole(shared_in.shape),
-        ],
-        out_specs=[whole((count, width)), whole((EXPERTS, count))],
-        out_shape=[
+        functools.partial(side_grads_kernel, sequences),
+        grid_spec=pltpu.PrefetchScalarGridSpec(
+            num_scalar_prefetch=1,
+            grid=(1,),
+            in_specs=[whole(a.shape) for a in operands]
+            + [pl.BlockSpec(memory_space=pltpu.SMEM)],
+            out_specs=[whole((3 * units, width // shards))] * shards + [whole((EXPERTS, width))],
+            scratch_shapes=[
+                pltpu.VMEM((2 * units + EXPERTS, count), BF16),
+                pltpu.VMEM((2 * units + EXPERTS, width), F32),
+                pltpu.VMEM((units, width), F32),
+            ],
+        ),
+        out_shape=[jax.ShapeDtypeStruct((3 * units, width // shards), BF16)] * shards
+        + [jax.ShapeDtypeStruct((EXPERTS, width), F32)],
+        compiler_params=params("arbitrary"),
+        name="side_grads",
+    )(blocks, *operands, base)
+
+
+def join_columns_kernel(block_ref, *refs):
+    pieces, router_ref, side_ref, out_ref = refs[:-3], refs[-3], refs[-2], refs[-1]
+    units = out_ref.shape[0]
+    columns = pieces[0].shape[1]
+    for k, piece in enumerate(pieces):
+        at = pl.ds(pl.multiple_of(block_ref[k] * columns, columns), columns)
+        side_ref[: 2 * units, at] = piece[: 2 * units]
+        out_ref[:, at] = piece[2 * units :]
+    side_ref[2 * units :] = router_ref[...]
+
+
+def join_rows_kernel(units, block_ref, *refs):
+    parts, in_ref, out_ref = refs[:-2], refs[-2], refs[-1]
+    padded = parts[0].shape[0] // 3
+    for k, part in enumerate(parts):
+        at = pl.ds(pl.multiple_of(block_ref[k] * units, 8), units)
+        value = part[...].astype(F32)
+        in_ref[0, at] = value[:units]
+        in_ref[1, at] = value[padded : padded + units]
+        out_ref[at] = value[2 * padded : 2 * padded + units]
+
+
+def sum_split_kernel(depth_ref, own_ref, x_ref, y_ref, *outs):
+    size = outs[0].shape[0]
+    for k, out in enumerate(outs):
+        at = pl.ds(pl.multiple_of(depth_ref[k] * size, size), size)
+        out[...] = (
+            own_ref[at].astype(F32) + x_ref[at].astype(F32) + y_ref[at].astype(F32)
+        ).astype(BF16)
+
+
+def join_depth_kernel(depth_ref, *refs):
+    pieces, out_ref = refs[:-1], refs[-1]
+    size = pieces[0].shape[0]
+    for k, piece in enumerate(pieces):
+        out_ref[pl.ds(pl.multiple_of(depth_ref[k] * size, size), size)] = piece[...]
+
+
+def replicated_kernel(used, block_ref, *refs):
+    chunks, latent_ref, router_ref, gains_ref = refs[:-3], refs[-3], refs[-2], refs[-1]
+    columns = chunks[0].shape[1]
+    for k, chunk in enumerate(chunks):
+        at = pl.ds(pl.multiple_of(block_ref[k] * columns, columns), columns)
+        latent_ref[:, at] = chunk[:used].astype(F32)
+        router_ref[:, at] = chunk[used : used + EXPERTS].astype(F32)
+        gains_ref[:, at] = chunk[used + EXPERTS : used + EXPERTS + 16].astype(F32)
+
+
+def rope_turn(first, second, cosine, sine):
+    return first * cosine - second * sine, first * sine + second * cosine
+
+
+def unit_rows(pieces):
+    values = jnp.concatenate([piece[...] for piece in pieces], axis=0).astype(F32)
+    inverse = lax.rsqrt(jnp.mean(values * values, axis=-1, keepdims=True) + EPSILON)
+    return values * inverse
+
+
+def latent_kernel(depth, *refs):
+    pieces = refs[:depth]
+    gain_ref, weight_ref, kv_gain_ref, cosine_ref, sine_ref = refs[depth : depth + 5]
+    normed_ref, comp_ref, low_ref, key_ref = refs[depth + 5 :]
+    normed = (unit_rows(pieces) * gain_ref[...]).astype(BF16)
+    normed_ref[...] = normed
+    latent = dot_nt(normed, weight_ref[...])
+    compressed = latent[:, :KVR]
+    comp_ref[...] = compressed
+    inverse = lax.rsqrt(jnp.mean(compressed * compressed, axis=-1, keepdims=True) + EPSILON)
+    low_ref[...] = (compressed * inverse * kv_gain_ref[...]).astype(BF16)
+    first, second = rope_turn(
+        latent[:, KVR : KVR + LANES], latent[:, KVR + LANES :], cosine_ref[...], sine_ref[...]
+    )
+    key_ref[...] = jnp.concatenate([first, second], axis=1).astype(BF16)
+
+
+def head_mask(head):
+    lane = lax.broadcasted_iota(jnp.int32, (1, LANES), 1)
+    return ((lane // (ROPE // 2)) == head).astype(F32)
+
+
+def keyval_weight(block_ref, packs, whole_ref, queries):
+    share = KVR // len(packs)
+    count = packs[0].shape[0] // share
+    columns = whole_ref.shape[1] // count
+    for k, pack in enumerate(packs):
+        start = pl.multiple_of(block_ref[k] * share, share)
+        for i in range(count):
+            whole_ref[pl.ds(start, share), i * columns : (i + 1) * columns] = pack[
+                i * share : (i + 1) * share, queries : queries + columns
+            ]
+
+
+def attention_kernel(heads, block_ref, *refs):
+    shards = len(refs) - 13
+    packs = refs[:shards]
+    normed_ref, low_ref, key_ref, bias_ref, cosine_ref, sine_ref = refs[shards : shards + 6]
+    query_ref, keyval_ref, soft_ref, attended_ref, part_ref, total_ref, weight_ref = refs[
+        shards + 6 :
+    ]
+    share = packs[0].shape[0]
+    nope = heads * NOPE
+    queries = heads * (NOPE + ROPE)
+    keyval_columns = keyval_ref.shape[1] * (KVR // shards) // share
+    keyval_weight(block_ref, packs, weight_ref, queries)
+    for k, pack in enumerate(packs):
+        start = pl.multiple_of(block_ref[k] * share, share)
+        value = dot_nn(normed_ref[:, pl.ds(start, share)], pack[:, :queries])
+        if k == 0:
+            total_ref[...] = value
+        else:
+            total_ref[...] += value
+    keyval_ref[...] = dot_nn(low_ref[...], weight_ref[...]).astype(BF16)
+    first, second = rope_turn(
+        total_ref[:, nope : nope + LANES], total_ref[:, nope + LANES :], cosine_ref[...], sine_ref[...]
+    )
+    query_ref[:, :nope] = total_ref[:, :nope].astype(BF16)
+    query_ref[:, nope : nope + LANES] = first.astype(BF16)
+    query_ref[:, nope + LANES :] = second.astype(BF16)
+    for head in range(heads):
+        mask = head_mask(head)
+        at = head * (NOPE + VD)
+        turned = jnp.concatenate([first * mask, second * mask], axis=1).astype(BF16)
+        scores = dot_nt(
+            query_ref[:, head * NOPE : (head + 1) * NOPE], keyval_ref[:, at : at + NOPE]
+        ) + dot_nt(turned, key_ref[...])
+        scores = scores * ((NOPE + ROPE) ** (-0.5)) + bias_ref[...]
+        raised = jnp.exp(scores - jnp.max(scores, axis=-1, keepdims=True))
+        soft = raised / jnp.sum(raised, axis=-1, keepdims=True)
+        soft_ref[head] = soft
+        attended_ref[:, head * VD : (head + 1) * VD] = dot_nn(
+            soft.astype(BF16), keyval_ref[:, at + NOPE : at + NOPE + VD]
+        ).astype(BF16)
+    output = queries + keyval_columns
+    columns = part_ref.shape[1] // shards
+    for k, pack in enumerate(packs):
+        start = pl.multiple_of(block_ref[k] * columns, columns)
+        value = dot_nn(attended_ref[:, :share], pack[:, output : output + columns])
+        for i in range(1, heads * VD // share):
+            value += dot_nn(
+                attended_ref[:, i * share : (i + 1) * share],
+                pack[:, output + i * columns : output + (i + 1) * columns],
+            )
+        part_ref[:, pl.ds(start, columns)] = value.astype(BF16)
+
+
+def attention_back_kernel(heads, depth, block_ref, *refs):
+    shards = (len(refs) - 2 * depth - 22) // 2
+    packs, refs = refs[:shards], refs[shards:]
+    tokens, refs = refs[:depth], refs[depth:]
+    grads, refs = refs[:depth], refs[depth:]
+    (
+        query_ref, keyval_ref, key_ref, soft_ref, attended_ref, comp_ref, low_ref, normed_ref,
+        latent_ref, kv_gain_ref, cosine_ref, sine_ref, router_ref, ffn_gain_ref,
+        grad_query_ref, grad_keyval_ref, grad_normed_ref, *chunk_refs,
+        gains_ref, grad_attended_ref, weight_ref, back_ref, stage_ref,
+    ) = refs
+    share = packs[0].shape[0]
+    own = tokens[0].shape[0]
+    nope = heads * NOPE
+    queries = heads * (NOPE + ROPE)
+    keyval_columns = keyval_ref.shape[1] * (KVR // shards) // share
+    output = queries + keyval_columns
+    columns = normed_ref.shape[1] // shards
+    scale = (NOPE + ROPE) ** (-0.5)
+    for z, piece in enumerate(grads):
+        stage_ref[z * own : (z + 1) * own] = piece[...]
+    blocks = heads * VD // share
+    for i in range(blocks):
+        value = None
+        for k, pack in enumerate(packs):
+            start = pl.multiple_of(block_ref[k] * columns, columns)
+            part = dot_nt(
+                stage_ref[:, pl.ds(start, columns)],
+                pack[:, output + i * columns : output + (i + 1) * columns],
+            )
+            value = part if value is None else value + part
+        grad_attended_ref[:, i * share : (i + 1) * share] = value.astype(BF16)
+    cosine, sine = cosine_ref[...], sine_ref[...]
+    turn_first, turn_second = None, None
+    key_turn = None
+    for head in range(heads):
+        mask = head_mask(head)
+        at = head * (NOPE + VD)
+        soft = soft_ref[head]
+        attended = attended_ref[:, head * VD : (head + 1) * VD]
+        grad = grad_attended_ref[:, head * VD : (head + 1) * VD]
+        delta = jnp.sum(grad.astype(F32) * attended.astype(F32), axis=-1, keepdims=True)
+        grad_soft = dot_nt(grad, keyval_ref[:, at + NOPE : at + NOPE + VD])
+        scores = (soft * (grad_soft - delta) * scale).astype(BF16)
+        query = query_ref[:, head * NOPE : (head + 1) * NOPE]
+        grad_query_ref[:, head * NOPE : (head + 1) * NOPE] = dot_nn(
+            scores, keyval_ref[:, at : at + NOPE]
+        ).astype(BF16)
+        turned = dot_nn(scores, key_ref[...])
+        first, second = turned[:, :LANES] * mask, turned[:, LANES:] * mask
+        turn_first = first if turn_first is None else turn_first + first
+        turn_second = second if turn_second is None else turn_second + second
+        wide = jnp.concatenate([mask, mask], axis=1)
+        masked = (query_ref[:, nope:].astype(F32) * wide).astype(BF16)
+        part = dot_tn(scores, masked)
+        key_turn = part if key_turn is None else key_turn + part
+        grad_keyval_ref[:, at : at + NOPE] = dot_tn(scores, query).astype(BF16)
+        grad_keyval_ref[:, at + NOPE : at + NOPE + VD] = dot_tn(soft.astype(BF16), grad).astype(BF16)
+    first, second = rope_turn(turn_first, turn_second, cosine, -sine)
+    grad_query_ref[:, nope : nope + LANES] = first.astype(BF16)
+    grad_query_ref[:, nope + LANES :] = second.astype(BF16)
+    keyval_weight(block_ref, packs, weight_ref, queries)
+    grad_comp = dot_nt(grad_keyval_ref[...], weight_ref[...])
+    compressed = comp_ref[...]
+    inverse = lax.rsqrt(jnp.mean(compressed * compressed, axis=-1, keepdims=True) + EPSILON)
+    weighted = grad_comp * kv_gain_ref[...]
+    grad_compressed = inverse * weighted - compressed * (inverse * inverse * inverse) * jnp.mean(
+        compressed * weighted, axis=-1, keepdims=True
+    )
+    gains_ref[...] = jnp.zeros_like(gains_ref)
+    gains_ref[2:3, :KVR] = jnp.sum(grad_comp * compressed * inverse, axis=0, keepdims=True)
+    back_ref[:, :KVR] = grad_compressed.astype(BF16)
+    first, second = rope_turn(key_turn[:, :LANES], key_turn[:, LANES:], cosine, -sine)
+    back_ref[:, KVR : KVR + LANES] = first.astype(BF16)
+    back_ref[:, KVR + LANES :] = second.astype(BF16)
+    unit = unit_rows(tokens)
+    half = ROPE // 2
+    for k, pack in enumerate(packs):
+        start = pl.multiple_of(block_ref[k] * columns, columns)
+        value = dot_nt(grad_query_ref[...], pack[:, :queries])
+        value += dot_nn(back_ref[...], latent_ref[:, pl.ds(start, columns)])
+        grad_normed_ref[:, pl.ds(start, columns)] = value.astype(BF16)
+        weight = dot_tn(back_ref[...], normed_ref[:, pl.ds(start, columns)])
+        turns = [
+            sum(weight[KVR + i * LANES + j * half : KVR + i * LANES + (j + 1) * half] for j in range(heads))
+            for i in range(2)
+        ]
+        chunk_refs[k][: KVR + ROPE] = jnp.concatenate([weight[:KVR]] + turns, axis=0).astype(BF16)
+    gains_ref[0:1, :] = jnp.sum(grad_normed_ref[...].astype(F32) * unit, axis=0, keepdims=True)
+    gains_ref[1:2, :] = ffn_gain_ref[...]
+    used = KVR + ROPE
+    for k in range(shards):
+        at = pl.ds(pl.multiple_of(block_ref[k] * columns, columns), columns)
+        chunk_refs[k][used : used + EXPERTS] = router_ref[:, at].astype(BF16)
+        rows = [gains_ref[:2, at]]
+        rows += [gains_ref[2:3, i * columns : (i + 1) * columns] for i in range(KVR // columns)]
+        filled = 2 + KVR // columns
+        rows.append(jnp.zeros((CHUNK_ROWS - used - EXPERTS - filled, columns), F32))
+        chunk_refs[k][used + EXPERTS :] = jnp.concatenate(rows, axis=0).astype(BF16)
+
+
+def attention_weights_kernel(heads, depth, block_ref, *refs):
+    grads, refs = refs[:depth], refs[depth:]
+    normed_ref, low_ref, attended_ref, query_ref, keyval_ref, *packs, stage_ref, whole_ref = refs
+    own = grads[0].shape[0]
+    shards, share = len(packs), packs[0].shape[0]
+    queries = heads * (NOPE + ROPE)
+    columns = normed_ref.shape[1] // shards
+    part = KVR // shards
+    count = share // part
+    keyval_columns = keyval_ref.shape[1] // count
+    output = queries + keyval_columns
+    for z, piece in enumerate(grads):
+        stage_ref[z * own : (z + 1) * own] = piece[...]
+    whole_ref[...] = dot_tn(low_ref[...], keyval_ref[...]).astype(BF16)
+    for k in range(shards):
+        start = pl.multiple_of(block_ref[k] * columns, columns)
+        packs[k][:, :queries] = dot_tn(
+            normed_ref[:, pl.ds(start, columns)], query_ref[...]
+        ).astype(BF16)
+        rows = pl.ds(pl.multiple_of(block_ref[k] * part, part), part)
+        for i in range(count):
+            packs[k][i * part : (i + 1) * part, queries:output] = whole_ref[
+                rows, i * keyval_columns : (i + 1) * keyval_columns
+            ]
+        value = dot_tn(attended_ref[...], stage_ref[:, pl.ds(start, columns)]).astype(BF16)
+        for i in range(heads * VD // share):
+            packs[k][:, output + i * columns : output + (i + 1) * columns] = value[
+                i * share : (i + 1) * share
+            ]
+
+
+def vmem_call(kernel, name, blocks, operands, out_shape, scratch):
+    if blocks is None:
+        return pl.pallas_call(
+            kernel,
+            out_shape=out_shape,
+            scratch_shapes=scratch,
+            compiler_params=params(),
+            name=name,
+        )(*operands)
+    return pl.pallas_call(
+        kernel,
+        grid_spec=pltpu.PrefetchScalarGridSpec(
+            num_scalar_prefetch=1,
+            grid=(1,),
+            in_specs=[whole(a.shape) for a in operands],
+            out_specs=[whole(a.shape) for a in out_shape],
+            scratch_shapes=scratch,
+        ),
+        out_shape=out_shape,
+        compiler_params=params("arbitrary"),
+        name=name,
+    )(blocks, *operands)
+
+
+def latent_rows(pieces, gain, weight, kv_gain, cosine, sine):
+    count = pieces[0].shape[0] * len(pieces)
+    width = pieces[0].shape[1]
+    return vmem_call(
+        functools.partial(latent_kernel, len(pieces)),
+        "latent_rows",
+        None,
+        [*pieces, gain[None], weight, kv_gain[None], cosine, sine],
+        [
             jax.ShapeDtypeStruct((count, width), BF16),
-            jax.ShapeDtypeStruct((EXPERTS, count), BF16),
-        ],
-        compiler_params=params(),
-        name="combine_back",
-    )(pick, slots, extra, gates, router, back, shared_in)
-
-
-def combine_out(place, local, pick, slots, hidden, shared_out):
-    count, width = pick.shape[1], slots.shape[2]
-    return pl.pallas_call(
-        functools.partial(combine_out_kernel, local),
-        grid=(1,),
-        in_specs=[
-            whole(pick.shape), strip(local, place, width), whole(hidden.shape),
-            whole(shared_out.shape),
-        ],
-        out_specs=whole((count, width)),
-        out_shape=jax.ShapeDtypeStruct((count, width), BF16),
-        compiler_params=params(),
-        name="combine_out",
-    )(pick, slots, hidden, shared_out)
-
-
-def expert_layer(rows, grads, routes, router, expert_in, expert_out, shared):
+            jax.ShapeDtypeStruct((count, KVR), F32),
+            jax.ShapeDtypeStruct((count, KVR), BF16),
+            jax.ShapeDtypeStruct((count, 2 * LANES), BF16),
+        ],
+        [],
+    )
+
+
+def attention_forward(heads, blocks, packs, normed, low, key, bias, cosine, sine):
+    count, width = normed.shape
+    queries = heads * (NOPE + ROPE)
+    keyval = heads * (NOPE + VD)
+    return vmem_call(
+        functools.partial(attention_kernel, heads),
+        "attention_forward",
+        blocks,
+        [*packs, normed, low, key, bias, cosine, sine],
+        [
+            jax.ShapeDtypeStruct((count, queries), BF16),
+            jax.ShapeDtypeStruct((count, keyval), BF16),
+            jax.ShapeDtypeStruct((heads, count, count), F32),
+            jax.ShapeDtypeStruct((count, heads * VD), BF16),
+            jax.ShapeDtypeStruct((count, width), BF16),
+        ],
+        [pltpu.VMEM((count, queries), F32), pltpu.VMEM((KVR, keyval), BF16)],
+    )
+
+
+def attention_backward(
+    heads, blocks, packs, tokens, grads, saved, latent, kv_gain, cosine, sine, router, ffn_gain
+):
+    query, keyval, key, soft, attended, compressed, low, normed = saved
+    count, width = normed.shape
+    shards = len(packs)
+    return vmem_call(
+        functools.partial(attention_back_kernel, heads, len(tokens)),
+        "attention_backward",
+        blocks,
+        [
+            *packs, *tokens, *grads, query, keyval, key, soft, attended, compressed, low, normed,
+            latent, kv_gain[None], cosine, sine, router, ffn_gain[None],
+        ],
+        [
+            jax.ShapeDtypeStruct(query.shape, BF16),
+            jax.ShapeDtypeStruct(keyval.shape, BF16),
+            jax.ShapeDtypeStruct((count, width), BF16),
+        ]
+        + [jax.ShapeDtypeStruct((CHUNK_ROWS, width // shards), BF16)] * shards,
+        [
+            pltpu.VMEM((8, width), F32),
+            pltpu.VMEM((count, heads * VD), BF16),
+            pltpu.VMEM((KVR, keyval.shape[1]), BF16),
+            pltpu.VMEM((count, latent.shape[0]), BF16),
+            pltpu.VMEM((count, width), BF16),
+        ],
+    )
+
+
+def attention_weights(heads, blocks, shape, grads, normed, low, attended, grad_query, grad_keyval):
+    count, width = normed.shape
+    shards = blocks.shape[0]
+    return vmem_call(
+        functools.partial(attention_weights_kernel, heads, len(grads)),
+        "attention_weights",
+        blocks,
+        [*grads, normed, low, attended, grad_query, grad_keyval],
+        [jax.ShapeDtypeStruct(shape, BF16)] * shards,
+        [pltpu.VMEM((count, width), BF16), pltpu.VMEM((KVR, grad_keyval.shape[1]), BF16)],
+    )
+
+
+def query_order(heads):
+    size, half = NOPE + ROPE, ROPE // 2
+    pieces = []
+    for start, stop in ((0, NOPE), (NOPE, NOPE + half), (NOPE + half, size)):
+        pieces += [(head * size + start, head * size + stop) for head in range(heads)]
+    return pieces
+
+
+def pack_weights(query, keyval, output, heads):
+    share, columns = query.shape[0], output.shape[1]
+    part = keyval.shape[0]
+    count = share // part
+    wide = keyval.shape[1] // count
+    return jnp.concatenate(
+        [query[:, start:stop] for start, stop in query_order(heads)]
+        + [
+            jnp.concatenate([keyval[:, i * wide : (i + 1) * wide] for i in range(count)], axis=0)
+        ]
+        + [output[i * share : (i + 1) * share] for i in range(output.shape[0] // share)],
+        axis=1,
+    )
+
+
+def unpack_weights(pack, keyval_shape, output_shape, heads):
+    size, half = NOPE + ROPE, ROPE // 2
+    queries = heads * size
+    share = pack.shape[0]
+    part = keyval_shape[0]
+    count = share // part
+    wide = keyval_shape[1] // count
+    nope = heads * NOPE
+    query = []
+    for head in range(heads):
+        query += [
+            pack[:, head * NOPE : (head + 1) * NOPE],
+            pack[:, nope + head * half : nope + (head + 1) * half],
+            pack[:, nope + (heads + head) * half : nope + (heads + head + 1) * half],
+        ]
+    keyval = jnp.concatenate(
+        [pack[i * part : (i + 1) * part, queries : queries + wide] for i in range(count)], axis=1
+    )
+    at, columns = queries + wide, output_shape[1]
+    output = jnp.concatenate(
+        [
+            pack[:, at + i * columns : at + (i + 1) * columns]
+            for i in range(output_shape[0] // share)
+        ],
+        axis=0,
+    )
+    return jnp.concatenate(query, axis=1), keyval, output
+
+
+def expert_layer(base, rows, grads, routes, router, expert_in, expert_out, shared):
     local, units, width = expert_out.shape
     sequences = len(rows)
+    pairs = range(sequences // 2)
     shared_units = shared.shape[0] // 3
-    shared_in, shared_out = shared[: 2 * shared_units], shared[2 * shared_units :]
-    order = list(range(sequences))
-    slot_grads, raws = None, [None] * sequences
-    for s in order:
-        slot_grads, raws[s] = dispatch_grads(
-            s, sequences, local, routes[s], grads[s], shared_out, slot_grads
+    side = jnp.concatenate([shared[: 2 * shared_units], router])
+    shared_out = shared[2 * shared_units :]
+    held = [None, None]
+    for m in pairs:
+        at = slice(2 * m, 2 * m + 2)
+        held = dispatch_grads(
+            m, sequences, local, base, routes[at], grads[at], shared_out, held
         )
-    slot_rows, infos = None, None
-    tables = [None] * sequences
-    for s in order:
-        slot_rows, infos, *tables[s] = dispatch_rows(
-            s, sequences, local, routes[s], rows[s], router, shared_in, raws[s], slot_rows, infos
+    slot_grads, shared_raw = held
+    raw = expert_raw(slot_grads, expert_out)
+    held = [None] * 6
+    for m in pairs:
+        at = slice(2 * m, 2 * m + 2)
+        held = dispatch_rows(
+            m, sequences, local, base, routes[at], rows[at], side, shared_raw, held
         )
-    out_rows, back_rows, extra, hidden, back = expert_rows(
-        slot_rows, slot_grads, infos, expert_in.reshape(local, 2 * units, width), expert_out
-    )
-    back_tokens, logits = [None] * sequences, [None] * sequences
-    for s in reversed(order):
-        pick, gates, _, shared_back = tables[s]
-        back_tokens[s], logits[s] = combine_back(
-            s, local, pick, back_rows, extra, gates, router, shared_back, shared_in
+    slot_rows, infos, picks, gates, shared_hidden, shared_back = held
+    back_rows, extra, hidden, back = expert_rows(
+        slot_rows, infos, expert_in.reshape(local, 2 * units, width), raw
+    )
+    back_tokens, logits = [], [None]
+    for m in pairs:
+        tokens, logits = combine_back(
+            m, picks, back_rows, extra, gates, shared_back, side, logits
         )
-    out_tokens = [None] * sequences
-    for s in reversed(order):
-        pick, _, shared_hidden, _ = tables[s]
-        out_tokens[s] = combine_out(s, local, pick, out_rows, shared_hidden, shared_out)
-    grad_in, grad_out = weight_grads(slot_rows, slot_grads, hidden, back)
+        back_tokens += tokens
+    out_rows = expert_out_rows(hidden, expert_out)
+    out_tokens = []
+    for m in pairs:
+        out_tokens += combine_out(m, picks, out_rows, shared_hidden, shared_out)
+    grad_in, grad_out = weight_grads(
+        0, local, slot_rows, slot_grads, hidden, back, [None, None]
+    )
     all_rows = jnp.stack(rows)
-    grad_router = contract("set,std->ed", jnp.stack(logits), all_rows)
+    grad_router = contract("set,std->ed", logits[0], all_rows)
     grad_shared = jnp.concatenate(
         [
-            contract("sft,std->fd", jnp.stack([table[3] for table in tables]), all_rows),
-            contract("sft,std->fd", jnp.stack([table[2] for table in tables]), jnp.stack(grads)),
+            contract("sft,std->fd", shared_back, all_rows),
+            contract("sft,std->fd", shared_hidden, jnp.stack(grads)),
         ]
     )
     return (
@@ -590,7 +1250,7 @@
     )
 
 
-def per_device(
+def general_device(
     tokens_in,
     out_grad,
     routes,
@@ -621,34 +1281,18 @@
     all_grads = grid.gather(jnp.concatenate(grid.gather_depth(out_grad)))
     routes_rel = jnp.concatenate(grid.relative_depth(routes.T, 1), axis=1)
     routes_all = [routes_rel] + [grid.fetch(routes_rel, offset) for offset in grid.offsets[1:]]
-    routes_all = [(part - base) % EXPERTS for part in routes_all]
     units = w_shared_out.shape[0] // grid.experts
     padding = ((0, -units % 32), (0, 0))
     padded_units = units + padding[0][1]
     shared_parts = [
-        jnp.concatenate([jnp.pad(part, padding) for part in (gate_rows, up_rows, out_rows)])
-        for gate_rows, up_rows, out_rows in zip(
+        jnp.concatenate([jnp.pad(part, padding) for part in parts])
+        for parts in zip(
             grid.relative(w_shared_in[0].T, 0),
             grid.relative(w_shared_in[1].T, 0),
             grid.relative(w_shared_out, 0),
         )
     ]
-    shared = grid.absolute(
-        [shared_parts[0]]
-        + [
-            grid.send(part, offset)
-            for offset, part in zip(
-                [(-dy, -dx, dc) for dy, dx, dc in grid.offsets[1:]],
-                [
-                    shared_parts[
-                        grid.offsets.index(((-dy) % grid.side, (-dx) % grid.side, dc))
-                    ]
-                    for dy, dx, dc in grid.offsets[1:]
-                ],
-            )
-        ],
-        1,
-    )
+    shared = grid.absolute(grid.exchange(shared_parts), 1)
     position = (
         (own_depth + jnp.arange(row_count) // own_rows) % depth * own_rows
         + jnp.arange(row_count) % own_rows
@@ -695,6 +1339,7 @@
         grad_router_rel,
         grad_shared,
     ) = expert_layer(
+        base.astype(jnp.int32)[None],
         all_rows,
         all_grads,
         routes_all,
@@ -764,13 +1409,7 @@
     grad_x_part, grad_attn_gain = rms_backward(stream_own, inverse_own, attn_gain, grad_normed_one)
     grad_in = grad_residual + grad_x_part
     grad_shared_parts = [part.astype(BF16) for part in grid.relative(grad_shared, 1)]
-    returned = [grad_shared_parts[0]] + [
-        grid.send(part, offset) for offset, part in zip(grid.offsets[1:], grad_shared_parts[1:])
-    ]
-    returned = [
-        returned[grid.offsets.index(((-dy) % grid.side, (-dx) % grid.side, dc))]
-        for dy, dx, dc in grid.offsets
-    ]
+    returned = grid.exchange(grad_shared_parts)
     sum_shared_in = jnp.stack(
         [
             grid.absolute([part[:units] for part in returned], 0).T,
@@ -812,6 +1451,250 @@
     )
 
 
+def after(array, *earlier):
+    return lax.optimization_barrier((array, *earlier))[0]
+
+
+def square_device(
+    tokens_in,
+    out_grad,
+    routes,
+    attn_gain,
+    kv_gain,
+    ffn_gain,
+    w_query,
+    w_latent,
+    w_keyval,
+    w_output,
+    w_router,
+    w_shared_in,
+    w_shared_out,
+    w_expert_in,
+    w_expert_out,
+):
+    grid = Grid()
+    depth = grid.depth
+    sequences = grid.experts
+    pairs = range(sequences // 2)
+    own_rows, width = tokens_in.shape
+    row_count = own_rows * depth
+    local = w_expert_in.shape[0]
+    hidden_units = w_expert_out.shape[1]
+    heads = w_query.shape[1] // (NOPE + ROPE)
+    own_depth = lax.axis_index("tensor")
+    blocks = jnp.stack([grid.place_of(offset) for offset in grid.offsets]).astype(jnp.int32)
+    depths = ((own_depth + jnp.arange(depth)) % depth).astype(jnp.int32)
+    base = (lax.axis_index("expert") * local).astype(jnp.int32)[None]
+
+    tokens = grid.gather_depth(tokens_in)
+    packs = grid.gather(pack_weights(w_query, w_keyval, w_output, heads))
+    position = (
+        (own_depth + jnp.arange(row_count) // own_rows) % depth * own_rows
+        + jnp.arange(row_count) % own_rows
+    )
+    cosine, sine = (jnp.tile(table, (1, heads)) for table in rope_tables(position))
+    bias = jnp.where(position[None, :] <= position[:, None], 0.0, -1e30).astype(F32)
+    half = ROPE // 2
+    latent_t = w_latent.T
+    latent_t = jnp.concatenate(
+        [latent_t[:KVR]] + [latent_t[KVR : KVR + half]] * heads + [latent_t[KVR + half :]] * heads
+    )
+    normed, compressed, low, key = latent_rows(tokens, attn_gain, latent_t, kv_gain, cosine, sine)
+
+    group_grads = jnp.concatenate(grid.gather_depth(after(out_grad, *tokens)))
+    all_grads = grid.gather(after(group_grads, *packs))
+    routes_t = after(routes, normed).T
+    routes_t = jnp.concatenate(grid.relative_depth(routes_t, 1), axis=1)
+    routes_all = grid.gather_small(routes_t)
+    units = w_shared_out.shape[0] // grid.experts
+    padding = ((0, -units % 32), (0, 0))
+    shared_in, shared_out = after(w_shared_in, normed), after(w_shared_out, normed)
+    shared_parts = [
+        jnp.concatenate([jnp.pad(part, padding) for part in parts])
+        for parts in zip(
+            grid.relative(shared_in[0].T, 0),
+            grid.relative(shared_in[1].T, 0),
+            grid.relative(shared_out, 0),
+        )
+    ]
+    pieces = grid.exchange(shared_parts)
+    router = jnp.roll(w_router.T, -base[0], axis=0)
+    padded_units = units + padding[0][1]
+    side, shared_out = vmem_call(
+        join_columns_kernel,
+        "join_columns",
+        blocks,
+        [*pieces, router],
+        [
+            jax.ShapeDtypeStruct((2 * padded_units + EXPERTS, width), BF16),
+            jax.ShapeDtypeStruct((padded_units, width), BF16),
+        ],
+        [],
+    )
+
+    query, keyval, soft, attended, part = attention_forward(
+        heads, blocks, packs, normed, low, key, bias, cosine, sine
+    )
+    stream = tokens_in.astype(F32)
+    residual = stream + grid.reduce_depth(split_rows(part, depth))
+    normed_two, inverse_two = rms_forward(residual, ffn_gain)
+    normed_two = normed_two.astype(BF16)
+
+    held = [None, None]
+    for m in pairs:
+        held = dispatch_grads(
+            m,
+            sequences,
+            local,
+            base,
+            routes_all[2 * m : 2 * m + 2],
+            all_grads[2 * m : 2 * m + 2],
+            shared_out,
+            held,
+        )
+    slot_grads, shared_raw = held
+    raw = expert_raw(slot_grads, w_expert_out)
+
+    rows = grid.gather(jnp.concatenate(grid.gather_depth(normed_two)))
+    held = [None] * 6
+    for m in pairs:
+        held = dispatch_rows(
+            m,
+            sequences,
+            local,
+            base,
+            routes_all[2 * m : 2 * m + 2],
+            rows[2 * m : 2 * m + 2],
+            side,
+            shared_raw,
+            held,
+        )
+    slot_rows, infos, picks, gates, shared_hidden, shared_back = held
+    expert_in = jnp.swapaxes(w_expert_in, 2, 3).reshape(local, 2 * hidden_units, width)
+    back_rows, extra, hidden, back = expert_rows(slot_rows, infos, expert_in, raw)
+    back_tokens, logits = [None] * sequences, [None]
+    for m in reversed(pairs):
+        back_tokens[2 * m : 2 * m + 2], logits = combine_back(
+            m, picks, back_rows, extra, gates, shared_back, side, logits
+        )
+    sums, first_mark, second_mark = grid.reduce_parts(back_tokens)
+    grad_group = sum(array.astype(F32) for array in sums).astype(BF16)
+    grad_normed = grid.reduce_depth(split_rows(grad_group, depth))
+
+    half_experts = local // 2
+    held = weight_grads(
+        0, half_experts, after(slot_rows, first_mark), slot_grads, hidden, back, [None, None]
+    )
+    grad_expert_in, grad_expert_out = weight_grads(
+        half_experts, local, after(slot_rows, second_mark), slot_grads, hidden, back, held
+    )
+    out_rows = expert_out_rows(after(hidden, second_mark), w_expert_out)
+    out_tokens = []
+    for m in pairs:
+        out_tokens += combine_out(
+            m, picks, after(out_rows, grad_group), shared_hidden, shared_out
+        )
+    *grad_parts, grad_router = side_grads(
+        blocks, base, rows, all_grads, after(logits[0], grad_group), shared_hidden, shared_back
+    )
+    out_sums, _, _ = grid.reduce_parts(out_tokens)
+    out_group = sum(array.astype(F32) for array in out_sums).astype(BF16)
+
+    grad_res_part, grad_ffn_gain = rms_backward(residual, inverse_two, ffn_gain, grad_normed)
+    grad_residual = out_grad.astype(F32) + grad_res_part
+    grads = grid.gather_depth(grad_residual.astype(BF16))
+
+    ffn_total = grid.reduce_depth(split_rows(after(out_group, *grads), depth))
+    block_out = (residual + ffn_total).astype(BF16)
+    returned = grid.exchange([after(part, grad_group) for part in grad_parts])
+    sum_shared_in, sum_shared_out = vmem_call(
+        functools.partial(join_rows_kernel, units),
+        "join_rows",
+        blocks,
+        returned,
+        [
+            jax.ShapeDtypeStruct((2, units * grid.experts, width // grid.experts), F32),
+            jax.ShapeDtypeStruct((units * grid.experts, width // grid.experts), F32),
+        ],
+        [],
+    )
+
+    grad_query, grad_keyval, grad_normed_one, *chunks = attention_backward(
+        heads,
+        blocks,
+        packs,
+        tokens,
+        grads,
+        (query, keyval, key, soft, attended, compressed, low, normed),
+        latent_t,
+        kv_gain,
+        cosine,
+        sine,
+        grad_router,
+        grad_ffn_gain,
+    )
+    grad_packs = attention_weights(
+        heads, blocks, packs[0].shape, grads, normed, low, attended, grad_query, grad_keyval
+    )
+    sums, _, _ = grid.reduce_parts(chunks)
+    size = CHUNK_ROWS // depth
+    columns = width // grid.experts
+    parts = vmem_call(
+        sum_split_kernel,
+        "sum_split",
+        depths,
+        sums,
+        [jax.ShapeDtypeStruct((size, columns), BF16)] * depth,
+        [],
+    )
+    parts = grid.gather_depth(grid.reduce_depth(parts).astype(BF16))
+    (chunk,) = vmem_call(
+        join_depth_kernel,
+        "join_depth",
+        depths,
+        parts,
+        [jax.ShapeDtypeStruct((CHUNK_ROWS, columns), BF16)],
+        [],
+    )
+    sum_latent, sum_router, sum_gains = vmem_call(
+        functools.partial(replicated_kernel, KVR + ROPE),
+        "replicated",
+        blocks,
+        grid.gather(chunk),
+        [
+            jax.ShapeDtypeStruct((KVR + ROPE, width), F32),
+            jax.ShapeDtypeStruct((EXPERTS, width), F32),
+            jax.ShapeDtypeStruct((16, width), F32),
+        ],
+        [],
+    )
+    sum_kv_gain = sum_gains[2 : 2 + KVR // columns, :columns].reshape(KVR)
+
+    grad_normed_one = grid.reduce_depth(split_rows(grad_normed_one, depth))
+    inverse_one = lax.rsqrt(jnp.mean(stream * stream, axis=-1, keepdims=True) + EPSILON)
+    grad_in = grad_residual + rms_backward(stream, inverse_one, attn_gain, grad_normed_one)[0]
+    sums, _, _ = grid.reduce_parts(grad_packs)
+    sum_query, sum_keyval, sum_output = unpack_weights(
+        sum(array.astype(F32) for array in sums), w_keyval.shape, w_output.shape, heads
+    )
+    return (
+        block_out,
+        grad_in,
+        sum_gains[0],
+        sum_kv_gain,
+        sum_gains[1],
+        sum_query,
+        sum_latent.T,
+        sum_keyval,
+        sum_output,
+        sum_router.T,
+        jnp.swapaxes(sum_shared_in, 1, 2),
+        sum_shared_out,
+        jnp.swapaxes(grad_expert_in.reshape(local, 2, hidden_units, width), 2, 3),
+        grad_expert_out,
+    )
+
+
 def solution(mesh):
     placed = (
         P(("expert", "tensor"), None),
@@ -830,8 +1713,9 @@
         P("expert", None, None, "tensor"),
         P("expert", "tensor", None),
     )
+    square = mesh.shape["expert"] == 8
     return jax.shard_map(
-        per_device,
+        square_device if square else general_device,
         mesh=mesh,
         in_specs=placed,
         out_specs=(

time: 791 us -> 690 us (0.87)
  Pallas kernels: 150 us -> 234 us
  local copies, waits for them, and re-layouts: 134 us -> 51.6 us
  matrix products: 35.4 us -> 0 us
  starting transfers between devices: 136 us -> 110 us
  other arithmetic: 51.4 us -> 26.9 us
  waiting for transfers between devices: 276 us -> 254 us
    pallas_call x26 -> x30, Pallas kernels: 117 us -> 203 us  [the longest x14 94.8 us: chain_call(): pl.pallas_call(kernel, grid_spec=pltpu.PrefetchScalarGridSpec(num_scalar_...]
    dot_general x24 -> x0, matrix products: 35.4 us -> none  [the longest x20 29.9 us: contract(): jnp.einsum(pattern, left_side, right_side, preferred_element_type=F32)]
    ppermute x61 -> x43, waiting for transfers between devices: 54 us -> 18.8 us  [fetch(): return lax.ppermute(array, 'expert', pairs)]
    ppermute x62 -> x46, waiting for transfers between devices: 124 us -> 151 us  [send(): return lax.ppermute(array, 'expert', pairs)]
    unnamed x354 -> x242, local copies, waits for them, and re-layouts: 43 us -> 19.5 us
    pallas_call x7 -> x0, local copies, waits for them, and re-layouts: 20.2 us -> none  [combine_back(): pl.pallas_call(functools.partial(combine_back_kernel, local), grid=(1,),...]
    dynamic_update_slice x44 -> x0, local copies, waits for them, and re-layouts: 20.1 us -> none  [the longest x41 20.1 us: absolute(): lax.dynamic_update_slice_in_dim(whole, piece, self.place_of(offset) * siz...]
    ppermute x61 -> x43, starting transfers between devices: 40.1 us -> 24.2 us  [fetch(): return lax.ppermute(array, 'expert', pairs)]
  transfers between devices with their start and end apart: 153 -> 119, of which waited for: 52 -> 43; matrix products, arithmetic and copies ran while one was open for 23% -> 9% of each run, Pallas kernels for 16% -> 27%
where the time goes in v2:
time: 690 us; the launch traced here: 680 us
  waiting for transfers between devices  254 us (37%)
  Pallas kernels  234 us (34%)
  starting transfers between devices  110 us (16%)
  local copies, waits for them, and re-layouts  51.6 us (7%)
  other arithmetic  26.9 us (4%)
    ppermute x46, waiting for transfers between devices, send(): return lax.ppermute(array, 'expert', pairs)  151 us
    pallas_call x14, Pallas kernels, chain_call(): pl.pallas_call(kernel, grid_spec=pltpu.PrefetchScalarGridSpec(num_scalar_...  94.8 us
    ppermute x15, waiting for transfers between devices, reduce_depth(): lax.ppermute(chunks[k], 'tensor', [(i, (i + k) % depth) for i in range(de...  64.9 us
    pallas_call x8, Pallas kernels, vmem_call(): pl.pallas_call(kernel, grid_spec=pltpu.PrefetchScalarGridSpec(num_scalar_...  46.9 us
    ppermute x46, starting transfers between devices, send(): return lax.ppermute(array, 'expert', pairs)  35.2 us
    pallas_call x1, Pallas kernels, expert_rows(): pl.pallas_call(functools.partial(expert_kernel, units), grid=(local, slot...  31.2 us
    ppermute x15, starting transfers between devices, reduce_depth(): lax.ppermute(chunks[k], 'tensor', [(i, (i + k) % depth) for i in range(de...  29.2 us
    ppermute x43, starting transfers between devices, fetch(): return lax.ppermute(array, 'expert', pairs)  24.2 us
  transfers between devices with their start and end apart: 119, of which 43 were waited for; matrix products, arithmetic and copies ran while one was open for 9% of the time, Pallas kernels for 27%

profile of v2, /device:TPU:0, one launch (start us, length us, event | category | flops | bytes accessed | tf_op | source)
XLA Modules:
  0.0 679.8 jit_solution(18431930512393047822)
XLA Ops:
  39.8 6.6 collective-permute-done.5
  52.3 9.1 %attention_forward.1 = (bf16[256,768]{1,0:T(8,128)(2,1)}, bf16[256,1024]{1,0:T(8,128)(2,1)}, f32[4,256,256]{2,1,0:T(8,128)}, bf16[256,512]{1,0:T(8,128)(2,1)}, bf16[256,2048]{1,0:T(8,128)(2,1)}) custom-call(s32[8]{0:T(128)} %stack.35.block_ref, bf16[256,1536]{1,0:T(8,128)(2,1)} %concatenate.104.refs_0_, bf16[256,1536]{1,0:T(8,128)(2,1)} %copy-done.18, ...), custom_call_target="tpu_custom_call" | custom-call | tf_op jit(solution)/shard_map/attention_forward/pallas_call | solution.py:1049
  67.4 6.3 collective-permute-done.12
  73.7 7.9 %collective-permute-done.14 = bf16[64,2048]{1,0:T(8,128)(2,1)S(1)} collective-permute-done((bf16[64,2048]{1,0:T(8,128)(2,1)S(1)}, bf16[64,2048]{1,0:T(8,128)(2,1)S(1)}, u32[]{:S(2)}, u32[]{:S(2)}) %collective-permute-start.14) | collective-permute-done | bytes 262176 | tf_op jit(solution)/shard_map/ppermute | solution.py:185
  83.2 9.8 %collective-permute-done.13 = bf16[64,2048]{1,0:T(8,128)(2,1)S(1)} collective-permute-done((bf16[64,2048]{1,0:T(8,128)(2,1)S(1)}, bf16[64,2048]{1,0:T(8,128)(2,1)S(1)}, u32[]{:S(2)}, u32[]{:S(2)}) %collective-permute-start.13) | collective-permute-done | bytes 262176 | tf_op jit(solution)/shard_map/ppermute | solution.py:185
  103.7 6.6 collective-permute-done.34
  125.2 44.7 %collective-permute-done.30.refs_4_ = bf16[288,256]{1,0:T(8,128)(2,1)S(1)} collective-permute-done((bf16[288,256]{1,0:T(8,128)(2,1)S(1)}, bf16[288,256]{1,0:T(8,128)(2,1)S(1)}, u32[]{:S(2)}, u32[]{:S(2)}) %collective-permute-start.30) | collective-permute-done | bytes 147488 | tf_op jit(solution)/shard_map/ppermute | solution.py:104
  184.1 19.2 %collective-permute-done.33.refs_7_ = bf16[288,256]{1,0:T(8,128)(2,1)} collective-permute-done((bf16[288,256]{1,0:T(8,128)(2,1)S(1)}, bf16[288,256]{1,0:T(8,128)(2,1)}, u32[]{:S(2)}, u32[]{:S(2)}) %collective-permute-start.33) | collective-permute-done | bytes 147488 | tf_op jit(solution)/shard_map/ppermute | solution.py:104
  236.4 11.5 %expert_raw.1.raw_ref = f32[8,352,256]{2,1,0:T(8,128)} custom-call(bf16[8,256,2048]{2,1,0:T(8,128)(2,1)} %get-tuple-element.180.grads_ref, bf16[8,352,2048]{2,1,0:T(8,128)(2,1)} %out_ref.3), custom_call_target="tpu_custom_call" | custom-call | tf_op jit(solution)/shard_map/expert_raw/pallas_call | solution.py:553
  272.6 31.2 %expert_rows.1 = (bf16[8,256,2048]{2,1,0:T(8,128)(2,1)}, bf16[8,256,128]{2,1,0:T(8,128)(2,1)}, bf16[8,352,256]{2,1,0:T(8,128)(2,1)}, bf16[8,704,256]{2,1,0:T(8,128)(2,1)}) custom-call(bf16[8,256,2048]{2,1,0:T(8,128)(2,1)} %get-tuple-element.263.rows_ref, bf16[8,256,128]{2,1,0:T(8,128)(2,1)} %get-tuple-element.179.info_ref, bf16[8,704,2048]{2,1,0:T(8,128)(2,1)} %bitcast.103, ...), custom_call_target="tpu_custom_call" | custom-call | tf_op jit(solution)/shard_map/expert_rows/pallas_call | solution.py:568
  334.4 9.6 %collective-permute-done.59 = bf16[128,2048]{1,0:T(8,128)(2,1)S(1)} collective-permute-done((bf16[128,2048]{1,0:T(8,128)(2,1)S(1)}, bf16[128,2048]{1,0:T(8,128)(2,1)S(1)}, u32[]{:S(2)}, u32[]{:S(2)}) %collective-permute-start.59) | collective-permute-done | bytes 524320 | tf_op jit(solution)/shard_map/ppermute | solution.py:104
  347.5 21.3 %collective-permute-done.60 = bf16[256,2048]{1,0:T(8,128)(2,1)S(1)} collective-permute-done((bf16[256,2048]{1,0:T(8,128)(2,1)S(1)}, bf16[256,2048]{1,0:T(8,128)(2,1)S(1)}, u32[]{:S(2)}, u32[]{:S(2)}) %collective-permute-start.60) | collective-permute-done | bytes 1048608 | tf_op jit(solution)/shard_map/ppermute | solution.py:104
  371.3 6.4 collective-permute-start.69
  381.3 6.4 collective-permute-done.69
  390.0 12.1 %collective-permute-done.70 = bf16[64,2048]{1,0:T(8,128)(2,1)S(1)} collective-permute-done((bf16[64,2048]{1,0:T(8,128)(2,1)S(1)}, bf16[64,2048]{1,0:T(8,128)(2,1)S(1)}, u32[]{:S(2)}, u32[]{:S(2)}) %collective-permute-start.70) | collective-permute-done | bytes 262176 | tf_op jit(solution)/shard_map/ppermute | solution.py:185
  407.2 11.7 %side_grads.1 = (bf16[288,256]{1,0:T(8,128)(2,1)}, bf16[288,256]{1,0:T(8,128)(2,1)}, bf16[288,256]{1,0:T(8,128)(2,1)}, bf16[288,256]{1,0:T(8,128)(2,1)}, bf16[28...) custom-call(s32[8]{0:T(128)} %stack.35.block_ref, ...), custom_call_target="tpu_custom_call" | custom-call | tf_op jit(solution)/shard_map/side_grads/pallas_call | solution.py:742
  426.4 14.3 %attention_backward.1 = (bf16[256,768]{1,0:T(8,128)(2,1)}, bf16[256,1024]{1,0:T(8,128)(2,1)}, bf16[256,2048]{1,0:T(8,128)(2,1)}, bf16[704,256]{1,0:T(8,128)(2,1)...) custom-call(s32[8]{0:T(128)} %stack.35.block_ref, ...), custom_call_target="tpu_custom_call" | custom-call | tf_op jit(solution)/shard_map/attention_backward/pallas_call | solution.py:1049
  449.7 15.1 %weight_grads.2 = (f32[8,704,2048]{2,1,0:T(8,128)}, f32[8,352,2048]{2,1,0:T(8,128)}) custom-call(bf16[8,256,2048]{2,1,0:T(8,128)(2,1)} %get-tuple-element.263.rows_ref, bf16[8,256,2048]{2,1,0:T(8,128)(2,1)} %get-tuple-element.180.grads_ref, bf16[8,352,256]{2,1,0:T(8,128)(2,1)} %get-tuple-element.192.hidden_ref, bf16[8,704,256]{2,1,0:T(8,128)(2,1)} %get-tuple-element.262.back_ref), custom_call_target="tpu_custom_call" | custom-call | tf_op jit(solution)/shard_map/weight_grads/pallas_call | solution.py:463
  464.9 12.7 %expert_out_rows.1.slots_ref = bf16[8,256,2048]{2,1,0:T(8,128)(2,1)} custom-call(bf16[8,352,256]{2,1,0:T(8,128)(2,1)} %get-tuple-element.192.hidden_ref, bf16[8,352,2048]{2,1,0:T(8,128)(2,1)} %out_ref.3), custom_call_target="tpu_custom_call" | custom-call | tf_op jit(solution)/shard_map/expert_out_rows/pallas_call | solution.py:598
  477.6 15.3 %weight_grads.3 = (f32[8,704,2048]{2,1,0:T(8,128)}, f32[8,352,2048]{2,1,0:T(8,128)}) custom-call(bf16[8,256,2048]{2,1,0:T(8,128)(2,1)} %get-tuple-element.263.rows_ref, bf16[8,256,2048]{2,1,0:T(8,128)(2,1)} %get-tuple-element.180.grads_ref, bf16[8,352,256]{2,1,0:T(8,128)(2,1)} %get-tuple-element.192.hidden_ref, ...), custom_call_target="tpu_custom_call", output_to_operand_aliasing={{0}: (4, {}), {1}: (5, {})} | custom-call | tf_op jit(solution)/shard_map/weight_grads/pallas_call | solution.py:463
  545.4 16.4 %collective-permute-done.85.x_ref = bf16[704,256]{1,0:T(8,128)(2,1)S(1)} collective-permute-done((bf16[704,256]{1,0:T(8,128)(2,1)S(1)}, bf16[704,256]{1,0:T(8,128)(2,1)S(1)}, u32[]{:S(2)}, u32[]{:S(2)}) %collective-permute-start.85) | collective-permute-done | bytes 360480 | tf_op jit(solution)/shard_map/ppermute | solution.py:104
  619.0 7.1 %collective-permute-done.108 = bf16[256,1536]{1,0:T(8,128)(2,1)S(1)} collective-permute-done((bf16[256,1536]{1,0:T(8,128)(2,1)}, bf16[256,1536]{1,0:T(8,128)(2,1)S(1)}, u32[]{:S(2)}, u32[]{:S(2)}) %collective-permute-start.108) | collective-permute-done | bytes 786464 | tf_op jit(solution)/shard_map/ppermute | solution.py:104
  631.2 18.2 %collective-permute-done.68 = bf16[256,2048]{1,0:T(8,128)(2,1)S(1)} collective-permute-done((bf16[256,2048]{1,0:T(8,128)(2,1)S(1)}, bf16[256,2048]{1,0:T(8,128)(2,1)S(1)}, u32[]{:S(2)}, u32[]{:S(2)}) %collective-permute-start.68) | collective-permute-done | bytes 1048608 | tf_op jit(solution)/shard_map/ppermute | solution.py:104
  665.5 11.9 %collective-permute-done.76 = bf16[64,2048]{1,0:T(8,128)(2,1)} collective-permute-done((bf16[64,2048]{1,0:T(8,128)(2,1)}, bf16[64,2048]{1,0:T(8,128)(2,1)}, u32[]{:S(2)}, u32[]{:S(2)}) %collective-permute-start.76) | collective-permute-done | bytes 262176 | tf_op jit(solution)/shard_map/ppermute | solution.py:185
  (608 shorter events, 345.1 us)
Async XLA Ops:
  48.6 51.6 %collective-permute-start.36 = (bf16[64,2048]{1,0:T(8,128)(2,1)S(1)}, bf16[64,2048]{1,0:T(8,128)(2,1)S(1)}, u32[]{:S(2)}, u32[]{:S(2)}) collective-permute-start(bf16[64,2048]{1,0:T(8,128)(2,1)S(1)} %copy-done.37), channel_id=1, source_target_pairs={{3,0},{0,1},{1,2},{2,3},{7,4},{4,5},{5,6},{6,7},{11,8},{8,9},{9,10... | collective-permute-start | bytes 786440 | tf_op jit(solution)/shard_map/ppermute | solution.py:177
  50.3 53.3 %collective-permute-start.35 = (bf16[64,2048]{1,0:T(8,128)(2,1)S(1)}, bf16[64,2048]{1,0:T(8,128)(2,1)S(1)}, u32[]{:S(2)}, u32[]{:S(2)}) collective-permute-start(bf16[64,2048]{1,0:T(8,128)(2,1)S(1)} %copy-done.37), channel_id=1, source_target_pairs={{2,0},{3,1},{0,2},{1,3},{6,4},{7,5},{4,6},{5,7},{10,8},{11,9},{8,1... | collective-permute-start | bytes 786440 | tf_op jit(solution)/shard_map/ppermute | solution.py:177
  119.3 51.3 %collective-permute-start.39 = (bf16[256,2048]{1,0:T(8,128)(2,1)S(1)}, bf16[256,2048]{1,0:T(8,128)(2,1)S(1)}, u32[]{:S(2)}, u32[]{:S(2)}) collective-permute-start(bf16[256,2048]{1,0:T(8,128)(2,1)S(1)} %pad_maximum_fusion.1.refs_2_.refs_8_), channel_id=1, source_target_pairs={{16,0},{20,4},{24,8},{28,12},{0,16},{4,20},{8,24},{12,28},{17,1},{... | collective-permute-start | bytes 3145736 | tf_op jit(solution)/shard_map/ppermute | solution.py:100
  120.8 49.9 %collective-permute-start.37 = (bf16[256,2048]{1,0:T(8,128)(2,1)S(1)}, bf16[256,2048]{1,0:T(8,128)(2,1)S(1)}, u32[]{:S(2)}, u32[]{:S(2)}) collective-permute-start(bf16[256,2048]{1,0:T(8,128)(2,1)S(1)} %pad_maximum_fusion.1.refs_2_.refs_8_), channel_id=1, source_target_pairs={{8,0},{12,4},{0,8},{4,12},{24,16},{28,20},{16,24},{20,28},{9,1},{1... | collective-permute-start | bytes 3145736 | tf_op jit(solution)/shard_map/ppermute | solution.py:100
  122.4 51.3 %collective-permute-start.23 = (bf16[256,2048]{1,0:T(8,128)(2,1)S(1)}, bf16[256,2048]{1,0:T(8,128)(2,1)S(1)}, u32[]{:S(2)}, u32[]{:S(2)}) collective-permute-start(bf16[256,2048]{1,0:T(8,128)(2,1)S(1)} %pad_maximum_fusion.refs_2_.refs_0_), channel_id=1, source_target_pairs={{16,0},{20,4},{24,8},{28,12},{0,16},{4,20},{8,24},{12,28},{17,1},{... | collective-permute-start | bytes 3145736 | tf_op jit(solution)/shard_map/ppermute | solution.py:100
  123.5 58.1 %collective-permute-start.21 = (bf16[256,2048]{1,0:T(8,128)(2,1)S(1)}, bf16[256,2048]{1,0:T(8,128)(2,1)}, u32[]{:S(2)}, u32[]{:S(2)}) collective-permute-start(bf16[256,2048]{1,0:T(8,128)(2,1)S(1)} %pad_maximum_fusion.refs_2_.refs_0_), channel_id=1, source_target_pairs={{8,0},{12,4},{0,8},{4,12},{24,16},{28,20},{16,24},{20,28},{9,1},{1... | collective-permute-start | bytes 3145736 | tf_op jit(solution)/shard_map/ppermute | solution.py:100
  124.1 45.9 %collective-permute-start.30 = (bf16[288,256]{1,0:T(8,128)(2,1)S(1)}, bf16[288,256]{1,0:T(8,128)(2,1)S(1)}, u32[]{:S(2)}, u32[]{:S(2)}) collective-permute-start(bf16[288,256]{1,0:T(8,128)(2,1)S(1)} %fusion.32), channel_id=1, source_target_pairs={{0,16},{4,20},{8,24},{12,28},{16,0},{20,4},{24,8},{28,12},{1,17},{... | collective-permute-start | bytes 442376 | tf_op jit(solution)/shard_map/ppermute | solution.py:104
  170.0 33.6 %collective-permute-start.49 = (bf16[256,2048]{1,0:T(8,128)(2,1)S(1)}, bf16[256,2048]{1,0:T(8,128)(2,1)}, u32[]{:S(2)}, u32[]{:S(2)}) collective-permute-start(bf16[256,2048]{1,0:T(8,128)(2,1)S(1)} %pad_maximum_fusion.1.refs_2_.refs_8_), channel_id=1, source_target_pairs={{4,0},{0,4},{12,8},{8,12},{20,16},{16,20},{28,24},{24,28},{5,1},{1... | collective-permute-start | bytes 3145736 | tf_op jit(solution)/shard_map/ppermute | solution.py:100
  173.7 32.2 %collective-permute-start.40 = (bf16[128,2048]{1,0:T(8,128)(2,1)}, bf16[128,2048]{1,0:T(8,128)(2,1)}, u32[]{:S(2)}, u32[]{:S(2)}) collective-permute-start(bf16[128,2048]{1,0:T(8,128)(2,1)} %slice.382), channel_id=1, source_target_pairs={{8,0},{12,4},{0,8},{4,12},{24,16},{28,20},{16,24},{20,28},{9,1},{1... | collective-permute-start | bytes 1572872 | tf_op jit(solution)/shard_map/ppermute | solution.py:100
  180.0 34.6 %collective-permute-start.38 = (bf16[128,2048]{1,0:T(8,128)(2,1)}, bf16[128,2048]{1,0:T(8,128)(2,1)}, u32[]{:S(2)}, u32[]{:S(2)}) collective-permute-start(bf16[128,2048]{1,0:T(8,128)(2,1)} %slice.381), channel_id=1, source_target_pairs={{16,0},{20,4},{24,8},{28,12},{0,16},{4,20},{8,24},{12,28},{17,1},{... | collective-permute-start | bytes 1572872 | tf_op jit(solution)/shard_map/ppermute | solution.py:100
  180.4 34.7 %collective-permute-start.24 = (bf16[128,2048]{1,0:T(8,128)(2,1)}, bf16[128,2048]{1,0:T(8,128)(2,1)}, u32[]{:S(2)}, u32[]{:S(2)}) collective-permute-start(bf16[128,2048]{1,0:T(8,128)(2,1)} %slice.380), channel_id=1, source_target_pairs={{8,0},{12,4},{0,8},{4,12},{24,16},{28,20},{16,24},{20,28},{9,1},{1... | collective-permute-start | bytes 1572872 | tf_op jit(solution)/shard_map/ppermute | solution.py:100
  218.8 42.6 %collective-permute-start.50 = (bf16[256,2048]{1,0:T(8,128)(2,1)S(1)}, bf16[256,2048]{1,0:T(8,128)(2,1)}, u32[]{:S(2)}, u32[]{:S(2)}) collective-permute-start(bf16[256,2048]{1,0:T(8,128)(2,1)S(1)} %copy-done.8), channel_id=1, source_target_pairs={{4,0},{0,4},{12,8},{8,12},{20,16},{16,20},{28,24},{24,28},{5,1},{1... | collective-permute-start | bytes 3145736 | tf_op jit(solution)/shard_map/ppermute | solution.py:100
  219.4 36.2 %collective-permute-start.51 = (bf16[256,2048]{1,0:T(8,128)(2,1)}, bf16[256,2048]{1,0:T(8,128)(2,1)}, u32[]{:S(2)}, u32[]{:S(2)}) collective-permute-start(bf16[256,2048]{1,0:T(8,128)(2,1)} %collective-permute-done.21.refs_2_), channel_id=1, source_target_pairs={{4,0},{0,4},{12,8},{8,12},{20,16},{16,20},{28,24},{24,28},{5,1},{1... | collective-permute-start | bytes 3145736 | tf_op jit(solution)/shard_map/ppermute | solution.py:100
  219.5 33.9 %collective-permute-start.25 = (bf16[128,2048]{1,0:T(8,128)(2,1)S(1)}, bf16[128,2048]{1,0:T(8,128)(2,1)}, u32[]{:S(2)}, u32[]{:S(2)}) collective-permute-start(bf16[128,2048]{1,0:T(8,128)(2,1)S(1)} %collective-permute-done.22), channel_id=1, source_target_pairs={{4,0},{0,4},{12,8},{8,12},{20,16},{16,20},{28,24},{24,28},{5,1},{1... | collective-permute-start | bytes 1572872 | tf_op jit(solution)/shard_map/ppermute | solution.py:100
  222.0 32.4 %collective-permute-start.26 = (bf16[128,2048]{1,0:T(8,128)(2,1)}, bf16[128,2048]{1,0:T(8,128)(2,1)}, u32[]{:S(2)}, u32[]{:S(2)}) collective-permute-start(bf16[128,2048]{1,0:T(8,128)(2,1)} %collective-permute-done.24), channel_id=1, source_target_pairs={{4,0},{0,4},{12,8},{8,12},{20,16},{16,20},{28,24},{24,28},{5,1},{1... | collective-permute-start | bytes 1572872 | tf_op jit(solution)/shard_map/ppermute | solution.py:100
  442.0 82.9 %collective-permute-start.78 = (bf16[64,2048]{1,0:T(8,128)(2,1)S(1)}, bf16[64,2048]{1,0:T(8,128)(2,1)S(1)}, u32[]{:S(2)}, u32[]{:S(2)}) collective-permute-start(bf16[64,2048]{1,0:T(8,128)(2,1)S(1)} %get-tuple-element.294), channel_id=1, source_target_pairs={{0,1},{1,2},{2,3},{3,0},{4,5},{5,6},{6,7},{7,4},{8,9},{9,10},{10,1... | collective-permute-start | bytes 786440 | tf_op jit(solution)/shard_map/ppermute | solution.py:185
  446.3 78.7 %collective-permute-start.80 = (bf16[64,2048]{1,0:T(8,128)(2,1)S(1)}, bf16[64,2048]{1,0:T(8,128)(2,1)S(1)}, u32[]{:S(2)}, u32[]{:S(2)}) collective-permute-start(bf16[64,2048]{1,0:T(8,128)(2,1)S(1)} %get-tuple-element.295), channel_id=1, source_target_pairs={{0,3},{1,0},{2,1},{3,2},{4,7},{5,4},{6,5},{7,6},{8,11},{9,8},{10,9... | collective-permute-start | bytes 786440 | tf_op jit(solution)/shard_map/ppermute | solution.py:185
  446.5 78.9 %collective-permute-start.79 = (bf16[64,2048]{1,0:T(8,128)(2,1)S(1)}, bf16[64,2048]{1,0:T(8,128)(2,1)S(1)}, u32[]{:S(2)}, u32[]{:S(2)}) collective-permute-start(bf16[64,2048]{1,0:T(8,128)(2,1)S(1)} %get-tuple-element.296), channel_id=1, source_target_pairs={{0,2},{1,3},{2,0},{3,1},{4,6},{5,7},{6,4},{7,5},{8,10},{9,11},{10,... | collective-permute-start | bytes 786440 | tf_op jit(solution)/shard_map/ppermute | solution.py:185
  448.1 65.6 %collective-permute-start.113 = (bf16[288,256]{1,0:T(8,128)(2,1)S(1)}, bf16[288,256]{1,0:T(8,128)(2,1)S(1)}, u32[]{:S(2)}, u32[]{:S(2)}) collective-permute-start(bf16[288,256]{1,0:T(8,128)(2,1)S(1)} %copy-done.113), channel_id=1, source_target_pairs={{0,8},{4,12},{8,0},{12,4},{16,24},{20,28},{24,16},{28,20},{1,9},{5... | collective-permute-start | bytes 442376 | tf_op jit(solution)/shard_map/ppermute | solution.py:104
  449.1 65.2 %collective-permute-start.112 = (bf16[288,256]{1,0:T(8,128)(2,1)S(1)}, bf16[288,256]{1,0:T(8,128)(2,1)S(1)}, u32[]{:S(2)}, u32[]{:S(2)}) collective-permute-start(bf16[288,256]{1,0:T(8,128)(2,1)S(1)} %copy-done.112), channel_id=1, source_target_pairs={{0,4},{4,0},{8,12},{12,8},{16,20},{20,16},{24,28},{28,24},{1,5},{5... | collective-permute-start | bytes 442376 | tf_op jit(solution)/shard_map/ppermute | solution.py:104
  540.3 39.7 %collective-permute-start.64 = (bf16[128,2048]{1,0:T(8,128)(2,1)S(1)}, bf16[128,2048]{1,0:T(8,128)(2,1)S(1)}, u32[]{:S(2)}, u32[]{:S(2)}) collective-permute-start(bf16[128,2048]{1,0:T(8,128)(2,1)S(1)} %get-tuple-element.303), channel_id=1, source_target_pairs={{0,16},{4,20},{8,24},{12,28},{16,0},{20,4},{24,8},{28,12},{1,17},{... | collective-permute-start | bytes 1572872 | tf_op jit(solution)/shard_map/ppermute | solution.py:104
  541.4 35.1 %collective-permute-start.67 = (bf16[128,2048]{1,0:T(8,128)(2,1)S(1)}, bf16[128,2048]{1,0:T(8,128)(2,1)S(1)}, u32[]{:S(2)}, u32[]{:S(2)}) collective-permute-start(bf16[128,2048]{1,0:T(8,128)(2,1)S(1)} %get-tuple-element.304), channel_id=1, source_target_pairs={{0,8},{4,12},{8,0},{12,4},{16,24},{20,28},{24,16},{28,20},{1,9},{5... | collective-permute-start | bytes 1572872 | tf_op jit(solution)/shard_map/ppermute | solution.py:104
  609.3 40.1 %collective-permute-start.68 = (bf16[256,2048]{1,0:T(8,128)(2,1)S(1)}, bf16[256,2048]{1,0:T(8,128)(2,1)S(1)}, u32[]{:S(2)}, u32[]{:S(2)}) collective-permute-start(bf16[256,2048]{1,0:T(8,128)(2,1)S(1)} %pad_maximum_fusion.5), channel_id=1, source_target_pairs={{0,16},{4,20},{8,24},{12,28},{16,0},{20,4},{24,8},{28,12},{1,17},{... | collective-permute-start | bytes 3145736 | tf_op jit(solution)/shard_map/ppermute | solution.py:104
  618.5 30.9 %collective-permute-start.65 = (bf16[256,2048]{1,0:T(8,128)(2,1)S(1)}, bf16[256,2048]{1,0:T(8,128)(2,1)S(1)}, u32[]{:S(2)}, u32[]{:S(2)}) collective-permute-start(bf16[256,2048]{1,0:T(8,128)(2,1)S(1)} %pad_maximum_fusion.4), channel_id=1, source_target_pairs={{0,8},{4,12},{8,0},{12,4},{16,24},{20,28},{24,16},{28,20},{1,9},{5... | collective-permute-start | bytes 3145736 | tf_op jit(solution)/shard_map/ppermute | solution.py:104
  (212 other events, 3031.2 us)

commit v3 on v2

--- a/solution.py
+++ b/solution.py
@@ -169,7 +169,38 @@
         to_x = jnp.concatenate([own[2][:half], low_add(own[2][half:], second)])
         from_x = self.send(to_x, (0, 1, 0))
         from_y = self.send(to_y, (1, 0, 0))
-        return [own[0], from_x, from_y], own[6], to_x
+        return [own[0], from_x, from_y], own[6], (to_x, to_y)
+
+    def ring(self, array, step):
+        depth = self.depth
+        return lax.ppermute(array, "tensor", [(i, (i + step) % depth) for i in range(depth)])
+
+    def ring_near(self, shard):
+        return self.ring(shard, -1), self.ring(shard, 1)
+
+    def ring_far(self, ahead, behind):
+        half = ahead.shape[0] // 2
+        return self.ring(ahead[:half], -1), self.ring(behind[half:], 1)
+
+    def ring_gather(self, shard):
+        ahead, behind = self.ring_near(shard)
+        return [shard, ahead, *self.ring_far(ahead, behind), behind]
+
+    def ring_start(self, chunks):
+        half = chunks[2].shape[0] // 2
+        first = self.ring(chunks[2][:half], 1)
+        second = self.ring(chunks[2][half:], -1)
+        return first, second
+
+    def ring_finish(self, chunks, first, second):
+        half = chunks[2].shape[0] // 2
+        to_ahead = jnp.concatenate([low_add(chunks[1][:half], first), chunks[1][half:]])
+        to_behind = jnp.concatenate([chunks[3][:half], low_add(chunks[3][half:], second)])
+        return self.ring(to_ahead, 1), self.ring(to_behind, -1), (to_ahead, to_behind)
+
+    def ring_reduce(self, chunks):
+        ahead, behind, _ = self.ring_finish(chunks, *self.ring_start(chunks))
+        return chunks[0].astype(F32) + ahead.astype(F32) + behind.astype(F32)
 
     def gather_depth(self, shard):
         depth = self.depth
@@ -294,15 +325,18 @@
     return jnp.concatenate(parts, axis=0), chosen
 
 
-def dispatch_grads_kernel(local, base_ref, *refs):
-    routes, grads, shared_ref = refs[:2], refs[2:4], refs[4]
-    slot_ref, raw_ref = refs[-2:]
-    for i in range(2):
-
-        @pl.when(pl.program_id(0) == i)
+def dispatch_grads_kernel(local, base_ref, routes_ref, *refs):
+    shared_ref, slot_ref, raw_ref = refs[-3:]
+    pieces = refs[:-3]
+    half = len(pieces) // 2
+    for core in range(2):
+
+        @pl.when(pl.program_id(0) % 2 == core)
         def _():
-            pick, _ = pick_rows(routes[i][...], base_ref[0], local)
-            values = grads[i][...]
+            pick, _ = pick_rows(routes_ref[0], base_ref[0], local)
+            values = jnp.concatenate(
+                [piece[...] for piece in pieces[core * half : (core + 1) * half]], axis=0
+            )
             slot_ref[...] = (
                 dot_nn(pick.astype(BF16), values).astype(BF16).reshape(slot_ref.shape)
             )
@@ -391,7 +425,8 @@
 
 
 def weight_grad_kernel(rows_ref, grads_ref, hidden_ref, back_ref, *rest):
-    in_ref, out_ref = rest[-2:]
+    in_ref, out_ref, mark_ref = rest[-3:]
+    mark_ref[...] = jnp.zeros_like(mark_ref)
 
     @pl.when(pl.program_id(1) == 0)
     def _():
@@ -476,27 +511,31 @@
     )(*prefetch, *operands, *chained)
 
 
-def dispatch_grads(pair, sequences, local, base, routes, grads, shared_out, held):
-    count, width = grads[0].shape
+def dispatch_grads(local, base, routes, grads, shared_out):
+    sequences, top, count = routes.shape
+    width = grads[0].shape[1]
+    part = count * 2 // len(grads)
     units = shared_out.shape[0]
-    operands = [*routes, *grads, shared_out]
-    return chain_call(
+    return pl.pallas_call(
         functools.partial(dispatch_grads_kernel, local),
-        "dispatch_grads",
-        (2,),
-        [base],
-        operands,
-        [whole(a.shape) for a in operands],
-        held,
-        [
-            pl.BlockSpec((local, SLOTS, width), lambda i, *_: (0, 2 * pair + i, 0)),
-            pl.BlockSpec((1, units, count), lambda i, *_: (2 * pair + i, 0, 0)),
-        ],
-        [
+        grid_spec=pltpu.PrefetchScalarGridSpec(
+            num_scalar_prefetch=1,
+            grid=(sequences,),
+            in_specs=[pl.BlockSpec((1, top, count), lambda s, *_: (s, 0, 0))]
+            + [pl.BlockSpec((part, width), lambda s, *_: (s // 2, 0))] * len(grads)
+            + [whole(shared_out.shape)],
+            out_specs=[
+                pl.BlockSpec((local, SLOTS, width), lambda s, *_: (0, s, 0)),
+                pl.BlockSpec((1, units, count), lambda s, *_: (s, 0, 0)),
+            ],
+        ),
+        out_shape=[
             jax.ShapeDtypeStruct((local, sequences * SLOTS, width), BF16),
             jax.ShapeDtypeStruct((sequences, units, count), F32),
         ],
-    )
+        compiler_params=params("arbitrary"),
+        name="dispatch_grads",
+    )(base, routes, *grads, shared_out)
 
 
 def dispatch_rows(pair, sequences, local, base, routes, rows, side, raws, held):
@@ -632,10 +671,11 @@
             )
         ],
         held,
-        [moved(one(2 * units, width)), moved(one(units, width))],
+        [moved(one(2 * units, width)), moved(one(units, width)), whole((8, LANES))],
         [
             jax.ShapeDtypeStruct((local, 2 * units, width), F32),
             jax.ShapeDtypeStruct((local, units, width), F32),
+            jax.ShapeDtypeStruct((8, LANES), F32),
         ],
     )
 
@@ -706,13 +746,19 @@
 
 def side_grads_kernel(sequences, block_ref, *refs):
     rows, grads, rest = refs[:sequences], refs[sequences : 2 * sequences], refs[2 * sequences :]
+    half = len(grads) // 2
+    part = rows[0].shape[0] // half
     logits_ref, hidden_ref, back_ref, first_ref, *parts, router_ref, left_ref, in_ref, out_ref = rest
     units = hidden_ref.shape[1]
     for s in range(sequences):
         left_ref[: 2 * units] = back_ref[s]
         left_ref[2 * units :] = logits_ref[s]
         value = dot_nn(left_ref[...], rows[s][...])
-        other = dot_nn(hidden_ref[s], grads[s][...])
+        held = grads[s % 2 * half : (s % 2 + 1) * half]
+        other = dot_nn(
+            hidden_ref[s],
+            jnp.concatenate([piece[s // 2 * part : (s // 2 + 1) * part] for piece in held], axis=0),
+        )
         if s == 0:
             in_ref[...] = value
             out_ref[...] = other
@@ -917,15 +963,13 @@
         gains_ref, grad_attended_ref, weight_ref, back_ref, stage_ref,
     ) = refs
     share = packs[0].shape[0]
-    own = tokens[0].shape[0]
     nope = heads * NOPE
     queries = heads * (NOPE + ROPE)
     keyval_columns = keyval_ref.shape[1] * (KVR // shards) // share
     output = queries + keyval_columns
     columns = normed_ref.shape[1] // shards
     scale = (NOPE + ROPE) ** (-0.5)
-    for z, piece in enumerate(grads):
-        stage_ref[z * own : (z + 1) * own] = piece[...]
+    stage_ref[...] = jnp.concatenate([piece[...] for piece in grads], axis=0)
     blocks = heads * VD // share
     for i in range(blocks):
         value = None
@@ -1009,7 +1053,6 @@
 def attention_weights_kernel(heads, depth, block_ref, *refs):
     grads, refs = refs[:depth], refs[depth:]
     normed_ref, low_ref, attended_ref, query_ref, keyval_ref, *packs, stage_ref, whole_ref = refs
-    own = grads[0].shape[0]
     shards, share = len(packs), packs[0].shape[0]
     queries = heads * (NOPE + ROPE)
     columns = normed_ref.shape[1] // shards
@@ -1017,8 +1060,7 @@
     count = share // part
     keyval_columns = keyval_ref.shape[1] // count
     output = queries + keyval_columns
-    for z, piece in enumerate(grads):
-        stage_ref[z * own : (z + 1) * own] = piece[...]
+    stage_ref[...] = jnp.concatenate([piece[...] for piece in grads], axis=0)
     whole_ref[...] = dot_tn(low_ref[...], keyval_ref[...]).astype(BF16)
     for k in range(shards):
         start = pl.multiple_of(block_ref[k] * columns, columns)
@@ -1062,7 +1104,7 @@
 
 
 def latent_rows(pieces, gain, weight, kv_gain, cosine, sine):
-    count = pieces[0].shape[0] * len(pieces)
+    count = sum(piece.shape[0] for piece in pieces)
     width = pieces[0].shape[1]
     return vmem_call(
         functools.partial(latent_kernel, len(pieces)),
@@ -1201,13 +1243,8 @@
     shared_units = shared.shape[0] // 3
     side = jnp.concatenate([shared[: 2 * shared_units], router])
     shared_out = shared[2 * shared_units :]
-    held = [None, None]
-    for m in pairs:
-        at = slice(2 * m, 2 * m + 2)
-        held = dispatch_grads(
-            m, sequences, local, base, routes[at], grads[at], shared_out, held
-        )
-    slot_grads, shared_raw = held
+    by_core = [jnp.concatenate(grads[core::2]) for core in range(2)]
+    slot_grads, shared_raw = dispatch_grads(local, base, jnp.stack(routes), by_core, shared_out)
     raw = expert_raw(slot_grads, expert_out)
     held = [None] * 6
     for m in pairs:
@@ -1229,7 +1266,7 @@
     out_tokens = []
     for m in pairs:
         out_tokens += combine_out(m, picks, out_rows, shared_hidden, shared_out)
-    grad_in, grad_out = weight_grads(
+    grad_in, grad_out, _ = weight_grads(
         0, local, slot_rows, slot_grads, hidden, back, [None, None]
     )
     all_rows = jnp.stack(rows)
@@ -1486,8 +1523,23 @@
     depths = ((own_depth + jnp.arange(depth)) % depth).astype(jnp.int32)
     base = (lax.axis_index("expert") * local).astype(jnp.int32)[None]
 
-    tokens = grid.gather_depth(tokens_in)
-    packs = grid.gather(pack_weights(w_query, w_keyval, w_output, heads))
+    tokens = grid.ring_gather(tokens_in)
+    quarter = own_rows // 2
+    along_x = grid.fetch(out_grad, (0, 1, 0))
+    along_y = grid.fetch(out_grad, (1, 0, 0))
+    crossed = [
+        grid.fetch(along_x[:quarter], (1, 0, 0)),
+        grid.fetch(along_y[quarter:], (0, 1, 0)),
+    ]
+    plane = jnp.concatenate([out_grad, along_x, along_y, *crossed])
+    packs = grid.gather(
+        after(pack_weights(w_query, w_keyval, w_output, heads), *crossed, tokens[1], tokens[4])
+    )
+    planes = grid.ring_near(after(plane, *tokens))
+    far = jnp.concatenate(grid.ring_far(*planes))
+    routes_t = jnp.concatenate(grid.relative_depth(routes.T, 1), axis=1)
+    routes_all = grid.gather_small(routes_t)
+
     position = (
         (own_depth + jnp.arange(row_count) // own_rows) % depth * own_rows
         + jnp.arange(row_count) % own_rows
@@ -1499,25 +1551,21 @@
     latent_t = jnp.concatenate(
         [latent_t[:KVR]] + [latent_t[KVR : KVR + half]] * heads + [latent_t[KVR + half :]] * heads
     )
-    normed, compressed, low, key = latent_rows(tokens, attn_gain, latent_t, kv_gain, cosine, sine)
-
-    group_grads = jnp.concatenate(grid.gather_depth(after(out_grad, *tokens)))
-    all_grads = grid.gather(after(group_grads, *packs))
-    routes_t = after(routes, normed).T
-    routes_t = jnp.concatenate(grid.relative_depth(routes_t, 1), axis=1)
-    routes_all = grid.gather_small(routes_t)
+    normed, compressed, low, key = latent_rows(
+        tokens, attn_gain, latent_t, kv_gain, cosine, sine
+    )
+
     units = w_shared_out.shape[0] // grid.experts
     padding = ((0, -units % 32), (0, 0))
-    shared_in, shared_out = after(w_shared_in, normed), after(w_shared_out, normed)
     shared_parts = [
         jnp.concatenate([jnp.pad(part, padding) for part in parts])
         for parts in zip(
-            grid.relative(shared_in[0].T, 0),
-            grid.relative(shared_in[1].T, 0),
-            grid.relative(shared_out, 0),
+            grid.relative(w_shared_in[0].T, 0),
+            grid.relative(w_shared_in[1].T, 0),
+            grid.relative(w_shared_out, 0),
         )
     ]
-    pieces = grid.exchange(shared_parts)
+    pieces = grid.exchange([after(part, packs[2], packs[4]) for part in shared_parts])
     router = jnp.roll(w_router.T, -base[0], axis=0)
     padded_units = units + padding[0][1]
     side, shared_out = vmem_call(
@@ -1533,29 +1581,39 @@
     )
 
     query, keyval, soft, attended, part = attention_forward(
-        heads, blocks, packs, normed, low, key, bias, cosine, sine
-    )
+        heads, blocks, packs, after(normed, far), low, key, bias, cosine, sine
+    )
+    core_grads = [plane, planes[0], far, planes[1]]
+    all_grads = core_grads + [grid.fetch(piece, (0, 0, 1)) for piece in core_grads]
     stream = tokens_in.astype(F32)
-    residual = stream + grid.reduce_depth(split_rows(part, depth))
+    residual = stream + grid.ring_reduce(split_rows(part, depth))
     normed_two, inverse_two = rms_forward(residual, ffn_gain)
     normed_two = normed_two.astype(BF16)
 
-    held = [None, None]
-    for m in pairs:
-        held = dispatch_grads(
-            m,
-            sequences,
-            local,
-            base,
-            routes_all[2 * m : 2 * m + 2],
-            all_grads[2 * m : 2 * m + 2],
-            shared_out,
-            held,
-        )
-    slot_grads, shared_raw = held
-    raw = expert_raw(slot_grads, w_expert_out)
-
-    rows = grid.gather(jnp.concatenate(grid.gather_depth(normed_two)))
+    near_rows = grid.ring_near(after(normed_two, *routes_all))
+    far_rows = grid.ring_far(*near_rows)
+    group_rows = jnp.concatenate([normed_two, near_rows[0], *far_rows, near_rows[1]])
+    group_rows = after(group_rows, *pieces)
+    middle = row_count // 2
+    along_x = grid.fetch(group_rows, (0, 1, 0))
+    along_y = grid.fetch(group_rows, (1, 0, 0))
+    pair_rows = grid.fetch(group_rows, (0, 0, 1))
+    slot_grads, shared_raw = dispatch_grads(
+        local, base, jnp.stack(routes_all), all_grads, after(shared_out, group_rows)
+    )
+    along_x, along_y = after(along_x, slot_grads), after(along_y, slot_grads)
+    first = grid.fetch(along_x[:middle], (1, 0, 0))
+    second = grid.fetch(along_y[middle:], (0, 1, 0))
+    raw = expert_raw(after(slot_grads, along_x, along_y), w_expert_out)
+    first, second = after(first, raw), after(second, raw)
+    rows = [group_rows, pair_rows]
+    for held in (along_x, along_y):
+        rows += [held, grid.fetch(held, (0, 0, 1))]
+    rows += [
+        jnp.concatenate([first, second]),
+        jnp.concatenate([grid.fetch(first, (0, 0, 1)), grid.fetch(second, (0, 0, 1))]),
+    ]
+
     held = [None] * 6
     for m in pairs:
         held = dispatch_rows(
@@ -1572,53 +1630,69 @@
     slot_rows, infos, picks, gates, shared_hidden, shared_back = held
     expert_in = jnp.swapaxes(w_expert_in, 2, 3).reshape(local, 2 * hidden_units, width)
     back_rows, extra, hidden, back = expert_rows(slot_rows, infos, expert_in, raw)
-    back_tokens, logits = [None] * sequences, [None]
-    for m in reversed(pairs):
-        back_tokens[2 * m : 2 * m + 2], logits = combine_back(
-            m, picks, back_rows, extra, gates, shared_back, side, logits
+
+    def backs(m, logits, *earlier):
+        return combine_back(
+            m, picks, after(back_rows, *earlier), extra, gates, shared_back, side, logits
         )
-    sums, first_mark, second_mark = grid.reduce_parts(back_tokens)
-    grad_group = sum(array.astype(F32) for array in sums).astype(BF16)
-    grad_normed = grid.reduce_depth(split_rows(grad_group, depth))
-
-    half_experts = local // 2
-    held = weight_grads(
-        0, half_experts, after(slot_rows, first_mark), slot_grads, hidden, back, [None, None]
-    )
-    grad_expert_in, grad_expert_out = weight_grads(
-        half_experts, local, after(slot_rows, second_mark), slot_grads, hidden, back, held
-    )
-    out_rows = expert_out_rows(after(hidden, second_mark), w_expert_out)
-    out_tokens = []
-    for m in pairs:
-        out_tokens += combine_out(
-            m, picks, after(out_rows, grad_group), shared_hidden, shared_out
-        )
-    *grad_parts, grad_router = side_grads(
-        blocks, base, rows, all_grads, after(logits[0], grad_group), shared_hidden, shared_back
-    )
-    out_sums, _, _ = grid.reduce_parts(out_tokens)
-    out_group = sum(array.astype(F32) for array in out_sums).astype(BF16)
+
+    front, rear = slice(None, row_count // 2), slice(row_count // 2, None)
+    (near_6, far_6), logits = backs(3, [None])
+    (near_4, far_4), logits = backs(2, logits, near_6)
+    own_6 = low_add(near_6, grid.send(far_6, (0, 0, 1)))
+    first = grid.send(own_6[front], (0, 1, 0))
+    second = grid.send(own_6[rear], (1, 0, 0))
+    (near_2, far_2), logits = backs(1, logits, own_6)
+    own_4 = low_add(near_4, grid.send(far_4, (0, 0, 1)))
+    (near_0, far_0), logits = backs(0, logits, own_4)
+    own_2 = low_add(near_2, grid.send(far_2, (0, 0, 1)))
+    first, second = after(first, near_0), after(second, near_0)
+    to_y = jnp.concatenate([low_add(own_4[front], first), own_4[rear]])
+    to_x = jnp.concatenate([own_2[front], low_add(own_2[rear], second)])
+    from_x = grid.send(to_x, (0, 1, 0))
+    from_y = grid.send(to_y, (1, 0, 0))
+
+    def outs(m, *earlier):
+        return combine_out(m, picks, after(out_rows, *earlier), shared_hidden, shared_out)
+
+    out_rows = expert_out_rows(after(hidden, to_x, to_y), w_expert_out)
+    own_0 = low_add(near_0, grid.send(far_0, (0, 0, 1)))
+    out_6, out_7 = outs(3)
+    out_4, out_5 = outs(2, out_6)
+    from_x, from_y = after(from_x, out_4), after(from_y, out_4)
+    grad_group = (own_0.astype(F32) + from_x.astype(F32) + from_y.astype(F32)).astype(BF16)
+    chunks = split_rows(grad_group, depth)
+    first, second = grid.ring_start(chunks)
+    out_own_6 = low_add(after(out_6, grad_group), grid.send(after(out_7, grad_group), (0, 0, 1)))
+    out_own_4 = low_add(out_4, grid.send(after(out_5, grad_group), (0, 0, 1)))
+    out_first = grid.send(out_own_6[front], (0, 1, 0))
+    out_second = grid.send(out_own_6[rear], (1, 0, 0))
+    out_2, out_3 = outs(1, grad_group)
+    first, second = after(first, out_2), after(second, out_2)
+    ahead, behind, marks = grid.ring_finish(chunks, first, second)
+    out_0, out_1 = outs(0, *marks)
+    ahead, behind = after(ahead, out_0), after(behind, out_0)
+    grad_normed = chunks[0].astype(F32) + ahead.astype(F32) + behind.astype(F32)
 
     grad_res_part, grad_ffn_gain = rms_backward(residual, inverse_two, ffn_gain, grad_normed)
     grad_residual = out_grad.astype(F32) + grad_res_part
-    grads = grid.gather_depth(grad_residual.astype(BF16))
-
-    ffn_total = grid.reduce_depth(split_rows(after(out_group, *grads), depth))
-    block_out = (residual + ffn_total).astype(BF16)
-    returned = grid.exchange([after(part, grad_group) for part in grad_parts])
-    sum_shared_in, sum_shared_out = vmem_call(
-        functools.partial(join_rows_kernel, units),
-        "join_rows",
-        blocks,
-        returned,
-        [
-            jax.ShapeDtypeStruct((2, units * grid.experts, width // grid.experts), F32),
-            jax.ShapeDtypeStruct((units * grid.experts, width // grid.experts), F32),
-        ],
-        [],
-    )
-
+    grad_low = grad_residual.astype(BF16)
+    near_grads = grid.ring_near(grad_low)
+    out_own_2 = low_add(out_2, grid.send(out_3, (0, 0, 1)))
+    out_own_0 = low_add(out_0, grid.send(out_1, (0, 0, 1)))
+    out_to_y = jnp.concatenate([low_add(out_own_4[front], out_first), out_own_4[rear]])
+    out_to_x = jnp.concatenate([out_own_2[front], low_add(out_own_2[rear], out_second)])
+    out_from_x = grid.send(out_to_x, (0, 1, 0))
+    out_from_y = grid.send(out_to_y, (1, 0, 0))
+    *grad_parts, grad_router = side_grads(
+        blocks, base, rows, all_grads, after(logits[0], grad_low, out_to_x, out_to_y), shared_hidden, shared_back
+    )
+    out_from_x, out_from_y = after(out_from_x, grad_router), after(out_from_y, grad_router)
+    far_grads = grid.ring_far(*near_grads)
+    grads = [grad_low, near_grads[0], *(after(piece, grad_router) for piece in far_grads), near_grads[1]]
+
+    returned = grid.exchange(grad_parts)
+    grads[0] = after(grads[0], out_from_x, out_from_y)
     grad_query, grad_keyval, grad_normed_one, *chunks = attention_backward(
         heads,
         blocks,
@@ -1633,21 +1707,70 @@
         grad_router,
         grad_ffn_gain,
     )
+    out_group = (
+        out_own_0.astype(F32)
+        + out_from_x.astype(F32)
+        + out_from_y.astype(F32)
+    ).astype(BF16)
     grad_packs = attention_weights(
-        heads, blocks, packs[0].shape, grads, normed, low, attended, grad_query, grad_keyval
-    )
-    sums, _, _ = grid.reduce_parts(chunks)
+        heads,
+        blocks,
+        packs[0].shape,
+        grads,
+        normed,
+        low,
+        attended,
+        after(grad_query, *returned),
+        grad_keyval,
+    )
+    ffn_total = grid.ring_reduce(split_rows(after(out_group, grad_query), depth))
+    block_out = (residual + ffn_total).astype(BF16)
+    sums, chunk_first, chunk_mark = grid.reduce_parts(chunks)
+    share = local // 4
+    held = [None, None]
+
+    def weights(step, held, *earlier):
+        return weight_grads(
+            step * share,
+            (step + 1) * share,
+            after(slot_rows, *earlier),
+            slot_grads,
+            hidden,
+            back,
+            held[:2],
+        )
+
+    held = weights(0, held, grad_packs[0], chunk_first)
+    held = weights(1, held, held[2], *chunk_mark)
+    mark = held[2]
     size = CHUNK_ROWS // depth
     columns = width // grid.experts
     parts = vmem_call(
         sum_split_kernel,
         "sum_split",
         depths,
-        sums,
+        [sums[0], after(sums[1], mark), after(sums[2], mark)],
         [jax.ShapeDtypeStruct((size, columns), BF16)] * depth,
         [],
     )
-    parts = grid.gather_depth(grid.reduce_depth(parts).astype(BF16))
+    pack_sums, pack_first, pack_mark = grid.reduce_parts([after(pack, mark) for pack in grad_packs])
+    held = weights(2, held, parts[0], pack_first)
+    part = grid.reduce_depth([parts[0]] + [after(part, pack_first) for part in parts[1:]])
+    part = after(part, held[2]).astype(BF16)
+    *held, mark = weights(3, held, part, *pack_mark)
+    grad_expert_in, grad_expert_out = held
+    parts = [after(piece, mark) for piece in grid.gather_depth(part)]
+    sum_shared_in, sum_shared_out = vmem_call(
+        functools.partial(join_rows_kernel, units),
+        "join_rows",
+        blocks,
+        [after(returned[0], mark), *returned[1:]],
+        [
+            jax.ShapeDtypeStruct((2, units * grid.experts, width // grid.experts), F32),
+            jax.ShapeDtypeStruct((units * grid.experts, width // grid.experts), F32),
+        ],
+        [],
+    )
     (chunk,) = vmem_call(
         join_depth_kernel,
         "join_depth",
@@ -1670,12 +1793,11 @@
     )
     sum_kv_gain = sum_gains[2 : 2 + KVR // columns, :columns].reshape(KVR)
 
-    grad_normed_one = grid.reduce_depth(split_rows(grad_normed_one, depth))
+    grad_normed_one = grid.ring_reduce(split_rows(grad_normed_one, depth))
     inverse_one = lax.rsqrt(jnp.mean(stream * stream, axis=-1, keepdims=True) + EPSILON)
     grad_in = grad_residual + rms_backward(stream, inverse_one, attn_gain, grad_normed_one)[0]
-    sums, _, _ = grid.reduce_parts(grad_packs)
     sum_query, sum_keyval, sum_output = unpack_weights(
-        sum(array.astype(F32) for array in sums), w_keyval.shape, w_output.shape, heads
+        sum(array.astype(F32) for array in pack_sums), w_keyval.shape, w_output.shape, heads
     )
     return (
         block_out,
@@ -1713,7 +1835,7 @@
         P("expert", None, None, "tensor"),
         P("expert", "tensor", None),
     )
-    square = mesh.shape["expert"] == 8
+    square = mesh.shape["expert"] == 8 and mesh.shape["tensor"] == 4
     return jax.shard_map(
         square_device if square else general_device,
         mesh=mesh,

time: 690 us -> 609 us (0.88)
  waiting for transfers between devices: 254 us -> 148 us
  starting transfers between devices: 110 us -> 120 us
  local copies, waits for them, and re-layouts: 51.6 us -> 59.9 us
    ppermute x46, waiting for transfers between devices: 151 us -> 41.9 us  [send(): return lax.ppermute(array, 'expert', pairs)]
    ppermute x0 -> x32, waiting for transfers between devices: none -> 79.2 us  [ring(): lax.ppermute(array, 'tensor', [(i, (i + step) % depth) for i in range(dep...]
    ppermute x15 -> x3, waiting for transfers between devices: 64.9 us -> 0.01 us  [reduce_depth(): lax.ppermute(chunks[k], 'tensor', [(i, (i + k) % depth) for i in range(de...]
    ppermute x0 -> x32, starting transfers between devices: none -> 53.3 us  [ring(): lax.ppermute(array, 'tensor', [(i, (i + step) % depth) for i in range(dep...]
    ppermute x15 -> x3, starting transfers between devices: 29.2 us -> 4.92 us  [reduce_depth(): lax.ppermute(chunks[k], 'tensor', [(i, (i + k) % depth) for i in range(de...]
    ppermute x15 -> x3, waiting for transfers between devices: 18.8 us -> 0.01 us  [gather_depth(): lax.ppermute(shard, 'tensor', [((i + k) % depth, i) for i in range(depth)])]
    ppermute x15 -> x3, starting transfers between devices: 21.7 us -> 3.1 us  [gather_depth(): lax.ppermute(shard, 'tensor', [((i + k) % depth, i) for i in range(depth)])]
    pallas_call x14 -> x12, Pallas kernels: 94.8 us -> 80.9 us  [chain_call(): pl.pallas_call(kernel, grid_spec=pltpu.PrefetchScalarGridSpec(num_scalar_...]
  transfers between devices with their start and end apart: 119 -> 126, of which waited for: 43 -> 37; matrix products, arithmetic and copies ran while one was open for 9% -> 13% of each run, Pallas kernels for 27% -> 31%
where the time goes in v3:
time: 609 us; the launch traced here: 598 us
  Pallas kernels  235 us (39%)
  waiting for transfers between devices  148 us (24%)
  starting transfers between devices  120 us (20%)
  local copies, waits for them, and re-layouts  59.9 us (10%)
  other arithmetic  32.8 us (5%)
    pallas_call x12, Pallas kernels, chain_call(): pl.pallas_call(kernel, grid_spec=pltpu.PrefetchScalarGridSpec(num_scalar_...  80.9 us
    ppermute x32, waiting for transfers between devices, ring(): lax.ppermute(array, 'tensor', [(i, (i + step) % depth) for i in range(dep...  79.2 us
    ppermute x32, starting transfers between devices, ring(): lax.ppermute(array, 'tensor', [(i, (i + step) % depth) for i in range(dep...  53.3 us
    pallas_call x8, Pallas kernels, vmem_call(): pl.pallas_call(kernel, grid_spec=pltpu.PrefetchScalarGridSpec(num_scalar_...  47.1 us
    ppermute x46, waiting for transfers between devices, send(): return lax.ppermute(array, 'expert', pairs)  41.9 us
    pallas_call x1, Pallas kernels, expert_rows(): pl.pallas_call(functools.partial(expert_kernel, units), grid=(local, slot...  31.6 us
    unnamed x260, local copies, waits for them, and re-layouts  29.7 us
    ppermute x46, starting transfers between devices, send(): return lax.ppermute(array, 'expert', pairs)  29.7 us
  transfers between devices with their start and end apart: 126, of which 37 were waited for; matrix products, arithmetic and copies ran while one was open for 13% of the time, Pallas kernels for 31%

profile of v3, /device:TPU:0, one launch (start us, length us, event | category | flops | bytes accessed | tf_op | source)
XLA Modules:
  0.0 598.4 jit_solution(13174383219519220122)
XLA Ops:
  50.9 7.8 %collective-permute-done.7.refs_2_ = bf16[256,1536]{1,0:T(8,128)(2,1)S(1)} collective-permute-done((bf16[256,1536]{1,0:T(8,128)(2,1)}, bf16[256,1536]{1,0:T(8,128)(2,1)S(1)}, u32[]{:S(2)}, u32[]{:S(2)}) %collective-permute-start.7) | collective-permute-done | bytes 786464 | tf_op jit(solution)/shard_map/ppermute | solution.py:100
  70.2 19.9 %collective-permute-done.17.refs_1_.refs_9_ = bf16[256,2048]{1,0:T(8,128)(2,1)} collective-permute-done((bf16[256,2048]{1,0:T(8,128)(2,1)}, bf16[256,2048]{1,0:T(8,128)(2,1)}, u32[]{:S(2)}, u32[]{:S(2)}) %collective-permute-start.17) | collective-permute-done | bytes 1048608 | tf_op jit(solution)/shard_map/ppermute | solution.py:176
  106.8 9.8 %collective-permute-done.20 = bf16[128,2048]{1,0:T(8,128)(2,1)S(1)} collective-permute-done((bf16[128,2048]{1,0:T(8,128)(2,1)S(1)}, bf16[128,2048]{1,0:T(8,128)(2,1)S(1)}, u32[]{:S(2)}, u32[]{:S(2)}) %collective-permute-start.20) | collective-permute-done | bytes 524320 | tf_op jit(solution)/shard_map/ppermute | solution.py:176
  120.4 9.2 %attention_forward.1 = (bf16[256,768]{1,0:T(8,128)(2,1)}, bf16[256,1024]{1,0:T(8,128)(2,1)}, f32[4,256,256]{2,1,0:T(8,128)}, bf16[256,512]{1,0:T(8,128)(2,1)}, bf16[256,2048]{1,0:T(8,128)(2,1)}) custom-call(s32[8]{0:T(128)} %stack.62.block_ref, bf16[256,1536]{1,0:T(8,128)(2,1)} %concatenate.125.refs_0_, bf16[256,1536]{1,0:T(8,128)(2,1)} %copy-done.18, ...), custom_call_target="tpu_custom_call" | custom-call | tf_op jit(solution)/shard_map/attention_forward/pallas_call | solution.py:1091
  149.9 6.0 collective-permute-done.22
  209.0 13.9 %dispatch_grads.1 = (bf16[8,256,2048]{2,1,0:T(8,128)(2,1)}, f32[8,96,256]{2,1,0:T(8,128)}) custom-call(s32[1]{0:T(128)} %bitcast.13.base_ref.refs_19_, s32[8,6,256]{2,1,0:T(8,128)} %constant_dynamic-update-slice_fusion.16.routes_ref, bf16[256,2048]{1,0:T(8,128)(2,1)} %constant_dynamic-update-slice_fusion.4.refs_0_.refs_8_, ...), custom_call_target="tpu_custom_call" | custom-call | tf_op jit(solution)/shard_map/dispatch_grads/pallas_call | solution.py:519
  228.1 11.5 %expert_raw.1.raw_ref = f32[8,352,256]{2,1,0:T(8,128)} custom-call(bf16[8,256,2048]{2,1,0:T(8,128)(2,1)} %get-tuple-element.211.grads_ref, bf16[8,352,2048]{2,1,0:T(8,128)(2,1)} %out_ref.3), custom_call_target="tpu_custom_call" | custom-call | tf_op jit(solution)/shard_map/expert_raw/pallas_call | solution.py:592
  265.5 31.6 %expert_rows.1 = (bf16[8,256,2048]{2,1,0:T(8,128)(2,1)}, bf16[8,256,128]{2,1,0:T(8,128)(2,1)}, bf16[8,352,256]{2,1,0:T(8,128)(2,1)}, bf16[8,704,256]{2,1,0:T(8,128)(2,1)}) custom-call(bf16[8,256,2048]{2,1,0:T(8,128)(2,1)} %get-tuple-element.343.rows_ref, bf16[8,256,128]{2,1,0:T(8,128)(2,1)} %get-tuple-element.236.info_ref, bf16[8,704,2048]{2,1,0:T(8,128)(2,1)} %bitcast.119, ...), custom_call_target="tpu_custom_call" | custom-call | tf_op jit(solution)/shard_map/expert_rows/pallas_call | solution.py:607
  297.1 6.1 %combine_back.4 = (bf16[8,64,256]{2,1,0:T(8,128)(2,1)}, bf16[256,2048]{1,0:T(8,128)(2,1)}, bf16[256,2048]{1,0:T(8,128)(2,1)}) custom-call(bf16[8,256,256]{2,1,0:T(8,128)(2,1)} %get-tuple-element.234.refs_0_.pick_ref, bf16[8,256,2048]{2,1,0:T(8,128)(2,1)} %get-tuple-element.244.refs_1_, bf16[8,256,128]{2,1,0:T(8,128)(2,1)} %get-tuple-element.239.refs_2_, ...), custom_call_target="tpu_custom_call" | custom-call | tf_op jit(solution)/shard_map/combine_back/pallas_call | solution.py:498
  303.6 6.1 %combine_back.5 = (bf16[8,64,256]{2,1,0:T(8,128)(2,1)}, bf16[256,2048]{1,0:T(8,128)(2,1)}, bf16[256,2048]{1,0:T(8,128)(2,1)}) custom-call(bf16[8,256,256]{2,1,0:T(8,128)(2,1)} %get-tuple-element.234.refs_0_.pick_ref, bf16[8,256,2048]{2,1,0:T(8,128)(2,1)} %get-tuple-element.244.refs_1_, ...), custom_call_target="tpu_custom_call", output_to_operand_aliasing={{0}: (6, {})} | custom-call | tf_op jit(solution)/shard_map/combine_back/pallas_call | solution.py:498
  312.0 6.1 %combine_back.6 = (bf16[8,64,256]{2,1,0:T(8,128)(2,1)}, bf16[256,2048]{1,0:T(8,128)(2,1)}, bf16[256,2048]{1,0:T(8,128)(2,1)}) custom-call(bf16[8,256,256]{2,1,0:T(8,128)(2,1)} %get-tuple-element.234.refs_0_.pick_ref, bf16[8,256,2048]{2,1,0:T(8,128)(2,1)} %get-tuple-element.244.refs_1_, ...), custom_call_target="tpu_custom_call", output_to_operand_aliasing={{0}: (6, {})} | custom-call | tf_op jit(solution)/shard_map/combine_back/pallas_call | solution.py:498
  318.6 6.1 %combine_back.7 = (bf16[8,64,256]{2,1,0:T(8,128)(2,1)}, bf16[256,2048]{1,0:T(8,128)(2,1)}, bf16[256,2048]{1,0:T(8,128)(2,1)}) custom-call(bf16[8,256,256]{2,1,0:T(8,128)(2,1)} %get-tuple-element.234.refs_0_.pick_ref, bf16[8,256,2048]{2,1,0:T(8,128)(2,1)} %get-tuple-element.244.refs_1_, ...), custom_call_target="tpu_custom_call", output_to_operand_aliasing={{0}: (6, {})} | custom-call | tf_op jit(solution)/shard_map/combine_back/pallas_call | solution.py:498
  328.2 12.7 %expert_out_rows.1.slots_ref = bf16[8,256,2048]{2,1,0:T(8,128)(2,1)} custom-call(bf16[8,352,256]{2,1,0:T(8,128)(2,1)} %get-tuple-element.257.hidden_ref, bf16[8,352,2048]{2,1,0:T(8,128)(2,1)} %out_ref.3), custom_call_target="tpu_custom_call" | custom-call | tf_op jit(solution)/shard_map/expert_out_rows/pallas_call | solution.py:637
  382.2 10.6 %collective-permute-done.74 = bf16[128,2048]{1,0:T(8,128)(2,1)S(1)} collective-permute-done((bf16[128,2048]{1,0:T(8,128)(2,1)S(1)}, bf16[128,2048]{1,0:T(8,128)(2,1)S(1)}, u32[]{:S(2)}, u32[]{:S(2)}) %collective-permute-start.74) | collective-permute-done | bytes 524320 | tf_op jit(solution)/shard_map/ppermute | solution.py:104
  399.9 7.2 %collective-permute-done.78.refs_17_.refs_4_ = bf16[64,2048]{1,0:T(8,128)(2,1)S(1)} collective-permute-done((bf16[64,2048]{1,0:T(8,128)(2,1)S(1)}, bf16[64,2048]{1,0:T(8,128)(2,1)S(1)}, u32[]{:S(2)}, u32[]{:S(2)}) %collective-permute-start.78) | collective-permute-done | bytes 262176 | tf_op jit(solution)/shard_map/ppermute | solution.py:176
  413.2 11.9 %side_grads.1 = (bf16[288,256]{1,0:T(8,128)(2,1)}, bf16[288,256]{1,0:T(8,128)(2,1)}, bf16[288,256]{1,0:T(8,128)(2,1)}, bf16[288,256]{1,0:T(8,128)(2,1)}, bf16[28...) custom-call(s32[8]{0:T(128)} %stack.62.block_ref, ...), custom_call_target="tpu_custom_call" | custom-call | tf_op jit(solution)/shard_map/side_grads/pallas_call | solution.py:788
  429.6 14.4 %attention_backward.1 = (bf16[256,768]{1,0:T(8,128)(2,1)}, bf16[256,1024]{1,0:T(8,128)(2,1)}, bf16[256,2048]{1,0:T(8,128)(2,1)}, bf16[704,256]{1,0:T(8,128)(2,1)...) custom-call(s32[8]{0:T(128)} %stack.62.block_ref, ...), custom_call_target="tpu_custom_call" | custom-call | tf_op jit(solution)/shard_map/attention_backward/pallas_call | solution.py:1091
  455.7 6.4 %attention_weights.1 = (bf16[256,1536]{1,0:T(8,128)(2,1)}, bf16[256,1536]{1,0:T(8,128)(2,1)}, bf16[256,1536]{1,0:T(8,128)(2,1)}, bf16[256,1536]{1,0:T(8,128)(2,1...) custom-call(s32[8]{0:T(128)} %stack.62.block_ref, ...), custom_call_target="tpu_custom_call" | custom-call | tf_op jit(solution)/shard_map/attention_weights/pallas_call | solution.py:1091
  476.8 8.7 %weight_grads.4 = (f32[8,704,2048]{2,1,0:T(8,128)}, f32[8,352,2048]{2,1,0:T(8,128)}, f32[8,128]{1,0:T(8,128)}) custom-call(bf16[8,256,2048]{2,1,0:T(8,128)(2,1)} %get-tuple-element.343.rows_ref, bf16[8,256,2048]{2,1,0:T(8,128)(2,1)} %get-tuple-element.211.grads_ref, bf16[8,352,256]{2,1,0:T(8,128)(2,1)} %get-tuple-element.257.hidden_ref, ...), custom_call_target="tpu_custom_call" | custom-call | tf_op jit(solution)/shard_map/weight_grads/pallas_call | solution.py:498
  485.7 8.7 %weight_grads.5 = (f32[8,704,2048]{2,1,0:T(8,128)}, f32[8,352,2048]{2,1,0:T(8,128)}, f32[8,128]{1,0:T(8,128)}) custom-call(bf16[8,256,2048]{2,1,0:T(8,128)(2,1)} %get-tuple-element.343.rows_ref, bf16[8,256,2048]{2,1,0:T(8,128)(2,1)} %get-tuple-element.211.grads_ref, ...), custom_call_target="tpu_custom_call", output_to_operand_aliasing={{0}: (4, {}), {1}: (5, {})} | custom-call | tf_op jit(solution)/shard_map/weight_grads/pallas_call | solution.py:498
  517.3 8.8 %weight_grads.6 = (f32[8,704,2048]{2,1,0:T(8,128)}, f32[8,352,2048]{2,1,0:T(8,128)}, f32[8,128]{1,0:T(8,128)}) custom-call(bf16[8,256,2048]{2,1,0:T(8,128)(2,1)} %get-tuple-element.343.rows_ref, bf16[8,256,2048]{2,1,0:T(8,128)(2,1)} %get-tuple-element.211.grads_ref, ...), custom_call_target="tpu_custom_call", output_to_operand_aliasing={{0}: (4, {}), {1}: (5, {})} | custom-call | tf_op jit(solution)/shard_map/weight_grads/pallas_call | solution.py:498
  538.6 8.7 %weight_grads.7 = (f32[8,704,2048]{2,1,0:T(8,128)}, f32[8,352,2048]{2,1,0:T(8,128)}, f32[8,128]{1,0:T(8,128)}) custom-call(bf16[8,256,2048]{2,1,0:T(8,128)(2,1)} %get-tuple-element.343.rows_ref, bf16[8,256,2048]{2,1,0:T(8,128)(2,1)} %get-tuple-element.211.grads_ref, ...), custom_call_target="tpu_custom_call", output_to_operand_aliasing={{0}: (4, {}), {1}: (5, {})} | custom-call | tf_op jit(solution)/shard_map/weight_grads/pallas_call | solution.py:498
  553.6 6.3 %collective-permute-done.117.refs_4_ = bf16[704,256]{1,0:T(8,128)(2,1)S(1)} collective-permute-done((bf16[704,256]{1,0:T(8,128)(2,1)}, bf16[704,256]{1,0:T(8,128)(2,1)S(1)}, u32[]{:S(2)}, u32[]{:S(2)}) %collective-permute-start.117) | collective-permute-done | bytes 360480 | tf_op jit(solution)/shard_map/ppermute | solution.py:100
  585.9 7.4 %collective-permute-done.124 = bf16[256,1536]{1,0:T(8,128)(2,1)S(1)} collective-permute-done((bf16[256,1536]{1,0:T(8,128)(2,1)S(1)}, bf16[256,1536]{1,0:T(8,128)(2,1)S(1)}, u32[]{:S(2)}, u32[]{:S(2)}) %collective-permute-start.124) | collective-permute-done | bytes 786464 | tf_op jit(solution)/shard_map/ppermute | solution.py:104
  (656 shorter events, 349.2 us)
Async XLA Ops:
  0.7 29.4 %collective-permute-start.2 = (bf16[64,2048]{1,0:T(8,128)(2,1)}, bf16[64,2048]{1,0:T(8,128)(2,1)}, u32[]{:S(2)}, u32[]{:S(2)}) collective-permute-start(bf16[64,2048]{1,0:T(8,128)(2,1)} %param.16), channel_id=1, source_target_pairs={{16,0},{20,4},{24,8},{28,12},{0,16},{4,20},{8,24},{12,28},{17,1},{... | collective-permute-start | bytes 786440 | tf_op jit(solution)/shard_map/ppermute | solution.py:100
  3.7 27.9 %collective-permute-start = (bf16[64,2048]{1,0:T(8,128)(2,1)}, bf16[64,2048]{1,0:T(8,128)(2,1)}, u32[]{:S(2)}, u32[]{:S(2)}) collective-permute-start(bf16[64,2048]{1,0:T(8,128)(2,1)} %param.16), channel_id=1, source_target_pairs={{8,0},{12,4},{0,8},{4,12},{24,16},{28,20},{16,24},{20,28},{9,1},{1... | collective-permute-start | bytes 786440 | tf_op jit(solution)/shard_map/ppermute | solution.py:100
  5.2 27.7 %collective-permute-start.5 = (bf16[64,2048]{1,0:T(8,128)(2,1)}, bf16[64,2048]{1,0:T(8,128)(2,1)S(1)}, u32[]{:S(2)}, u32[]{:S(2)}) collective-permute-start(bf16[64,2048]{1,0:T(8,128)(2,1)} %refs_8_.1), channel_id=1, source_target_pairs={{0,1},{1,2},{2,3},{3,0},{4,5},{5,6},{6,7},{7,4},{8,9},{9,10},{10,1... | collective-permute-start | bytes 786440 | tf_op jit(solution)/shard_map/ppermute | solution.py:176
  6.8 26.2 %collective-permute-start.4 = (bf16[64,2048]{1,0:T(8,128)(2,1)}, bf16[64,2048]{1,0:T(8,128)(2,1)}, u32[]{:S(2)}, u32[]{:S(2)}) collective-permute-start(bf16[64,2048]{1,0:T(8,128)(2,1)} %refs_8_.1), channel_id=1, source_target_pairs={{0,3},{1,0},{2,1},{3,2},{4,7},{5,4},{6,5},{7,6},{8,11},{9,8},{10,9... | collective-permute-start | bytes 786440 | tf_op jit(solution)/shard_map/ppermute | solution.py:176
  44.2 45.9 %collective-permute-start.17 = (bf16[256,2048]{1,0:T(8,128)(2,1)}, bf16[256,2048]{1,0:T(8,128)(2,1)}, u32[]{:S(2)}, u32[]{:S(2)}) collective-permute-start(bf16[256,2048]{1,0:T(8,128)(2,1)} %constant_dynamic-update-slice_fusion.4.refs_0_.refs_8_), channel_id=1, source_target_pairs={{0,3},{1,0},{2,1},{3,2},{4,7},{5,4},{6,5},{7,6},{8,11},{9,8},{10,9... | collective-permute-start | bytes 3145736 | tf_op jit(solution)/shard_map/ppermute | solution.py:176
  45.4 53.8 %collective-permute-start.19 = (bf16[256,2048]{1,0:T(8,128)(2,1)}, bf16[256,2048]{1,0:T(8,128)(2,1)}, u32[]{:S(2)}, u32[]{:S(2)}) collective-permute-start(bf16[256,2048]{1,0:T(8,128)(2,1)} %constant_dynamic-update-slice_fusion.4.refs_0_.refs_8_), channel_id=1, source_target_pairs={{0,1},{1,2},{2,3},{3,0},{4,5},{5,6},{6,7},{7,4},{8,9},{9,10},{10,1... | collective-permute-start | bytes 3145736 | tf_op jit(solution)/shard_map/ppermute | solution.py:176
  60.3 40.6 %collective-permute-start.11 = (bf16[128,1536]{1,0:T(8,128)(2,1)}, bf16[128,1536]{1,0:T(8,128)(2,1)}, u32[]{:S(2)}, u32[]{:S(2)}) collective-permute-start(bf16[128,1536]{1,0:T(8,128)(2,1)} %slice.491), channel_id=1, source_target_pairs={{16,0},{20,4},{24,8},{28,12},{0,16},{4,20},{8,24},{12,28},{17,1},{... | collective-permute-start | bytes 1179656 | tf_op jit(solution)/shard_map/ppermute | solution.py:100
  70.1 33.9 %collective-permute-start.12 = (bf16[128,1536]{1,0:T(8,128)(2,1)}, bf16[128,1536]{1,0:T(8,128)(2,1)}, u32[]{:S(2)}, u32[]{:S(2)}) collective-permute-start(bf16[128,1536]{1,0:T(8,128)(2,1)} %slice.492), channel_id=1, source_target_pairs={{8,0},{12,4},{0,8},{4,12},{24,16},{28,20},{16,24},{20,28},{9,1},{1... | collective-permute-start | bytes 1179656 | tf_op jit(solution)/shard_map/ppermute | solution.py:100
  116.7 28.9 %collective-permute-start.30 = (s32[6,256]{1,0:T(8,128)S(1)}, s32[6,256]{1,0:T(8,128)S(1)}, u32[]{:S(2)}, u32[]{:S(2)}) collective-permute-start(s32[6,256]{1,0:T(8,128)S(1)} %get-tuple-element.371.refs_0_), channel_id=1, source_target_pairs={{16,0},{20,4},{24,8},{28,12},{0,16},{4,20},{8,24},{12,28},{17,1},{... | collective-permute-start | bytes 18440 | tf_op jit(solution)/shard_map/ppermute | solution.py:100
  118.5 39.2 %collective-permute-start.28 = (s32[6,256]{1,0:T(8,128)S(1)}, s32[6,256]{1,0:T(8,128)S(1)}, u32[]{:S(2)}, u32[]{:S(2)}) collective-permute-start(s32[6,256]{1,0:T(8,128)S(1)} %get-tuple-element.371.refs_0_), channel_id=1, source_target_pairs={{4,0},{0,4},{12,8},{8,12},{20,16},{16,20},{28,24},{24,28},{5,1},{1... | collective-permute-start | bytes 18440 | tf_op jit(solution)/shard_map/ppermute | solution.py:100
  162.3 38.0 %collective-permute-start.44 = (bf16[256,2048]{1,0:T(8,128)(2,1)}, bf16[256,2048]{1,0:T(8,128)(2,1)S(1)}, u32[]{:S(2)}, u32[]{:S(2)}) collective-permute-start(bf16[256,2048]{1,0:T(8,128)(2,1)} %constant_dynamic-update-slice_fusion.4.refs_0_.refs_8_), channel_id=1, source_target_pairs={{4,0},{0,4},{12,8},{8,12},{20,16},{16,20},{28,24},{24,28},{5,1},{1... | collective-permute-start | bytes 3145736 | tf_op jit(solution)/shard_map/ppermute | solution.py:100
  170.4 32.4 %collective-permute-start.47 = (bf16[256,2048]{1,0:T(8,128)(2,1)}, bf16[256,2048]{1,0:T(8,128)(2,1)S(1)}, u32[]{:S(2)}, u32[]{:S(2)}) collective-permute-start(bf16[256,2048]{1,0:T(8,128)(2,1)} %collective-permute-done.19.refs_3_.refs_11_), channel_id=1, source_target_pairs={{4,0},{0,4},{12,8},{8,12},{20,16},{16,20},{28,24},{24,28},{5,1},{1... | collective-permute-start | bytes 3145736 | tf_op jit(solution)/shard_map/ppermute | solution.py:100
  198.6 27.7 %collective-permute-start.49 = (bf16[256,2048]{1,0:T(8,128)(2,1)S(1)}, bf16[256,2048]{1,0:T(8,128)(2,1)S(1)}, u32[]{:S(2)}, u32[]{:S(2)}) collective-permute-start(bf16[256,2048]{1,0:T(8,128)(2,1)S(1)} %constant_dynamic-update-slice_fusion.11.refs_2_.refs_0_), channel_id=1, source_target_pairs={{16,0},{20,4},{24,8},{28,12},{0,16},{4,20},{8,24},{12,28},{17,1},{... | collective-permute-start | bytes 3145736 | tf_op jit(solution)/shard_map/ppermute | solution.py:100
  202.8 36.9 %collective-permute-start.55 = (bf16[256,2048]{1,0:T(8,128)(2,1)S(1)}, bf16[256,2048]{1,0:T(8,128)(2,1)}, u32[]{:S(2)}, u32[]{:S(2)}) collective-permute-start(bf16[256,2048]{1,0:T(8,128)(2,1)S(1)} %constant_dynamic-update-slice_fusion.11.refs_2_.refs_0_), channel_id=1, source_target_pairs={{4,0},{0,4},{12,8},{8,12},{20,16},{16,20},{28,24},{24,28},{5,1},{1... | collective-permute-start | bytes 3145736 | tf_op jit(solution)/shard_map/ppermute | solution.py:100
  227.6 26.1 %collective-permute-start.53 = (bf16[256,2048]{1,0:T(8,128)(2,1)S(1)}, bf16[256,2048]{1,0:T(8,128)(2,1)S(1)}, u32[]{:S(2)}, u32[]{:S(2)}) collective-permute-start(bf16[256,2048]{1,0:T(8,128)(2,1)S(1)} %collective-permute-done.49.refs_2_.refs_4_), channel_id=1, source_target_pairs={{4,0},{0,4},{12,8},{8,12},{20,16},{16,20},{28,24},{24,28},{5,1},{1... | collective-permute-start | bytes 3145736 | tf_op jit(solution)/shard_map/ppermute | solution.py:100
  325.3 26.0 %collective-permute-start.63 = (bf16[256,2048]{1,0:T(8,128)(2,1)S(1)}, bf16[256,2048]{1,0:T(8,128)(2,1)S(1)}, u32[]{:S(2)}, u32[]{:S(2)}) collective-permute-start(bf16[256,2048]{1,0:T(8,128)(2,1)S(1)} %pad_maximum_fusion.1), channel_id=1, source_target_pairs={{0,16},{4,20},{8,24},{12,28},{16,0},{20,4},{24,8},{28,12},{1,17},{... | collective-permute-start | bytes 3145736 | tf_op jit(solution)/shard_map/ppermute | solution.py:104
  371.1 57.2 %collective-permute-start.66 = (bf16[256,2048]{1,0:T(8,128)(2,1)}, bf16[256,2048]{1,0:T(8,128)(2,1)S(1)}, u32[]{:S(2)}, u32[]{:S(2)}) collective-permute-start(bf16[256,2048]{1,0:T(8,128)(2,1)} %get-tuple-element.271), channel_id=1, source_target_pairs={{0,4},{4,0},{8,12},{12,8},{16,20},{20,16},{24,28},{28,24},{1,5},{5... | collective-permute-start | bytes 3145736 | tf_op jit(solution)/shard_map/ppermute | solution.py:104
  393.0 33.7 %collective-permute-start.75 = (bf16[256,2048]{1,0:T(8,128)(2,1)S(1)}, bf16[256,2048]{1,0:T(8,128)(2,1)S(1)}, u32[]{:S(2)}, u32[]{:S(2)}) collective-permute-start(bf16[256,2048]{1,0:T(8,128)(2,1)S(1)} %pad_maximum_fusion.3), channel_id=1, source_target_pairs={{0,16},{4,20},{8,24},{12,28},{16,0},{20,4},{24,8},{28,12},{1,17},{... | collective-permute-start | bytes 3145736 | tf_op jit(solution)/shard_map/ppermute | solution.py:104
  395.1 32.0 %collective-permute-start.70 = (bf16[256,2048]{1,0:T(8,128)(2,1)}, bf16[256,2048]{1,0:T(8,128)(2,1)S(1)}, u32[]{:S(2)}, u32[]{:S(2)}) collective-permute-start(bf16[256,2048]{1,0:T(8,128)(2,1)} %pad_maximum_fusion.2), channel_id=1, source_target_pairs={{0,8},{4,12},{8,0},{12,4},{16,24},{20,28},{24,16},{28,20},{1,9},{5... | collective-permute-start | bytes 3145736 | tf_op jit(solution)/shard_map/ppermute | solution.py:104
  452.8 43.8 %collective-permute-start.88 = (bf16[704,256]{1,0:T(8,128)(2,1)}, bf16[704,256]{1,0:T(8,128)(2,1)S(1)}, u32[]{:S(2)}, u32[]{:S(2)}) collective-permute-start(bf16[704,256]{1,0:T(8,128)(2,1)} %get-tuple-element.297), channel_id=1, source_target_pairs={{0,4},{4,0},{8,12},{12,8},{16,20},{20,16},{24,28},{28,24},{1,5},{5... | collective-permute-start | bytes 1081352 | tf_op jit(solution)/shard_map/ppermute | solution.py:104
  470.5 27.8 %collective-permute-start.87 = (bf16[64,2048]{1,0:T(8,128)(2,1)}, bf16[64,2048]{1,0:T(8,128)(2,1)S(1)}, u32[]{:S(2)}, u32[]{:S(2)}) collective-permute-start(bf16[64,2048]{1,0:T(8,128)(2,1)} %pad_maximum_fusion.18), channel_id=1, source_target_pairs={{0,3},{1,0},{2,1},{3,2},{4,7},{5,4},{6,5},{7,6},{8,11},{9,8},{10,9... | collective-permute-start | bytes 786440 | tf_op jit(solution)/shard_map/ppermute | solution.py:176
  473.8 28.4 %collective-permute-start.85 = (bf16[64,2048]{1,0:T(8,128)(2,1)}, bf16[64,2048]{1,0:T(8,128)(2,1)S(1)}, u32[]{:S(2)}, u32[]{:S(2)}) collective-permute-start(bf16[64,2048]{1,0:T(8,128)(2,1)} %pad_maximum_fusion.17), channel_id=1, source_target_pairs={{0,1},{1,2},{2,3},{3,0},{4,5},{5,6},{6,7},{7,4},{8,9},{9,10},{10,1... | collective-permute-start | bytes 786440 | tf_op jit(solution)/shard_map/ppermute | solution.py:176
  498.3 65.4 %collective-permute-start.83 = (bf16[64,2048]{1,0:T(8,128)(2,1)}, bf16[64,2048]{1,0:T(8,128)(2,1)}, u32[]{:S(2)}, u32[]{:S(2)}) collective-permute-start(bf16[64,2048]{1,0:T(8,128)(2,1)} %pad_maximum_fusion.16), channel_id=1, source_target_pairs={{0,3},{1,0},{2,1},{3,2},{4,7},{5,4},{6,5},{7,6},{8,11},{9,8},{10,9... | collective-permute-start | bytes 786440 | tf_op jit(solution)/shard_map/ppermute | solution.py:176
  526.1 38.2 %collective-permute-start.81 = (bf16[64,2048]{1,0:T(8,128)(2,1)S(1)}, bf16[64,2048]{1,0:T(8,128)(2,1)}, u32[]{:S(2)}, u32[]{:S(2)}) collective-permute-start(bf16[64,2048]{1,0:T(8,128)(2,1)S(1)} %copy-done.57), channel_id=1, source_target_pairs={{0,1},{1,2},{2,3},{3,0},{4,5},{5,6},{6,7},{7,4},{8,9},{9,10},{10,1... | collective-permute-start | bytes 786440 | tf_op jit(solution)/shard_map/ppermute | solution.py:176
  (219 other events, 3048.4 us)

commit v4 on v3

--- a/solution.py
+++ b/solution.py
@@ -311,7 +311,7 @@
     expert = lax.broadcasted_iota(jnp.int32, (EXPERTS, count), 0) + base
     expert = jnp.where(expert >= EXPERTS, expert - EXPERTS, expert)
     chosen = expert == routes[0:1]
-    for k in range(1, routes.shape[0]):
+    for k in range(1, TOP):
         chosen = chosen | (expert == routes[k : k + 1])
     chosen = chosen.astype(F32)
     rows = max(local, 16)
@@ -325,18 +325,15 @@
     return jnp.concatenate(parts, axis=0), chosen
 
 
-def dispatch_grads_kernel(local, base_ref, routes_ref, *refs):
-    shared_ref, slot_ref, raw_ref = refs[-3:]
-    pieces = refs[:-3]
-    half = len(pieces) // 2
-    for core in range(2):
-
-        @pl.when(pl.program_id(0) % 2 == core)
+def dispatch_grads_kernel(local, base_ref, *refs):
+    routes, grads, shared_ref = refs[:2], refs[2:4], refs[4]
+    slot_ref, raw_ref = refs[-2:]
+    for i in range(2):
+
+        @pl.when(pl.program_id(0) == i)
         def _():
-            pick, _ = pick_rows(routes_ref[0], base_ref[0], local)
-            values = jnp.concatenate(
-                [piece[...] for piece in pieces[core * half : (core + 1) * half]], axis=0
-            )
+            pick, _ = pick_rows(routes[i][...], base_ref[0], local)
+            values = grads[i][...]
             slot_ref[...] = (
                 dot_nn(pick.astype(BF16), values).astype(BF16).reshape(slot_ref.shape)
             )
@@ -511,31 +508,27 @@
     )(*prefetch, *operands, *chained)
 
 
-def dispatch_grads(local, base, routes, grads, shared_out):
-    sequences, top, count = routes.shape
-    width = grads[0].shape[1]
-    part = count * 2 // len(grads)
+def dispatch_grads(pair, sequences, local, base, routes, grads, shared_out, held):
+    count, width = grads[0].shape
     units = shared_out.shape[0]
-    return pl.pallas_call(
+    operands = [*routes, *grads, shared_out]
+    return chain_call(
         functools.partial(dispatch_grads_kernel, local),
-        grid_spec=pltpu.PrefetchScalarGridSpec(
-            num_scalar_prefetch=1,
-            grid=(sequences,),
-            in_specs=[pl.BlockSpec((1, top, count), lambda s, *_: (s, 0, 0))]
-            + [pl.BlockSpec((part, width), lambda s, *_: (s // 2, 0))] * len(grads)
-            + [whole(shared_out.shape)],
-            out_specs=[
-                pl.BlockSpec((local, SLOTS, width), lambda s, *_: (0, s, 0)),
-                pl.BlockSpec((1, units, count), lambda s, *_: (s, 0, 0)),
-            ],
-        ),
-        out_shape=[
+        "dispatch_grads",
+        (2,),
+        [base],
+        operands,
+        [whole(a.shape) for a in operands],
+        held,
+        [
+            pl.BlockSpec((local, SLOTS, width), lambda i, *_: (0, 2 * pair + i, 0)),
+            pl.BlockSpec((1, units, count), lambda i, *_: (2 * pair + i, 0, 0)),
+        ],
+        [
             jax.ShapeDtypeStruct((local, sequences * SLOTS, width), BF16),
             jax.ShapeDtypeStruct((sequences, units, count), F32),
         ],
-        compiler_params=params("arbitrary"),
-        name="dispatch_grads",
-    )(base, routes, *grads, shared_out)
+    )
 
 
 def dispatch_rows(pair, sequences, local, base, routes, rows, side, raws, held):
@@ -746,19 +739,13 @@
 
 def side_grads_kernel(sequences, block_ref, *refs):
     rows, grads, rest = refs[:sequences], refs[sequences : 2 * sequences], refs[2 * sequences :]
-    half = len(grads) // 2
-    part = rows[0].shape[0] // half
     logits_ref, hidden_ref, back_ref, first_ref, *parts, router_ref, left_ref, in_ref, out_ref = rest
     units = hidden_ref.shape[1]
     for s in range(sequences):
         left_ref[: 2 * units] = back_ref[s]
         left_ref[2 * units :] = logits_ref[s]
         value = dot_nn(left_ref[...], rows[s][...])
-        held = grads[s % 2 * half : (s % 2 + 1) * half]
-        other = dot_nn(
-            hidden_ref[s],
-            jnp.concatenate([piece[s // 2 * part : (s // 2 + 1) * part] for piece in held], axis=0),
-        )
+        other = dot_nn(hidden_ref[s], grads[s][...])
         if s == 0:
             in_ref[...] = value
             out_ref[...] = other
@@ -806,14 +793,19 @@
     )(blocks, *operands, base)
 
 
-def join_columns_kernel(block_ref, *refs):
-    pieces, router_ref, side_ref, out_ref = refs[:-3], refs[-3], refs[-2], refs[-1]
+def join_columns_kernel(used, block_ref, *refs):
+    shards = (len(refs) - 3) // 2
+    pieces, router_ref, side_ref, out_ref, routes = (
+        refs[:shards], refs[shards], refs[shards + 1], refs[shards + 2], refs[shards + 3 :]
+    )
     units = out_ref.shape[0]
     columns = pieces[0].shape[1]
     for k, piece in enumerate(pieces):
         at = pl.ds(pl.multiple_of(block_ref[k] * columns, columns), columns)
         side_ref[: 2 * units, at] = piece[: 2 * units]
         out_ref[:, at] = piece[2 * units :]
+        routes[k][...] = piece[:units].astype(F32)[used:].astype(jnp.int32)
+    side_ref[used:units] = jnp.zeros((units - used, side_ref.shape[1]), BF16)
     side_ref[2 * units :] = router_ref[...]
 
 
@@ -867,10 +859,17 @@
 def latent_kernel(depth, *refs):
     pieces = refs[:depth]
     gain_ref, weight_ref, kv_gain_ref, cosine_ref, sine_ref = refs[depth : depth + 5]
-    normed_ref, comp_ref, low_ref, key_ref = refs[depth + 5 :]
+    normed_ref, comp_ref, low_ref, key_ref, wide_ref = refs[depth + 5 :]
+    half = ROPE // 2
+    wide_ref[:KVR] = weight_ref[:KVR]
+    for i in range(2):
+        piece = weight_ref[KVR + i * half : KVR + (i + 1) * half]
+        for j in range(LANES // half):
+            start = KVR + i * LANES + j * half
+            wide_ref[start : start + half] = piece
     normed = (unit_rows(pieces) * gain_ref[...]).astype(BF16)
     normed_ref[...] = normed
-    latent = dot_nt(normed, weight_ref[...])
+    latent = dot_nt(normed, wide_ref[...])
     compressed = latent[:, :KVR]
     comp_ref[...] = compressed
     inverse = lax.rsqrt(jnp.mean(compressed * compressed, axis=-1, keepdims=True) + EPSILON)
@@ -1116,6 +1115,7 @@
             jax.ShapeDtypeStruct((count, KVR), F32),
             jax.ShapeDtypeStruct((count, KVR), BF16),
             jax.ShapeDtypeStruct((count, 2 * LANES), BF16),
+            jax.ShapeDtypeStruct((KVR + 2 * LANES, width), BF16),
         ],
         [],
     )
@@ -1243,8 +1243,13 @@
     shared_units = shared.shape[0] // 3
     side = jnp.concatenate([shared[: 2 * shared_units], router])
     shared_out = shared[2 * shared_units :]
-    by_core = [jnp.concatenate(grads[core::2]) for core in range(2)]
-    slot_grads, shared_raw = dispatch_grads(local, base, jnp.stack(routes), by_core, shared_out)
+    held = [None, None]
+    for m in pairs:
+        at = slice(2 * m, 2 * m + 2)
+        held = dispatch_grads(
+            m, sequences, local, base, routes[at], grads[at], shared_out, held
+        )
+    slot_grads, shared_raw = held
     raw = expert_raw(slot_grads, expert_out)
     held = [None] * 6
     for m in pairs:
@@ -1524,83 +1529,93 @@
     base = (lax.axis_index("expert") * local).astype(jnp.int32)[None]
 
     tokens = grid.ring_gather(tokens_in)
-    quarter = own_rows // 2
-    along_x = grid.fetch(out_grad, (0, 1, 0))
-    along_y = grid.fetch(out_grad, (1, 0, 0))
-    crossed = [
-        grid.fetch(along_x[:quarter], (1, 0, 0)),
-        grid.fetch(along_y[quarter:], (0, 1, 0)),
-    ]
-    plane = jnp.concatenate([out_grad, along_x, along_y, *crossed])
-    packs = grid.gather(
-        after(pack_weights(w_query, w_keyval, w_output, heads), *crossed, tokens[1], tokens[4])
-    )
-    planes = grid.ring_near(after(plane, *tokens))
-    far = jnp.concatenate(grid.ring_far(*planes))
-    routes_t = jnp.concatenate(grid.relative_depth(routes.T, 1), axis=1)
-    routes_all = grid.gather_small(routes_t)
-
+    packs = grid.gather(pack_weights(w_query, w_keyval, w_output, heads))
+    group_grads = jnp.concatenate(grid.ring_gather(after(out_grad, packs[2], packs[4], *tokens)))
     position = (
         (own_depth + jnp.arange(row_count) // own_rows) % depth * own_rows
         + jnp.arange(row_count) % own_rows
     )
     cosine, sine = (jnp.tile(table, (1, heads)) for table in rope_tables(position))
     bias = jnp.where(position[None, :] <= position[:, None], 0.0, -1e30).astype(F32)
-    half = ROPE // 2
-    latent_t = w_latent.T
-    latent_t = jnp.concatenate(
-        [latent_t[:KVR]] + [latent_t[KVR : KVR + half]] * heads + [latent_t[KVR + half :]] * heads
-    )
-    normed, compressed, low, key = latent_rows(
-        tokens, attn_gain, latent_t, kv_gain, cosine, sine
+    normed, compressed, low, key, latent_t = latent_rows(
+        tokens, attn_gain, w_latent.T, kv_gain, cosine, sine
     )
 
     units = w_shared_out.shape[0] // grid.experts
-    padding = ((0, -units % 32), (0, 0))
+    padding = -units % 32
+    padded_units = units + padding
+    shared_in, shared_out = after(w_shared_in, packs[2]), after(w_shared_out, packs[2])
+    routes_t = jnp.concatenate(grid.relative_depth(routes.T, 1), axis=1).astype(BF16)
+    assert padding >= TOP and padding % 8 == 0 and units % 8 == 0
+    fill = jnp.zeros((padding, w_shared_out.shape[1]), BF16)
+    routes_fill = lax.dynamic_update_slice(fill, routes_t, (0, 0))
     shared_parts = [
-        jnp.concatenate([jnp.pad(part, padding) for part in parts])
-        for parts in zip(
-            grid.relative(w_shared_in[0].T, 0),
-            grid.relative(w_shared_in[1].T, 0),
-            grid.relative(w_shared_out, 0),
+        jnp.concatenate([first, routes_fill, second, fill, third, fill])
+        for first, second, third in zip(
+            grid.relative(shared_in[0].T, 0),
+            grid.relative(shared_in[1].T, 0),
+            grid.relative(shared_out, 0),
         )
     ]
-    pieces = grid.exchange([after(part, packs[2], packs[4]) for part in shared_parts])
-    router = jnp.roll(w_router.T, -base[0], axis=0)
-    padded_units = units + padding[0][1]
-    side, shared_out = vmem_call(
-        join_columns_kernel,
+    pieces = grid.exchange([after(part, packs[6]) for part in shared_parts])
+    router = jnp.roll(after(w_router, packs[2]).T, -base[0], axis=0)
+    side, shared_out, *routes_all = vmem_call(
+        functools.partial(join_columns_kernel, units),
         "join_columns",
         blocks,
         [*pieces, router],
         [
             jax.ShapeDtypeStruct((2 * padded_units + EXPERTS, width), BF16),
             jax.ShapeDtypeStruct((padded_units, width), BF16),
-        ],
+        ]
+        + [jax.ShapeDtypeStruct((padding, row_count), jnp.int32)] * sequences,
         [],
     )
 
     query, keyval, soft, attended, part = attention_forward(
-        heads, blocks, packs, after(normed, far), low, key, bias, cosine, sine
-    )
-    core_grads = [plane, planes[0], far, planes[1]]
-    all_grads = core_grads + [grid.fetch(piece, (0, 0, 1)) for piece in core_grads]
+        heads, blocks, packs, after(normed, group_grads), low, key, bias, cosine, sine
+    )
+    part = after(part, *pieces)
+
+    middle = row_count // 2
+    group_grads = after(group_grads, part)
+    along_x = grid.fetch(group_grads, (0, 1, 0))
+    along_y = grid.fetch(group_grads, (1, 0, 0))
     stream = tokens_in.astype(F32)
     residual = stream + grid.ring_reduce(split_rows(part, depth))
     normed_two, inverse_two = rms_forward(residual, ffn_gain)
     normed_two = normed_two.astype(BF16)
-
-    near_rows = grid.ring_near(after(normed_two, *routes_all))
+    near_rows = grid.ring_near(normed_two)
+    first = grid.fetch(along_x[:middle], (1, 0, 0))
+    second = grid.fetch(along_y[middle:], (0, 1, 0))
+    all_grads = [group_grads, grid.fetch(group_grads, (0, 0, 1))]
+    for held in (along_x, along_y):
+        all_grads += [held, grid.fetch(held, (0, 0, 1))]
+    near_rows = [after(piece, along_x, along_y) for piece in near_rows]
     far_rows = grid.ring_far(*near_rows)
     group_rows = jnp.concatenate([normed_two, near_rows[0], *far_rows, near_rows[1]])
-    group_rows = after(group_rows, *pieces)
-    middle = row_count // 2
+    group_rows = after(group_rows, first, second)
+    all_grads += [
+        jnp.concatenate([first, second]),
+        jnp.concatenate([grid.fetch(first, (0, 0, 1)), grid.fetch(second, (0, 0, 1))]),
+    ]
+
     along_x = grid.fetch(group_rows, (0, 1, 0))
     along_y = grid.fetch(group_rows, (1, 0, 0))
     pair_rows = grid.fetch(group_rows, (0, 0, 1))
-    slot_grads, shared_raw = dispatch_grads(
-        local, base, jnp.stack(routes_all), all_grads, after(shared_out, group_rows)
-    )
+    held = [None, None]
+    for m in pairs:
+        held = dispatch_grads(
+            m,
+            sequences,
+            local,
+            base,
+            routes_all[2 * m : 2 * m + 2],
+            all_grads[2 * m : 2 * m + 2],
+            after(shared_out, group_rows),
+            held,
+        )
+    slot_grads, shared_raw = held
     along_x, along_y = after(along_x, slot_grads), after(along_y, slot_grads)
     first = grid.fetch(along_x[:middle], (1, 0, 0))
     second = grid.fetch(along_y[middle:], (0, 1, 0))
@@ -1680,6 +1695,7 @@
     near_grads = grid.ring_near(grad_low)
     out_own_2 = low_add(out_2, grid.send(out_3, (0, 0, 1)))
     out_own_0 = low_add(out_0, grid.send(out_1, (0, 0, 1)))
+    out_first, out_second = after(out_first, *near_grads), after(out_second, *near_grads)
     out_to_y = jnp.concatenate([low_add(out_own_4[front], out_first), out_own_4[rear]])
     out_to_x = jnp.concatenate([out_own_2[front], low_add(out_own_2[rear], out_second)])
     out_from_x = grid.send(out_to_x, (0, 1, 0))
@@ -1723,8 +1739,6 @@
         after(grad_query, *returned),
         grad_keyval,
     )
-    ffn_total = grid.ring_reduce(split_rows(after(out_group, grad_query), depth))
-    block_out = (residual + ffn_total).astype(BF16)
     sums, chunk_first, chunk_mark = grid.reduce_parts(chunks)
     share = local // 4
     held = [None, None]
@@ -1740,9 +1754,17 @@
             held[:2],
         )
 
+    def ring_rounds(rows, start, middle, stop):
+        parts = split_rows(after(rows, start), depth)
+        first, second = grid.ring_start(parts)
+        ahead, behind, _ = grid.ring_finish(parts, after(first, middle), after(second, middle))
+        return sum(a.astype(F32) for a in (parts[0], after(ahead, stop), after(behind, stop)))
+
     held = weights(0, held, grad_packs[0], chunk_first)
+    marks = [held[2]]
     held = weights(1, held, held[2], *chunk_mark)
     mark = held[2]
+    marks.append(mark)
     size = CHUNK_ROWS // depth
     columns = width // grid.experts
     parts = vmem_call(
@@ -1755,22 +1777,15 @@
     )
     pack_sums, pack_first, pack_mark = grid.reduce_parts([after(pack, mark) for pack in grad_packs])
     held = weights(2, held, parts[0], pack_first)
+    marks.append(held[2])
     part = grid.reduce_depth([parts[0]] + [after(part, pack_first) for part in parts[1:]])
     part = after(part, held[2]).astype(BF16)
     *held, mark = weights(3, held, part, *pack_mark)
     grad_expert_in, grad_expert_out = held
+    marks.append(mark)
+    block_out = (residual + ring_rounds(out_group, *marks[:3])).astype(BF16)
+    grad_normed_one = ring_rounds(grad_normed_one, *marks[1:])
     parts = [after(piece, mark) for piece in grid.gather_depth(part)]
-    sum_shared_in, sum_shared_out = vmem_call(
-        functools.partial(join_rows_kernel, units),
-        "join_rows",
-        blocks,
-        [after(returned[0], mark), *returned[1:]],
-        [
-            jax.ShapeDtypeStruct((2, units * grid.experts, width // grid.experts), F32),
-            jax.ShapeDtypeStruct((units * grid.experts, width // grid.experts), F32),
-        ],
-        [],
-    )
     (chunk,) = vmem_call(
         join_depth_kernel,
         "join_depth",
@@ -1779,11 +1794,24 @@
         [jax.ShapeDtypeStruct((CHUNK_ROWS, columns), BF16)],
         [],
     )
+    sum_shared_in, sum_shared_out = vmem_call(
+        functools.partial(join_rows_kernel, units),
+        "join_rows",
+        blocks,
+        [after(returned[0], chunk), *returned[1:]],
+        [
+            jax.ShapeDtypeStruct((2, units * grid.experts, width // grid.experts), F32),
+            jax.ShapeDtypeStruct((units * grid.experts, width // grid.experts), F32),
+        ],
+        [],
+    )
+    gathered = grid.gather(chunk)
+    gathered[0] = after(gathered[0], sum_shared_out, *pack_sums[1:])
     sum_latent, sum_router, sum_gains = vmem_call(
         functools.partial(replicated_kernel, KVR + ROPE),
         "replicated",
         blocks,
-        grid.gather(chunk),
+        gathered,
         [
             jax.ShapeDtypeStruct((KVR + ROPE, width), F32),
             jax.ShapeDtypeStruct((EXPERTS, width), F32),
@@ -1793,7 +1821,6 @@
     )
     sum_kv_gain = sum_gains[2 : 2 + KVR // columns, :columns].reshape(KVR)
 
-    grad_normed_one = grid.ring_reduce(split_rows(grad_normed_one, depth))
     inverse_one = lax.rsqrt(jnp.mean(stream * stream, axis=-1, keepdims=True) + EPSILON)
     grad_in = grad_residual + rms_backward(stream, inverse_one, attn_gain, grad_normed_one)[0]
     sum_query, sum_keyval, sum_output = unpack_weights(

time: 609 us -> 554 us (0.910)
  waiting for transfers between devices: 148 us -> 107 us
  local copies, waits for them, and re-layouts: 59.9 us -> 38.5 us
  starting transfers between devices: 120 us -> 129 us
    ppermute x32, waiting for transfers between devices: 79.2 us -> 52.5 us  [ring(): lax.ppermute(array, 'tensor', [(i, (i + step) % depth) for i in range(dep...]
    ppermute x46, waiting for transfers between devices: 41.9 us -> 19.2 us  [send(): return lax.ppermute(array, 'expert', pairs)]
    pallas_call x12 -> x16, Pallas kernels: 80.9 us -> 99.1 us  [chain_call(): pl.pallas_call(kernel, grid_spec=pltpu.PrefetchScalarGridSpec(num_scalar_...]
    pallas_call x1 -> x0, Pallas kernels: 13.9 us -> none  [dispatch_grads(): pl.pallas_call(functools.partial(dispatch_grads_kernel, local), grid_spec...]
    unnamed x260 -> x199, local copies, waits for them, and re-layouts: 29.7 us -> 20.2 us
    ppermute x42 -> x36, waiting for transfers between devices: 26.6 us -> 34 us  [fetch(): return lax.ppermute(array, 'expert', pairs)]
    ppermute x3, starting transfers between devices: 3.1 us -> 9.33 us  [gather_depth(): lax.ppermute(shard, 'tensor', [((i + k) % depth, i) for i in range(depth)])]
    ppermute x42 -> x36, starting transfers between devices: 28.5 us -> 23.3 us  [fetch(): return lax.ppermute(array, 'expert', pairs)]
  transfers between devices with their start and end apart: 126 -> 120, of which waited for: 37 -> 33; matrix products, arithmetic and copies ran while one was open for 13% -> 9% of each run, Pallas kernels for 31% -> 34%
where the time goes in v4:
time: 554 us; the launch traced here: 545 us
  Pallas kernels  239 us (43%)
  starting transfers between devices  129 us (23%)
  waiting for transfers between devices  107 us (19%)
  local copies, waits for them, and re-layouts  38.5 us (7%)
  other arithmetic  27.9 us (5%)
    pallas_call x16, Pallas kernels, chain_call(): pl.pallas_call(kernel, grid_spec=pltpu.PrefetchScalarGridSpec(num_scalar_...  99.1 us
    ppermute x32, starting transfers between devices, ring(): lax.ppermute(array, 'tensor', [(i, (i + step) % depth) for i in range(dep...  58.6 us
    ppermute x32, waiting for transfers between devices, ring(): lax.ppermute(array, 'tensor', [(i, (i + step) % depth) for i in range(dep...  52.5 us
    pallas_call x8, Pallas kernels, vmem_call(): pl.pallas_call(kernel, grid_spec=pltpu.PrefetchScalarGridSpec(num_scalar_...  46.5 us
    ppermute x36, waiting for transfers between devices, fetch(): return lax.ppermute(array, 'expert', pairs)  34 us
    ppermute x46, starting transfers between devices, send(): return lax.ppermute(array, 'expert', pairs)  33.4 us
    pallas_call x1, Pallas kernels, expert_rows(): pl.pallas_call(functools.partial(expert_kernel, units), grid=(local, slot...  31.2 us
    ppermute x36, starting transfers between devices, fetch(): return lax.ppermute(array, 'expert', pairs)  23.3 us
  transfers between devices with their start and end apart: 120, of which 33 were waited for; matrix products, arithmetic and copies ran while one was open for 9% of the time, Pallas kernels for 34%

profile of v4, /device:TPU:0, one launch (start us, length us, event | category | flops | bytes accessed | tf_op | source)
XLA Modules:
  0.0 544.8 jit_solution(8331635623651253441)
XLA Ops:
  74.4 9.1 %attention_forward.1 = (bf16[256,768]{1,0:T(8,128)(2,1)}, bf16[256,1024]{1,0:T(8,128)(2,1)}, f32[4,256,256]{2,1,0:T(8,128)}, bf16[256,512]{1,0:T(8,128)(2,1)}, bf16[256,2048]{1,0:T(8,128)(2,1)}) custom-call(s32[8]{0:T(128)} %stack.35.block_ref, bf16[256,1536]{1,0:T(8,128)(2,1)} %copy-done, bf16[256,1536]{1,0:T(8,128)(2,1)} %collective-permute-done.refs_1_, ...), custom_call_target="tpu_custom_call" | custom-call | tf_op jit(solution)/shard_map/attention_forward/pallas_call | solution.py:1090
  103.8 5.7 %collective-permute-done.25 = bf16[64,2048]{1,0:T(8,128)(2,1)S(1)} collective-permute-done((bf16[64,2048]{1,0:T(8,128)(2,1)S(1)}, bf16[64,2048]{1,0:T(8,128)(2,1)S(1)}, u32[]{:S(2)}, u32[]{:S(2)}) %collective-permute-start.25) | collective-permute-done | bytes 262176 | tf_op jit(solution)/shard_map/ppermute | solution.py:176
  115.5 5.8 %collective-permute-done.30.refs_2_.refs_12_ = bf16[256,2048]{1,0:T(8,128)(2,1)S(1)} collective-permute-done((bf16[256,2048]{1,0:T(8,128)(2,1)}, bf16[256,2048]{1,0:T(8,128)(2,1)S(1)}, u32[]{:S(2)}, u32[]{:S(2)}) %collective-permute-start.30) | collective-permute-done | bytes 1048608 | tf_op jit(solution)/shard_map/ppermute | solution.py:100
  132.4 6.0 %collective-permute-done.33 = bf16[32,2048]{1,0:T(8,128)(2,1)S(1)} collective-permute-done((bf16[32,2048]{1,0:T(8,128)(2,1)S(1)}, bf16[32,2048]{1,0:T(8,128)(2,1)S(1)}, u32[]{:S(2)}, u32[]{:S(2)}) %collective-permute-start.33) | collective-permute-done | bytes 131104 | tf_op jit(solution)/shard_map/ppermute | solution.py:176
  170.8 11.5 %expert_raw.1.raw_ref = f32[8,352,256]{2,1,0:T(8,128)} custom-call(bf16[8,256,2048]{2,1,0:T(8,128)(2,1)} %get-tuple-element.265.grads_ref, bf16[8,352,2048]{2,1,0:T(8,128)(2,1)} %out_ref.3), custom_call_target="tpu_custom_call" | custom-call | tf_op jit(solution)/shard_map/expert_raw/pallas_call | solution.py:585
  199.5 5.8 %dispatch_rows.6 = (bf16[8,256,2048]{2,1,0:T(8,128)(2,1)}, bf16[8,256,128]{2,1,0:T(8,128)(2,1)}, bf16[8,256,256]{2,1,0:T(8,128)(2,1)}, f32[8,2,64,256]{3,2,1,0:T...) custom-call(s32[1]{0:T(128)} %bitcast.49.base_ref.refs_19_, ...), custom_call_target="tpu_custom_call", output_to_operand_aliasing={{0}: (7, {}), {1}: (8, {}), {2}: (9, {}), {3}: (10, {}), {4... | custom-call | tf_op jit(solution)/shard_map/dispatch_rows/pallas_call | solution.py:495
  210.7 31.2 %expert_rows.1 = (bf16[8,256,2048]{2,1,0:T(8,128)(2,1)}, bf16[8,256,128]{2,1,0:T(8,128)(2,1)}, bf16[8,352,256]{2,1,0:T(8,128)(2,1)}, bf16[8,704,256]{2,1,0:T(8,128)(2,1)}) custom-call(bf16[8,256,2048]{2,1,0:T(8,128)(2,1)} %get-tuple-element.411.rows_ref, bf16[8,256,128]{2,1,0:T(8,128)(2,1)} %get-tuple-element.290.info_ref, bf16[8,704,2048]{2,1,0:T(8,128)(2,1)} %bitcast.103, ...), custom_call_target="tpu_custom_call" | custom-call | tf_op jit(solution)/shard_map/expert_rows/pallas_call | solution.py:600
  241.9 6.1 %combine_back.4 = (bf16[8,64,256]{2,1,0:T(8,128)(2,1)}, bf16[256,2048]{1,0:T(8,128)(2,1)}, bf16[256,2048]{1,0:T(8,128)(2,1)}) custom-call(bf16[8,256,256]{2,1,0:T(8,128)(2,1)} %get-tuple-element.288.refs_0_.pick_ref, bf16[8,256,2048]{2,1,0:T(8,128)(2,1)} %get-tuple-element.298.refs_1_, bf16[8,256,128]{2,1,0:T(8,128)(2,1)} %get-tuple-element.293.refs_2_, ...), custom_call_target="tpu_custom_call" | custom-call | tf_op jit(solution)/shard_map/combine_back/pallas_call | solution.py:495
  248.0 6.2 %combine_back.5 = (bf16[8,64,256]{2,1,0:T(8,128)(2,1)}, bf16[256,2048]{1,0:T(8,128)(2,1)}, bf16[256,2048]{1,0:T(8,128)(2,1)}) custom-call(bf16[8,256,256]{2,1,0:T(8,128)(2,1)} %get-tuple-element.288.refs_0_.pick_ref, bf16[8,256,2048]{2,1,0:T(8,128)(2,1)} %get-tuple-element.298.refs_1_, ...), custom_call_target="tpu_custom_call", output_to_operand_aliasing={{0}: (6, {})} | custom-call | tf_op jit(solution)/shard_map/combine_back/pallas_call | solution.py:495
  257.4 6.1 %combine_back.6 = (bf16[8,64,256]{2,1,0:T(8,128)(2,1)}, bf16[256,2048]{1,0:T(8,128)(2,1)}, bf16[256,2048]{1,0:T(8,128)(2,1)}) custom-call(bf16[8,256,256]{2,1,0:T(8,128)(2,1)} %get-tuple-element.288.refs_0_.pick_ref, bf16[8,256,2048]{2,1,0:T(8,128)(2,1)} %get-tuple-element.298.refs_1_, ...), custom_call_target="tpu_custom_call", output_to_operand_aliasing={{0}: (6, {})} | custom-call | tf_op jit(solution)/shard_map/combine_back/pallas_call | solution.py:495
  264.0 6.1 %combine_back.7 = (bf16[8,64,256]{2,1,0:T(8,128)(2,1)}, bf16[256,2048]{1,0:T(8,128)(2,1)}, bf16[256,2048]{1,0:T(8,128)(2,1)}) custom-call(bf16[8,256,256]{2,1,0:T(8,128)(2,1)} %get-tuple-element.288.refs_0_.pick_ref, bf16[8,256,2048]{2,1,0:T(8,128)(2,1)} %get-tuple-element.298.refs_1_, ...), custom_call_target="tpu_custom_call", output_to_operand_aliasing={{0}: (6, {})} | custom-call | tf_op jit(solution)/shard_map/combine_back/pallas_call | solution.py:495
  274.7 12.7 %expert_out_rows.1.slots_ref = bf16[8,256,2048]{2,1,0:T(8,128)(2,1)} custom-call(bf16[8,352,256]{2,1,0:T(8,128)(2,1)} %get-tuple-element.311.hidden_ref, bf16[8,352,2048]{2,1,0:T(8,128)(2,1)} %out_ref.3), custom_call_target="tpu_custom_call" | custom-call | tf_op jit(solution)/shard_map/expert_out_rows/pallas_call | solution.py:630
  292.6 5.4 combine_out.5
  345.4 11.8 %side_grads.1 = (bf16[288,256]{1,0:T(8,128)(2,1)}, bf16[288,256]{1,0:T(8,128)(2,1)}, bf16[288,256]{1,0:T(8,128)(2,1)}, bf16[288,256]{1,0:T(8,128)(2,1)}, bf16[28...) custom-call(s32[8]{0:T(128)} %stack.35.block_ref, ...), custom_call_target="tpu_custom_call" | custom-call | tf_op jit(solution)/shard_map/side_grads/pallas_call | solution.py:775
  365.6 6.1 %collective-permute-done.75.refs_2_ = bf16[288,256]{1,0:T(8,128)(2,1)S(1)} collective-permute-done((bf16[288,256]{1,0:T(8,128)(2,1)}, bf16[288,256]{1,0:T(8,128)(2,1)S(1)}, u32[]{:S(2)}, u32[]{:S(2)}) %collective-permute-start.75) | collective-permute-done | bytes 147488 | tf_op jit(solution)/shard_map/ppermute | solution.py:104
  376.6 14.2 %attention_backward.1 = (bf16[256,768]{1,0:T(8,128)(2,1)}, bf16[256,1024]{1,0:T(8,128)(2,1)}, bf16[256,2048]{1,0:T(8,128)(2,1)}, bf16[704,256]{1,0:T(8,128)(2,1)...) custom-call(s32[8]{0:T(128)} %stack.35.block_ref, ...), custom_call_target="tpu_custom_call" | custom-call | tf_op jit(solution)/shard_map/attention_backward/pallas_call | solution.py:1090
  392.2 6.2 %attention_weights.1 = (bf16[256,1536]{1,0:T(8,128)(2,1)}, bf16[256,1536]{1,0:T(8,128)(2,1)}, bf16[256,1536]{1,0:T(8,128)(2,1)}, bf16[256,1536]{1,0:T(8,128)(2,1...) custom-call(s32[8]{0:T(128)} %stack.35.block_ref, ...), custom_call_target="tpu_custom_call" | custom-call | tf_op jit(solution)/shard_map/attention_weights/pallas_call | solution.py:1090
  404.1 8.7 %weight_grads.4 = (f32[8,704,2048]{2,1,0:T(8,128)}, f32[8,352,2048]{2,1,0:T(8,128)}, f32[8,128]{1,0:T(8,128)}) custom-call(bf16[8,256,2048]{2,1,0:T(8,128)(2,1)} %get-tuple-element.411.rows_ref, bf16[8,256,2048]{2,1,0:T(8,128)(2,1)} %get-tuple-element.265.grads_ref, bf16[8,352,256]{2,1,0:T(8,128)(2,1)} %get-tuple-element.311.hidden_ref, ...), custom_call_target="tpu_custom_call" | custom-call | tf_op jit(solution)/shard_map/weight_grads/pallas_call | solution.py:495
  420.5 8.8 %weight_grads.5 = (f32[8,704,2048]{2,1,0:T(8,128)}, f32[8,352,2048]{2,1,0:T(8,128)}, f32[8,128]{1,0:T(8,128)}) custom-call(bf16[8,256,2048]{2,1,0:T(8,128)(2,1)} %get-tuple-element.411.rows_ref, bf16[8,256,2048]{2,1,0:T(8,128)(2,1)} %get-tuple-element.265.grads_ref, ...), custom_call_target="tpu_custom_call", output_to_operand_aliasing={{0}: (4, {}), {1}: (5, {})} | custom-call | tf_op jit(solution)/shard_map/weight_grads/pallas_call | solution.py:495
  438.9 8.8 %weight_grads.6 = (f32[8,704,2048]{2,1,0:T(8,128)}, f32[8,352,2048]{2,1,0:T(8,128)}, f32[8,128]{1,0:T(8,128)}) custom-call(bf16[8,256,2048]{2,1,0:T(8,128)(2,1)} %get-tuple-element.411.rows_ref, bf16[8,256,2048]{2,1,0:T(8,128)(2,1)} %get-tuple-element.265.grads_ref, ...), custom_call_target="tpu_custom_call", output_to_operand_aliasing={{0}: (4, {}), {1}: (5, {})} | custom-call | tf_op jit(solution)/shard_map/weight_grads/pallas_call | solution.py:495
  459.1 5.5 %collective-permute-start.95 = (bf16[64,2048]{1,0:T(8,128)(2,1)S(1)}, bf16[64,2048]{1,0:T(8,128)(2,1)S(1)}, u32[]{:S(2)}, u32[]{:S(2)}) collective-permute-start(bf16[64,2048]{1,0:T(8,128)(2,1)S(1)} %pad_maximum_fusion.17), channel_id=1, source_target_pairs={{0,1},{1,2},{2,3},{3,0},{4,5},{5,6},{6,7},{7,4},{8,9},{9,10},{10,1... | collective-permute-start | bytes 786440 | tf_op jit(solution)/shard_map/ppermute | solution.py:176
  476.9 8.7 %weight_grads.7 = (f32[8,704,2048]{2,1,0:T(8,128)}, f32[8,352,2048]{2,1,0:T(8,128)}, f32[8,128]{1,0:T(8,128)}) custom-call(bf16[8,256,2048]{2,1,0:T(8,128)(2,1)} %get-tuple-element.411.rows_ref, bf16[8,256,2048]{2,1,0:T(8,128)(2,1)} %get-tuple-element.265.grads_ref, ...), custom_call_target="tpu_custom_call", output_to_operand_aliasing={{0}: (4, {}), {1}: (5, {})} | custom-call | tf_op jit(solution)/shard_map/weight_grads/pallas_call | solution.py:495
  493.6 8.6 %collective-permute-done.113.refs_4_ = bf16[704,256]{1,0:T(8,128)(2,1)S(1)} collective-permute-done((bf16[704,256]{1,0:T(8,128)(2,1)}, bf16[704,256]{1,0:T(8,128)(2,1)S(1)}, u32[]{:S(2)}, u32[]{:S(2)}) %collective-permute-start.113) | collective-permute-done | bytes 360480 | tf_op jit(solution)/shard_map/ppermute | solution.py:100
  502.8 11.2 %collective-permute-done.111.refs_2_ = bf16[704,256]{1,0:T(8,128)(2,1)S(1)} collective-permute-done((bf16[704,256]{1,0:T(8,128)(2,1)}, bf16[704,256]{1,0:T(8,128)(2,1)S(1)}, u32[]{:S(2)}, u32[]{:S(2)}) %collective-permute-start.111) | collective-permute-done | bytes 360480 | tf_op jit(solution)/shard_map/ppermute | solution.py:100
  (583 shorter events, 325.6 us)
Async XLA Ops:
  13.7 46.9 %collective-permute-start = (bf16[256,1536]{1,0:T(8,128)(2,1)S(1)}, bf16[256,1536]{1,0:T(8,128)(2,1)}, u32[]{:S(2)}, u32[]{:S(2)}) collective-permute-start(bf16[256,1536]{1,0:T(8,128)(2,1)S(1)} %concatenate.126.refs_0_), channel_id=1, source_target_pairs={{4,0},{0,4},{12,8},{8,12},{20,16},{16,20},{28,24},{24,28},{5,1},{1... | collective-permute-start | bytes 2359304 | tf_op jit(solution)/shard_map/ppermute | solution.py:100
  35.9 24.1 %collective-permute-start.6 = (bf16[128,1536]{1,0:T(8,128)(2,1)S(1)}, bf16[128,1536]{1,0:T(8,128)(2,1)S(1)}, u32[]{:S(2)}, u32[]{:S(2)}) collective-permute-start(bf16[128,1536]{1,0:T(8,128)(2,1)S(1)} %slice.473), channel_id=1, source_target_pairs={{8,0},{12,4},{0,8},{4,12},{24,16},{28,20},{16,24},{20,28},{9,1},{1... | collective-permute-start | bytes 1179656 | tf_op jit(solution)/shard_map/ppermute | solution.py:100
  36.7 23.8 %collective-permute-start.5 = (bf16[128,1536]{1,0:T(8,128)(2,1)S(1)}, bf16[128,1536]{1,0:T(8,128)(2,1)S(1)}, u32[]{:S(2)}, u32[]{:S(2)}) collective-permute-start(bf16[128,1536]{1,0:T(8,128)(2,1)S(1)} %slice.472), channel_id=1, source_target_pairs={{16,0},{20,4},{24,8},{28,12},{0,16},{4,20},{8,24},{12,28},{17,1},{... | collective-permute-start | bytes 1179656 | tf_op jit(solution)/shard_map/ppermute | solution.py:100
  45.5 24.7 %collective-permute-start.4 = (bf16[256,1536]{1,0:T(8,128)(2,1)S(1)}, bf16[256,1536]{1,0:T(8,128)(2,1)S(1)}, u32[]{:S(2)}, u32[]{:S(2)}) collective-permute-start(bf16[256,1536]{1,0:T(8,128)(2,1)S(1)} %collective-permute-done.3.refs_4_), channel_id=1, source_target_pairs={{4,0},{0,4},{12,8},{8,12},{20,16},{16,20},{28,24},{24,28},{5,1},{1... | collective-permute-start | bytes 2359304 | tf_op jit(solution)/shard_map/ppermute | solution.py:100
  97.2 24.1 %collective-permute-start.30 = (bf16[256,2048]{1,0:T(8,128)(2,1)}, bf16[256,2048]{1,0:T(8,128)(2,1)S(1)}, u32[]{:S(2)}, u32[]{:S(2)}) collective-permute-start(bf16[256,2048]{1,0:T(8,128)(2,1)} %constant_dynamic-update-slice_fusion.4.refs_2_.refs_8_), channel_id=1, source_target_pairs={{16,0},{20,4},{24,8},{28,12},{0,16},{4,20},{8,24},{12,28},{17,1},{... | collective-permute-start | bytes 3145736 | tf_op jit(solution)/shard_map/ppermute | solution.py:100
  98.1 25.3 %collective-permute-start.29 = (bf16[256,2048]{1,0:T(8,128)(2,1)}, bf16[256,2048]{1,0:T(8,128)(2,1)S(1)}, u32[]{:S(2)}, u32[]{:S(2)}) collective-permute-start(bf16[256,2048]{1,0:T(8,128)(2,1)} %constant_dynamic-update-slice_fusion.4.refs_2_.refs_8_), channel_id=1, source_target_pairs={{8,0},{12,4},{0,8},{4,12},{24,16},{28,20},{16,24},{20,28},{9,1},{1... | collective-permute-start | bytes 3145736 | tf_op jit(solution)/shard_map/ppermute | solution.py:100
  115.5 26.6 %collective-permute-start.41 = (bf16[256,2048]{1,0:T(8,128)(2,1)}, bf16[256,2048]{1,0:T(8,128)(2,1)}, u32[]{:S(2)}, u32[]{:S(2)}) collective-permute-start(bf16[256,2048]{1,0:T(8,128)(2,1)} %constant_dynamic-update-slice_fusion.4.refs_2_.refs_8_), channel_id=1, source_target_pairs={{4,0},{0,4},{12,8},{8,12},{20,16},{16,20},{28,24},{24,28},{5,1},{1... | collective-permute-start | bytes 3145736 | tf_op jit(solution)/shard_map/ppermute | solution.py:100
  139.8 30.4 %collective-permute-start.43 = (bf16[256,2048]{1,0:T(8,128)(2,1)}, bf16[256,2048]{1,0:T(8,128)(2,1)S(1)}, u32[]{:S(2)}, u32[]{:S(2)}) collective-permute-start(bf16[256,2048]{1,0:T(8,128)(2,1)} %constant_dynamic-update-slice_fusion.57.refs_2_.refs_0_), channel_id=1, source_target_pairs={{16,0},{20,4},{24,8},{28,12},{0,16},{4,20},{8,24},{12,28},{17,1},{... | collective-permute-start | bytes 3145736 | tf_op jit(solution)/shard_map/ppermute | solution.py:100
  140.6 27.6 %collective-permute-start.36 = (bf16[256,2048]{1,0:T(8,128)(2,1)}, bf16[256,2048]{1,0:T(8,128)(2,1)S(1)}, u32[]{:S(2)}, u32[]{:S(2)}) collective-permute-start(bf16[256,2048]{1,0:T(8,128)(2,1)} %constant_dynamic-update-slice_fusion.57.refs_2_.refs_0_), channel_id=1, source_target_pairs={{8,0},{12,4},{0,8},{4,12},{24,16},{28,20},{16,24},{20,28},{9,1},{1... | collective-permute-start | bytes 3145736 | tf_op jit(solution)/shard_map/ppermute | solution.py:100
  157.1 25.4 %collective-permute-start.49 = (bf16[256,2048]{1,0:T(8,128)(2,1)}, bf16[256,2048]{1,0:T(8,128)(2,1)S(1)}, u32[]{:S(2)}, u32[]{:S(2)}) collective-permute-start(bf16[256,2048]{1,0:T(8,128)(2,1)} %constant_dynamic-update-slice_fusion.57.refs_2_.refs_0_), channel_id=1, source_target_pairs={{4,0},{0,4},{12,8},{8,12},{20,16},{16,20},{28,24},{24,28},{5,1},{1... | collective-permute-start | bytes 3145736 | tf_op jit(solution)/shard_map/ppermute | solution.py:100
  170.3 28.2 %collective-permute-start.47 = (bf16[256,2048]{1,0:T(8,128)(2,1)S(1)}, bf16[256,2048]{1,0:T(8,128)(2,1)S(1)}, u32[]{:S(2)}, u32[]{:S(2)}) collective-permute-start(bf16[256,2048]{1,0:T(8,128)(2,1)S(1)} %collective-permute-done.43.refs_2_.refs_4_), channel_id=1, source_target_pairs={{4,0},{0,4},{12,8},{8,12},{20,16},{16,20},{28,24},{24,28},{5,1},{1... | collective-permute-start | bytes 3145736 | tf_op jit(solution)/shard_map/ppermute | solution.py:100
  271.0 27.1 %collective-permute-start.57 = (bf16[256,2048]{1,0:T(8,128)(2,1)S(1)}, bf16[256,2048]{1,0:T(8,128)(2,1)S(1)}, u32[]{:S(2)}, u32[]{:S(2)}) collective-permute-start(bf16[256,2048]{1,0:T(8,128)(2,1)S(1)} %pad_maximum_fusion.1), channel_id=1, source_target_pairs={{0,16},{4,20},{8,24},{12,28},{16,0},{20,4},{24,8},{28,12},{1,17},{... | collective-permute-start | bytes 3145736 | tf_op jit(solution)/shard_map/ppermute | solution.py:104
  273.9 25.5 %collective-permute-start.56 = (bf16[256,2048]{1,0:T(8,128)(2,1)}, bf16[256,2048]{1,0:T(8,128)(2,1)S(1)}, u32[]{:S(2)}, u32[]{:S(2)}) collective-permute-start(bf16[256,2048]{1,0:T(8,128)(2,1)} %pad_maximum_fusion), channel_id=1, source_target_pairs={{0,8},{4,12},{8,0},{12,4},{16,24},{20,28},{24,16},{28,20},{1,9},{5... | collective-permute-start | bytes 3145736 | tf_op jit(solution)/shard_map/ppermute | solution.py:104
  274.5 24.9 %collective-permute-start.55 = (bf16[256,2048]{1,0:T(8,128)(2,1)}, bf16[256,2048]{1,0:T(8,128)(2,1)S(1)}, u32[]{:S(2)}, u32[]{:S(2)}) collective-permute-start(bf16[256,2048]{1,0:T(8,128)(2,1)} %get-tuple-element.312), channel_id=1, source_target_pairs={{0,4},{4,0},{8,12},{12,8},{16,20},{20,16},{24,28},{28,24},{1,5},{5... | collective-permute-start | bytes 3145736 | tf_op jit(solution)/shard_map/ppermute | solution.py:104
  343.2 30.1 %collective-permute-start.71 = (bf16[256,2048]{1,0:T(8,128)(2,1)}, bf16[256,2048]{1,0:T(8,128)(2,1)S(1)}, u32[]{:S(2)}, u32[]{:S(2)}) collective-permute-start(bf16[256,2048]{1,0:T(8,128)(2,1)} %pad_maximum_fusion.3), channel_id=1, source_target_pairs={{0,16},{4,20},{8,24},{12,28},{16,0},{20,4},{24,8},{28,12},{1,17},{... | collective-permute-start | bytes 3145736 | tf_op jit(solution)/shard_map/ppermute | solution.py:104
  343.8 31.0 %collective-permute-start.68 = (bf16[256,2048]{1,0:T(8,128)(2,1)S(1)}, bf16[256,2048]{1,0:T(8,128)(2,1)S(1)}, u32[]{:S(2)}, u32[]{:S(2)}) collective-permute-start(bf16[256,2048]{1,0:T(8,128)(2,1)S(1)} %pad_maximum_fusion.2), channel_id=1, source_target_pairs={{0,8},{4,12},{8,0},{12,4},{16,24},{20,28},{24,16},{28,20},{1,9},{5... | collective-permute-start | bytes 3145736 | tf_op jit(solution)/shard_map/ppermute | solution.py:104
  345.3 53.1 %collective-permute-start.60 = (bf16[256,2048]{1,0:T(8,128)(2,1)}, bf16[256,2048]{1,0:T(8,128)(2,1)S(1)}, u32[]{:S(2)}, u32[]{:S(2)}) collective-permute-start(bf16[256,2048]{1,0:T(8,128)(2,1)} %get-tuple-element.325), channel_id=1, source_target_pairs={{0,4},{4,0},{8,12},{12,8},{16,20},{20,16},{24,28},{28,24},{1,5},{5... | collective-permute-start | bytes 3145736 | tf_op jit(solution)/shard_map/ppermute | solution.py:104
  391.9 25.6 %collective-permute-start.88 = (bf16[704,256]{1,0:T(8,128)(2,1)}, bf16[704,256]{1,0:T(8,128)(2,1)S(1)}, u32[]{:S(2)}, u32[]{:S(2)}) collective-permute-start(bf16[704,256]{1,0:T(8,128)(2,1)} %get-tuple-element.378), channel_id=1, source_target_pairs={{0,4},{4,0},{8,12},{12,8},{16,20},{20,16},{24,28},{28,24},{1,5},{5... | collective-permute-start | bytes 1081352 | tf_op jit(solution)/shard_map/ppermute | solution.py:104
  455.7 35.2 %collective-permute-start.104 = (bf16[64,2048]{1,0:T(8,128)(2,1)S(1)}, bf16[64,2048]{1,0:T(8,128)(2,1)S(1)}, u32[]{:S(2)}, u32[]{:S(2)}) collective-permute-start(bf16[64,2048]{1,0:T(8,128)(2,1)S(1)} %pad_maximum_fusion.18), channel_id=1, source_target_pairs={{0,3},{1,0},{2,1},{3,2},{4,7},{5,4},{6,5},{7,6},{8,11},{9,8},{10,9... | collective-permute-start | bytes 786440 | tf_op jit(solution)/shard_map/ppermute | solution.py:176
  459.1 33.4 %collective-permute-start.95 = (bf16[64,2048]{1,0:T(8,128)(2,1)S(1)}, bf16[64,2048]{1,0:T(8,128)(2,1)S(1)}, u32[]{:S(2)}, u32[]{:S(2)}) collective-permute-start(bf16[64,2048]{1,0:T(8,128)(2,1)S(1)} %pad_maximum_fusion.17), channel_id=1, source_target_pairs={{0,1},{1,2},{2,3},{3,0},{4,5},{5,6},{6,7},{7,4},{8,9},{9,10},{10,1... | collective-permute-start | bytes 786440 | tf_op jit(solution)/shard_map/ppermute | solution.py:176
  485.7 45.2 %collective-permute-start.119 = (bf16[256,1536]{1,0:T(8,128)(2,1)}, bf16[256,1536]{1,0:T(8,128)(2,1)S(1)}, u32[]{:S(2)}, u32[]{:S(2)}) collective-permute-start(bf16[256,1536]{1,0:T(8,128)(2,1)} %get-tuple-element.428), channel_id=1, source_target_pairs={{0,4},{4,0},{8,12},{12,8},{16,20},{20,16},{24,28},{28,24},{1,5},{5... | collective-permute-start | bytes 2359304 | tf_op jit(solution)/shard_map/ppermute | solution.py:104
  485.8 45.5 %collective-permute-start.108 = (bf16[256,1536]{1,0:T(8,128)(2,1)S(1)}, bf16[256,1536]{1,0:T(8,128)(2,1)S(1)}, u32[]{:S(2)}, u32[]{:S(2)}) collective-permute-start(bf16[256,1536]{1,0:T(8,128)(2,1)S(1)} %pad_maximum_fusion.4), channel_id=1, source_target_pairs={{0,8},{4,12},{8,0},{12,4},{16,24},{20,28},{24,16},{28,20},{1,9},{5... | collective-permute-start | bytes 2359304 | tf_op jit(solution)/shard_map/ppermute | solution.py:104
  491.0 23.0 %collective-permute-start.111 = (bf16[704,256]{1,0:T(8,128)(2,1)}, bf16[704,256]{1,0:T(8,128)(2,1)S(1)}, u32[]{:S(2)}, u32[]{:S(2)}) collective-permute-start(bf16[704,256]{1,0:T(8,128)(2,1)} %join_depth.1.refs_0_), channel_id=1, source_target_pairs={{8,0},{12,4},{0,8},{4,12},{24,16},{28,20},{16,24},{20,28},{9,1},{1... | collective-permute-start | bytes 1081352 | tf_op jit(solution)/shard_map/ppermute | solution.py:100
  492.5 38.8 %collective-permute-start.109 = (bf16[256,1536]{1,0:T(8,128)(2,1)S(1)}, bf16[256,1536]{1,0:T(8,128)(2,1)S(1)}, u32[]{:S(2)}, u32[]{:S(2)}) collective-permute-start(bf16[256,1536]{1,0:T(8,128)(2,1)S(1)} %pad_maximum_fusion.5), channel_id=1, source_target_pairs={{0,16},{4,20},{8,24},{12,28},{16,0},{20,4},{24,8},{28,12},{1,17},{... | collective-permute-start | bytes 2359304 | tf_op jit(solution)/shard_map/ppermute | solution.py:104
  (184 other events, 2115.5 us)

commit v5 on v4

--- a/solution.py
+++ b/solution.py
@@ -159,6 +159,13 @@
         return pieces
 
     def reduce_parts(self, chunks):
+        own, first, marks = self.reduce_first(chunks)
+        return [own, *self.reduce_second(*marks)], first, marks
+
+    def reduce_second(self, to_x, to_y):
+        return self.send(to_x, (0, 1, 0)), self.send(to_y, (1, 0, 0))
+
+    def reduce_first(self, chunks):
         half = chunks[0].shape[0] // 2
         own = {}
         for place in (6, 2, 4, 0):
@@ -167,9 +174,7 @@
         second = self.send(own[6][half:], (1, 0, 0))
         to_y = jnp.concatenate([low_add(own[4][:half], first), own[4][half:]])
         to_x = jnp.concatenate([own[2][:half], low_add(own[2][half:], second)])
-        from_x = self.send(to_x, (0, 1, 0))
-        from_y = self.send(to_y, (1, 0, 0))
-        return [own[0], from_x, from_y], own[6], (to_x, to_y)
+        return own[0], own[6], (to_x, to_y)
 
     def ring(self, array, step):
         depth = self.depth
@@ -327,7 +332,8 @@
 
 def dispatch_grads_kernel(local, base_ref, *refs):
     routes, grads, shared_ref = refs[:2], refs[2:4], refs[4]
-    slot_ref, raw_ref = refs[-2:]
+    slot_ref, raw_ref, mark_ref = refs[-3:]
+    mark_ref[...] = jnp.zeros_like(mark_ref)
     for i in range(2):
 
         @pl.when(pl.program_id(0) == i)
@@ -523,10 +529,12 @@
         [
             pl.BlockSpec((local, SLOTS, width), lambda i, *_: (0, 2 * pair + i, 0)),
             pl.BlockSpec((1, units, count), lambda i, *_: (2 * pair + i, 0, 0)),
+            whole((8, LANES)),
         ],
         [
             jax.ShapeDtypeStruct((local, sequences * SLOTS, width), BF16),
             jax.ShapeDtypeStruct((sequences, units, count), F32),
+            jax.ShapeDtypeStruct((8, LANES), F32),
         ],
     )
 
@@ -820,22 +828,6 @@
         out_ref[at] = value[2 * padded : 2 * padded + units]
 
 
-def sum_split_kernel(depth_ref, own_ref, x_ref, y_ref, *outs):
-    size = outs[0].shape[0]
-    for k, out in enumerate(outs):
-        at = pl.ds(pl.multiple_of(depth_ref[k] * size, size), size)
-        out[...] = (
-            own_ref[at].astype(F32) + x_ref[at].astype(F32) + y_ref[at].astype(F32)
-        ).astype(BF16)
-
-
-def join_depth_kernel(depth_ref, *refs):
-    pieces, out_ref = refs[:-1], refs[-1]
-    size = pieces[0].shape[0]
-    for k, piece in enumerate(pieces):
-        out_ref[pl.ds(pl.multiple_of(depth_ref[k] * size, size), size)] = piece[...]
-
-
 def replicated_kernel(used, block_ref, *refs):
     chunks, latent_ref, router_ref, gains_ref = refs[:-3], refs[-3], refs[-2], refs[-1]
     columns = chunks[0].shape[1]
@@ -850,8 +842,8 @@
     return first * cosine - second * sine, first * sine + second * cosine
 
 
-def unit_rows(pieces):
-    values = jnp.concatenate([piece[...] for piece in pieces], axis=0).astype(F32)
+def unit_rows(pieces, width):
+    values = jnp.concatenate([piece[:, :width] for piece in pieces], axis=0).astype(F32)
     inverse = lax.rsqrt(jnp.mean(values * values, axis=-1, keepdims=True) + EPSILON)
     return values * inverse
 
@@ -867,7 +859,7 @@
         for j in range(LANES // half):
             start = KVR + i * LANES + j * half
             wide_ref[start : start + half] = piece
-    normed = (unit_rows(pieces) * gain_ref[...]).astype(BF16)
+    normed = (unit_rows(pieces, gain_ref.shape[1]) * gain_ref[...]).astype(BF16)
     normed_ref[...] = normed
     latent = dot_nt(normed, wide_ref[...])
     compressed = latent[:, :KVR]
@@ -1023,7 +1015,7 @@
     first, second = rope_turn(key_turn[:, :LANES], key_turn[:, LANES:], cosine, -sine)
     back_ref[:, KVR : KVR + LANES] = first.astype(BF16)
     back_ref[:, KVR + LANES :] = second.astype(BF16)
-    unit = unit_rows(tokens)
+    unit = unit_rows(tokens, normed_ref.shape[1])
     half = ROPE // 2
     for k, pack in enumerate(packs):
         start = pl.multiple_of(block_ref[k] * columns, columns)
@@ -1104,7 +1096,7 @@
 
 def latent_rows(pieces, gain, weight, kv_gain, cosine, sine):
     count = sum(piece.shape[0] for piece in pieces)
-    width = pieces[0].shape[1]
+    width = gain.shape[0]
     return vmem_call(
         functools.partial(latent_kernel, len(pieces)),
         "latent_rows",
@@ -1247,9 +1239,9 @@
     for m in pairs:
         at = slice(2 * m, 2 * m + 2)
         held = dispatch_grads(
-            m, sequences, local, base, routes[at], grads[at], shared_out, held
+            m, sequences, local, base, routes[at], grads[at], shared_out, held[:2]
         )
-    slot_grads, shared_raw = held
+    slot_grads, shared_raw, _ = held
     raw = expert_raw(slot_grads, expert_out)
     held = [None] * 6
     for m in pairs:
@@ -1525,12 +1517,15 @@
     heads = w_query.shape[1] // (NOPE + ROPE)
     own_depth = lax.axis_index("tensor")
     blocks = jnp.stack([grid.place_of(offset) for offset in grid.offsets]).astype(jnp.int32)
-    depths = ((own_depth + jnp.arange(depth)) % depth).astype(jnp.int32)
     base = (lax.axis_index("expert") * local).astype(jnp.int32)[None]
 
-    tokens = grid.ring_gather(tokens_in)
+    both = jnp.concatenate([tokens_in, out_grad], axis=1)
+    near = grid.ring_near(both)
     packs = grid.gather(pack_weights(w_query, w_keyval, w_output, heads))
-    group_grads = jnp.concatenate(grid.ring_gather(after(out_grad, packs[2], packs[4], *tokens)))
+    near = [after(piece, packs[2], packs[4]) for piece in near]
+    tokens = [both, near[0], *grid.ring_far(*near), near[1]]
+    group_grads = jnp.concatenate([piece[:, width:] for piece in tokens])
+
     position = (
         (own_depth + jnp.arange(row_count) // own_rows) % depth * own_rows
         + jnp.arange(row_count) % own_rows
@@ -1538,7 +1533,7 @@
     cosine, sine = (jnp.tile(table, (1, heads)) for table in rope_tables(position))
     bias = jnp.where(position[None, :] <= position[:, None], 0.0, -1e30).astype(F32)
     normed, compressed, low, key, latent_t = latent_rows(
-        tokens, attn_gain, w_latent.T, kv_gain, cosine, sine
+        [after(tokens[0], packs[6]), *tokens[1:]], attn_gain, w_latent.T, kv_gain, cosine, sine
     )
 
     units = w_shared_out.shape[0] // grid.experts
@@ -1573,50 +1568,59 @@
     )
 
     query, keyval, soft, attended, part = attention_forward(
-        heads, blocks, packs, after(normed, group_grads), low, key, bias, cosine, sine
-    )
-    part = after(part, *pieces)
-
-    middle = row_count // 2
-    group_grads = after(group_grads, part)
-    along_x = grid.fetch(group_grads, (0, 1, 0))
-    along_y = grid.fetch(group_grads, (1, 0, 0))
-    stream = tokens_in.astype(F32)
-    residual = stream + grid.ring_reduce(split_rows(part, depth))
-    normed_two, inverse_two = rms_forward(residual, ffn_gain)
-    normed_two = normed_two.astype(BF16)
-    near_rows = grid.ring_near(normed_two)
-    first = grid.fetch(along_x[:middle], (1, 0, 0))
-    second = grid.fetch(along_y[middle:], (0, 1, 0))
-    all_grads = [group_grads, grid.fetch(group_grads, (0, 0, 1))]
-    for held in (along_x, along_y):
-        all_grads += [held, grid.fetch(held, (0, 0, 1))]
-    near_rows = [after(piece, along_x, along_y) for piece in near_rows]
-    far_rows = grid.ring_far(*near_rows)
-    group_rows = jnp.concatenate([normed_two, near_rows[0], *far_rows, near_rows[1]])
-    group_rows = after(group_rows, first, second)
-    all_grads += [
-        jnp.concatenate([first, second]),
-        jnp.concatenate([grid.fetch(first, (0, 0, 1)), grid.fetch(second, (0, 0, 1))]),
-    ]
-
-    along_x = grid.fetch(group_rows, (0, 1, 0))
-    along_y = grid.fetch(group_rows, (1, 0, 0))
-    pair_rows = grid.fetch(group_rows, (0, 0, 1))
-    held = [None, None]
-    for m in pairs:
-        held = dispatch_grads(
+        heads, blocks, packs, normed, low, key, bias, cosine, sine
+    )
+
+    def slots(m, held, *earlier):
+        return dispatch_grads(
             m,
             sequences,
             local,
             base,
             routes_all[2 * m : 2 * m + 2],
             all_grads[2 * m : 2 * m + 2],
-            after(shared_out, group_rows),
-            held,
+            after(shared_out, *earlier),
+            held[:2],
         )
-    slot_grads, shared_raw = held
-    along_x, along_y = after(along_x, slot_grads), after(along_y, slot_grads)
+
+    middle = row_count // 2
+    group_grads = after(group_grads, part)
+    along_x = grid.fetch(group_grads, (0, 1, 0))
+    along_y = grid.fetch(group_grads, (1, 0, 0))
+    all_grads = [group_grads, grid.fetch(group_grads, (0, 0, 1))]
+    parts = split_rows(part, depth)
+    first, second = grid.ring_start(parts)
+    first, second = after(first, *pieces), after(second, *pieces)
+    ahead, behind, _ = grid.ring_finish(parts, first, second)
+    ahead, behind = after(ahead, side), after(behind, side)
+    stream = tokens_in.astype(F32)
+    residual = stream + sum(array.astype(F32) for array in (parts[0], ahead, behind))
+    normed_two, inverse_two = rms_forward(residual, ffn_gain)
+    normed_two = normed_two.astype(BF16)
+    near_rows = grid.ring_near(normed_two)
+    held = slots(0, [None, None], normed_two)
+    near_rows = [after(piece, held[2]) for piece in near_rows]
+    along_x, along_y = after(along_x, *near_rows), after(along_y, *near_rows)
+    first = grid.fetch(along_x[:middle], (1, 0, 0))
+    second = grid.fetch(along_y[middle:], (0, 1, 0))
+    for piece in (along_x, along_y):
+        all_grads += [piece, grid.fetch(piece, (0, 0, 1))]
+    far_rows = grid.ring_far(*near_rows)
+    held = slots(1, held, *near_rows)
+    far_rows = [after(piece, held[2]) for piece in far_rows]
+    group_rows = jnp.concatenate([normed_two, near_rows[0], *far_rows, near_rows[1]])
+    all_grads += [
+        jnp.concatenate([first, second]),
+        jnp.concatenate([grid.fetch(first, (0, 0, 1)), grid.fetch(second, (0, 0, 1))]),
+    ]
+
+    along_x = grid.fetch(group_rows, (0, 1, 0))
+    along_y = grid.fetch(group_rows, (1, 0, 0))
+    pair_rows = grid.fetch(group_rows, (0, 0, 1))
+    for m in pairs[2:]:
+        held = slots(m, held, group_rows)
+    slot_grads, shared_raw, mark = held
+    along_x, along_y = after(along_x, mark), after(along_y, mark)
     first = grid.fetch(along_x[:middle], (1, 0, 0))
     second = grid.fetch(along_y[middle:], (0, 1, 0))
     raw = expert_raw(after(slot_grads, along_x, along_y), w_expert_out)
@@ -1685,8 +1689,8 @@
     out_2, out_3 = outs(1, grad_group)
     first, second = after(first, out_2), after(second, out_2)
     ahead, behind, marks = grid.ring_finish(chunks, first, second)
-    out_0, out_1 = outs(0, *marks)
-    ahead, behind = after(ahead, out_0), after(behind, out_0)
+    out_0, out_1 = outs(0, *marks, out_own_6, out_own_4)
+    ahead, behind = after(ahead, out_0, out_first, out_second), after(behind, out_0)
     grad_normed = chunks[0].astype(F32) + ahead.astype(F32) + behind.astype(F32)
 
     grad_res_part, grad_ffn_gain = rms_backward(residual, inverse_two, ffn_gain, grad_normed)
@@ -1695,7 +1699,6 @@
     near_grads = grid.ring_near(grad_low)
     out_own_2 = low_add(out_2, grid.send(out_3, (0, 0, 1)))
     out_own_0 = low_add(out_0, grid.send(out_1, (0, 0, 1)))
-    out_first, out_second = after(out_first, *near_grads), after(out_second, *near_grads)
     out_to_y = jnp.concatenate([low_add(out_own_4[front], out_first), out_own_4[rear]])
     out_to_x = jnp.concatenate([out_own_2[front], low_add(out_own_2[rear], out_second)])
     out_from_x = grid.send(out_to_x, (0, 1, 0))
@@ -1704,10 +1707,11 @@
         blocks, base, rows, all_grads, after(logits[0], grad_low, out_to_x, out_to_y), shared_hidden, shared_back
     )
     out_from_x, out_from_y = after(out_from_x, grad_router), after(out_from_y, grad_router)
+    near_grads = [after(piece, grad_router) for piece in near_grads]
     far_grads = grid.ring_far(*near_grads)
-    grads = [grad_low, near_grads[0], *(after(piece, grad_router) for piece in far_grads), near_grads[1]]
-
-    returned = grid.exchange(grad_parts)
+    grads = [grad_low, near_grads[0], *far_grads, near_grads[1]]
+
+    returned = grid.exchange([after(piece, *near_grads) for piece in grad_parts])
     grads[0] = after(grads[0], out_from_x, out_from_y)
     grad_query, grad_keyval, grad_normed_one, *chunks = attention_backward(
         heads,
@@ -1765,35 +1769,23 @@
     held = weights(1, held, held[2], *chunk_mark)
     mark = held[2]
     marks.append(mark)
-    size = CHUNK_ROWS // depth
     columns = width // grid.experts
-    parts = vmem_call(
-        sum_split_kernel,
-        "sum_split",
-        depths,
-        [sums[0], after(sums[1], mark), after(sums[2], mark)],
-        [jax.ShapeDtypeStruct((size, columns), BF16)] * depth,
-        [],
-    )
-    pack_sums, pack_first, pack_mark = grid.reduce_parts([after(pack, mark) for pack in grad_packs])
-    held = weights(2, held, parts[0], pack_first)
+    chunk = sum(a.astype(F32) for a in (sums[0], after(sums[1], mark), after(sums[2], mark)))
+    chunk = chunk.astype(BF16)
+    pack_own, pack_first, pack_mark = grid.reduce_first([after(pack, mark) for pack in grad_packs])
+    flip = [(i, i ^ 1) for i in range(depth)]
+    other = lax.ppermute(chunk, "tensor", flip)
+    held = weights(2, held, chunk, pack_first)
     marks.append(held[2])
-    part = grid.reduce_depth([parts[0]] + [after(part, pack_first) for part in parts[1:]])
-    part = after(part, held[2]).astype(BF16)
-    *held, mark = weights(3, held, part, *pack_mark)
+    chunk = (chunk.astype(F32) + other.astype(F32) + held[2][:1, :1]).astype(BF16)
+    flip = [(i, i ^ 2) for i in range(depth)]
+    other = lax.ppermute(chunk, "tensor", flip)
+    *held, mark = weights(3, held, chunk, *pack_mark)
     grad_expert_in, grad_expert_out = held
     marks.append(mark)
     block_out = (residual + ring_rounds(out_group, *marks[:3])).astype(BF16)
     grad_normed_one = ring_rounds(grad_normed_one, *marks[1:])
-    parts = [after(piece, mark) for piece in grid.gather_depth(part)]
-    (chunk,) = vmem_call(
-        join_depth_kernel,
-        "join_depth",
-        depths,
-        parts,
-        [jax.ShapeDtypeStruct((CHUNK_ROWS, columns), BF16)],
-        [],
-    )
+    chunk = (chunk.astype(F32) + other.astype(F32) + mark[:1, :1]).astype(BF16)
     sum_shared_in, sum_shared_out = vmem_call(
         functools.partial(join_rows_kernel, units),
         "join_rows",
@@ -1806,7 +1798,9 @@
         [],
     )
     gathered = grid.gather(chunk)
-    gathered[0] = after(gathered[0], sum_shared_out, *pack_sums[1:])
+    pack_mark = [after(part, gathered[2], gathered[4]) for part in pack_mark]
+    pack_sums = [pack_own, *grid.reduce_second(*pack_mark)]
+    gathered[0] = after(gathered[0], sum_shared_out)
     sum_latent, sum_router, sum_gains = vmem_call(
         functools.partial(replicated_kernel, KVR + ROPE),
         "replicated",

time: 554 us -> 538 us (0.971)
  starting transfers between devices: 129 us -> 104 us
  waiting for transfers between devices: 107 us -> 123 us
    ppermute x32 -> x28, starting transfers between devices: 58.6 us -> 43.2 us  [ring(): lax.ppermute(array, 'tensor', [(i, (i + step) % depth) for i in range(dep...]
    ppermute x6 -> x2, starting transfers between devices: 13.8 us -> 1.35 us  [square_device(): other = lax.ppermute(chunk, 'tensor', flip)]
    ppermute x46, waiting for transfers between devices: 19.2 us -> 31.4 us  [send(): return lax.ppermute(array, 'expert', pairs)]
    ppermute x32 -> x28, waiting for transfers between devices: 52.5 us -> 40.4 us  [ring(): lax.ppermute(array, 'tensor', [(i, (i + step) % depth) for i in range(dep...]
    ppermute x36, waiting for transfers between devices: 34 us -> 44.2 us  [fetch(): return lax.ppermute(array, 'expert', pairs)]
    ppermute x6 -> x2, waiting for transfers between devices: 1.3 us -> 7.3 us  [square_device(): other = lax.ppermute(chunk, 'tensor', flip)]
    pallas_call x8 -> x6, Pallas kernels: 46.5 us -> 42 us  [vmem_call(): pl.pallas_call(kernel, grid_spec=pltpu.PrefetchScalarGridSpec(num_scalar_...]
    unnamed x199 -> x208, local copies, waits for them, and re-layouts: 20.2 us -> 17.2 us
  transfers between devices with their start and end apart: 120 -> 112, of which waited for: 33 -> 33; matrix products, arithmetic and copies ran while one was open for 9% -> 8% of each run, Pallas kernels for 34% -> 35%
where the time goes in v5:
time: 538 us; the launch traced here: 527 us
  Pallas kernels  235 us (44%)
  waiting for transfers between devices  123 us (23%)
  starting transfers between devices  104 us (19%)
  local copies, waits for them, and re-layouts  37.6 us (7%)
  other arithmetic  24.2 us (4%)
    pallas_call x16, Pallas kernels, chain_call(): pl.pallas_call(kernel, grid_spec=pltpu.PrefetchScalarGridSpec(num_scalar_...  98.8 us
    ppermute x36, waiting for transfers between devices, fetch(): return lax.ppermute(array, 'expert', pairs)  44.2 us
    ppermute x28, starting transfers between devices, ring(): lax.ppermute(array, 'tensor', [(i, (i + step) % depth) for i in range(dep...  43.2 us
    pallas_call x6, Pallas kernels, vmem_call(): pl.pallas_call(kernel, grid_spec=pltpu.PrefetchScalarGridSpec(num_scalar_...  42 us
    ppermute x28, waiting for transfers between devices, ring(): lax.ppermute(array, 'tensor', [(i, (i + step) % depth) for i in range(dep...  40.4 us
    ppermute x46, starting transfers between devices, send(): return lax.ppermute(array, 'expert', pairs)  33.7 us
    ppermute x46, waiting for transfers between devices, send(): return lax.ppermute(array, 'expert', pairs)  31.4 us
    pallas_call x1, Pallas kernels, expert_rows(): pl.pallas_call(functools.partial(expert_kernel, units), grid=(local, slot...  31.2 us
  transfers between devices with their start and end apart: 112, of which 33 were waited for; matrix products, arithmetic and copies ran while one was open for 8% of the time, Pallas kernels for 35%

profile of v5, /device:TPU:0, one launch (start us, length us, event | category | flops | bytes accessed | tf_op | source)
XLA Modules:
  0.0 527.4 jit_solution(954495534137933287)
XLA Ops:
  32.1 7.4 %collective-permute-done.9.refs_1_.refs_9_ = bf16[64,4096]{1,0:T(8,128)(2,1)} collective-permute-done((bf16[64,4096]{1,0:T(8,128)(2,1)}, bf16[64,4096]{1,0:T(8,128)(2,1)}, u32[]{:S(2)}, u32[]{:S(2)}) %collective-permute-start.9) | collective-permute-done | bytes 524320 | tf_op jit(solution)/shard_map/ppermute | solution.py:181
  63.3 9.2 %attention_forward.1 = (bf16[256,768]{1,0:T(8,128)(2,1)}, bf16[256,1024]{1,0:T(8,128)(2,1)}, f32[4,256,256]{2,1,0:T(8,128)}, bf16[256,512]{1,0:T(8,128)(2,1)}, bf16[256,2048]{1,0:T(8,128)(2,1)}) custom-call(s32[8]{0:T(128)} %stack.35.block_ref, bf16[256,1536]{1,0:T(8,128)(2,1)} %copy-done, bf16[256,1536]{1,0:T(8,128)(2,1)} %collective-permute-done.refs_1_, ...), custom_call_target="tpu_custom_call" | custom-call | tf_op jit(solution)/shard_map/attention_forward/pallas_call | solution.py:1082
  119.4 10.6 %collective-permute-done.33.refs_2_.refs_12_ = bf16[256,2048]{1,0:T(8,128)(2,1)S(1)} collective-permute-done((bf16[256,2048]{1,0:T(8,128)(2,1)S(1)}, bf16[256,2048]{1,0:T(8,128)(2,1)S(1)}, u32[]{:S(2)}, u32[]{:S(2)}) %collective-permute-start.33) | collective-permute-done | bytes 1048608 | tf_op jit(solution)/shard_map/ppermute | solution.py:100
  163.5 6.8 %collective-permute-done.31.refs_2_ = bf16[256,2048]{1,0:T(8,128)(2,1)S(1)} collective-permute-done((bf16[256,2048]{1,0:T(8,128)(2,1)S(1)}, bf16[256,2048]{1,0:T(8,128)(2,1)S(1)}, u32[]{:S(2)}, u32[]{:S(2)}) %collective-permute-start.31) | collective-permute-done | bytes 1048608 | tf_op jit(solution)/shard_map/ppermute | solution.py:100
  176.7 11.5 %expert_raw.1.raw_ref = f32[8,352,256]{2,1,0:T(8,128)} custom-call(bf16[8,256,2048]{2,1,0:T(8,128)(2,1)} %get-tuple-element.286.grads_ref, bf16[8,352,2048]{2,1,0:T(8,128)(2,1)} %out_ref.3), custom_call_target="tpu_custom_call" | custom-call | tf_op jit(solution)/shard_map/expert_raw/pallas_call | solution.py:593
  213.6 31.2 %expert_rows.1 = (bf16[8,256,2048]{2,1,0:T(8,128)(2,1)}, bf16[8,256,128]{2,1,0:T(8,128)(2,1)}, bf16[8,352,256]{2,1,0:T(8,128)(2,1)}, bf16[8,704,256]{2,1,0:T(8,128)(2,1)}) custom-call(bf16[8,256,2048]{2,1,0:T(8,128)(2,1)} %get-tuple-element.429.rows_ref, bf16[8,256,128]{2,1,0:T(8,128)(2,1)} %get-tuple-element.310.info_ref, bf16[8,704,2048]{2,1,0:T(8,128)(2,1)} %bitcast.105, ...), custom_call_target="tpu_custom_call" | custom-call | tf_op jit(solution)/shard_map/expert_rows/pallas_call | solution.py:608
  244.8 6.1 %combine_back.4 = (bf16[8,64,256]{2,1,0:T(8,128)(2,1)}, bf16[256,2048]{1,0:T(8,128)(2,1)}, bf16[256,2048]{1,0:T(8,128)(2,1)}) custom-call(bf16[8,256,256]{2,1,0:T(8,128)(2,1)} %get-tuple-element.308.refs_0_.pick_ref, bf16[8,256,2048]{2,1,0:T(8,128)(2,1)} %get-tuple-element.318.refs_1_, bf16[8,256,128]{2,1,0:T(8,128)(2,1)} %get-tuple-element.313.refs_2_, ...), custom_call_target="tpu_custom_call" | custom-call | tf_op jit(solution)/shard_map/combine_back/pallas_call | solution.py:501
  251.2 6.2 %combine_back.5 = (bf16[8,64,256]{2,1,0:T(8,128)(2,1)}, bf16[256,2048]{1,0:T(8,128)(2,1)}, bf16[256,2048]{1,0:T(8,128)(2,1)}) custom-call(bf16[8,256,256]{2,1,0:T(8,128)(2,1)} %get-tuple-element.308.refs_0_.pick_ref, bf16[8,256,2048]{2,1,0:T(8,128)(2,1)} %get-tuple-element.318.refs_1_, ...), custom_call_target="tpu_custom_call", output_to_operand_aliasing={{0}: (6, {})} | custom-call | tf_op jit(solution)/shard_map/combine_back/pallas_call | solution.py:501
  260.3 6.1 %combine_back.6 = (bf16[8,64,256]{2,1,0:T(8,128)(2,1)}, bf16[256,2048]{1,0:T(8,128)(2,1)}, bf16[256,2048]{1,0:T(8,128)(2,1)}) custom-call(bf16[8,256,256]{2,1,0:T(8,128)(2,1)} %get-tuple-element.308.refs_0_.pick_ref, bf16[8,256,2048]{2,1,0:T(8,128)(2,1)} %get-tuple-element.318.refs_1_, ...), custom_call_target="tpu_custom_call", output_to_operand_aliasing={{0}: (6, {})} | custom-call | tf_op jit(solution)/shard_map/combine_back/pallas_call | solution.py:501
  266.9 6.1 %combine_back.7 = (bf16[8,64,256]{2,1,0:T(8,128)(2,1)}, bf16[256,2048]{1,0:T(8,128)(2,1)}, bf16[256,2048]{1,0:T(8,128)(2,1)}) custom-call(bf16[8,256,256]{2,1,0:T(8,128)(2,1)} %get-tuple-element.308.refs_0_.pick_ref, bf16[8,256,2048]{2,1,0:T(8,128)(2,1)} %get-tuple-element.318.refs_1_, ...), custom_call_target="tpu_custom_call", output_to_operand_aliasing={{0}: (6, {})} | custom-call | tf_op jit(solution)/shard_map/combine_back/pallas_call | solution.py:501
  276.8 12.7 %expert_out_rows.1.slots_ref = bf16[8,256,2048]{2,1,0:T(8,128)(2,1)} custom-call(bf16[8,352,256]{2,1,0:T(8,128)(2,1)} %get-tuple-element.331.hidden_ref, bf16[8,352,2048]{2,1,0:T(8,128)(2,1)} %out_ref.3), custom_call_target="tpu_custom_call" | custom-call | tf_op jit(solution)/shard_map/expert_out_rows/pallas_call | solution.py:638
  322.9 6.7 %collective-permute-done.63 = bf16[128,2048]{1,0:T(8,128)(2,1)} collective-permute-done((bf16[128,2048]{1,0:T(8,128)(2,1)S(1)}, bf16[128,2048]{1,0:T(8,128)(2,1)}, u32[]{:S(2)}, u32[]{:S(2)}) %collective-permute-start.63) | collective-permute-done | bytes 524320 | tf_op jit(solution)/shard_map/ppermute | solution.py:104
  340.0 11.8 %side_grads.1 = (bf16[288,256]{1,0:T(8,128)(2,1)}, bf16[288,256]{1,0:T(8,128)(2,1)}, bf16[288,256]{1,0:T(8,128)(2,1)}, bf16[288,256]{1,0:T(8,128)(2,1)}, bf16[28...) custom-call(s32[8]{0:T(128)} %stack.35.block_ref, ...), custom_call_target="tpu_custom_call" | custom-call | tf_op jit(solution)/shard_map/side_grads/pallas_call | solution.py:783
  352.0 7.9 %collective-permute-done.69.refs_16_.refs_3_ = bf16[32,2048]{1,0:T(8,128)(2,1)S(1)} collective-permute-done((bf16[32,2048]{1,0:T(8,128)(2,1)S(1)}, bf16[32,2048]{1,0:T(8,128)(2,1)S(1)}, u32[]{:S(2)}, u32[]{:S(2)}) %collective-permute-start.69) | collective-permute-done | bytes 131104 | tf_op jit(solution)/shard_map/ppermute | solution.py:181
  365.6 6.4 %collective-permute-done.71.refs_2_ = bf16[288,256]{1,0:T(8,128)(2,1)S(1)} collective-permute-done((bf16[288,256]{1,0:T(8,128)(2,1)}, bf16[288,256]{1,0:T(8,128)(2,1)S(1)}, u32[]{:S(2)}, u32[]{:S(2)}) %collective-permute-start.71) | collective-permute-done | bytes 147488 | tf_op jit(solution)/shard_map/ppermute | solution.py:104
  376.3 14.6 %attention_backward.1 = (bf16[256,768]{1,0:T(8,128)(2,1)}, bf16[256,1024]{1,0:T(8,128)(2,1)}, bf16[256,2048]{1,0:T(8,128)(2,1)}, bf16[704,256]{1,0:T(8,128)(2,1)...) custom-call(s32[8]{0:T(128)} %stack.35.block_ref, ...), custom_call_target="tpu_custom_call" | custom-call | tf_op jit(solution)/shard_map/attention_backward/pallas_call | solution.py:1082
  392.7 6.3 %attention_weights.1 = (bf16[256,1536]{1,0:T(8,128)(2,1)}, bf16[256,1536]{1,0:T(8,128)(2,1)}, bf16[256,1536]{1,0:T(8,128)(2,1)}, bf16[256,1536]{1,0:T(8,128)(2,1...) custom-call(s32[8]{0:T(128)} %stack.35.block_ref, ...), custom_call_target="tpu_custom_call" | custom-call | tf_op jit(solution)/shard_map/attention_weights/pallas_call | solution.py:1082
  402.0 8.7 %weight_grads.4 = (f32[8,704,2048]{2,1,0:T(8,128)}, f32[8,352,2048]{2,1,0:T(8,128)}, f32[8,128]{1,0:T(8,128)}) custom-call(bf16[8,256,2048]{2,1,0:T(8,128)(2,1)} %get-tuple-element.429.rows_ref, bf16[8,256,2048]{2,1,0:T(8,128)(2,1)} %get-tuple-element.286.grads_ref, bf16[8,352,256]{2,1,0:T(8,128)(2,1)} %get-tuple-element.331.hidden_ref, ...), custom_call_target="tpu_custom_call" | custom-call | tf_op jit(solution)/shard_map/weight_grads/pallas_call | solution.py:501
  417.6 8.8 %weight_grads.5 = (f32[8,704,2048]{2,1,0:T(8,128)}, f32[8,352,2048]{2,1,0:T(8,128)}, f32[8,128]{1,0:T(8,128)}) custom-call(bf16[8,256,2048]{2,1,0:T(8,128)(2,1)} %get-tuple-element.429.rows_ref, bf16[8,256,2048]{2,1,0:T(8,128)(2,1)} %get-tuple-element.286.grads_ref, ...), custom_call_target="tpu_custom_call", output_to_operand_aliasing={{0}: (4, {}), {1}: (5, {})} | custom-call | tf_op jit(solution)/shard_map/weight_grads/pallas_call | solution.py:501
  433.1 8.7 %weight_grads.6 = (f32[8,704,2048]{2,1,0:T(8,128)}, f32[8,352,2048]{2,1,0:T(8,128)}, f32[8,128]{1,0:T(8,128)}) custom-call(bf16[8,256,2048]{2,1,0:T(8,128)(2,1)} %get-tuple-element.429.rows_ref, bf16[8,256,2048]{2,1,0:T(8,128)(2,1)} %get-tuple-element.286.grads_ref, ...), custom_call_target="tpu_custom_call", output_to_operand_aliasing={{0}: (4, {}), {1}: (5, {})} | custom-call | tf_op jit(solution)/shard_map/weight_grads/pallas_call | solution.py:501
  460.8 6.6 %collective-permute-done.94 = bf16[128,1536]{1,0:T(8,128)(2,1)S(1)} collective-permute-done((bf16[128,1536]{1,0:T(8,128)(2,1)S(1)}, bf16[128,1536]{1,0:T(8,128)(2,1)S(1)}, u32[]{:S(2)}, u32[]{:S(2)}) %collective-permute-start.94) | collective-permute-done | bytes 393248 | tf_op jit(solution)/shard_map/ppermute | solution.py:104
  467.8 8.7 %weight_grads.7 = (f32[8,704,2048]{2,1,0:T(8,128)}, f32[8,352,2048]{2,1,0:T(8,128)}, f32[8,128]{1,0:T(8,128)}) custom-call(bf16[8,256,2048]{2,1,0:T(8,128)(2,1)} %get-tuple-element.429.rows_ref, bf16[8,256,2048]{2,1,0:T(8,128)(2,1)} %get-tuple-element.286.grads_ref, ...), custom_call_target="tpu_custom_call", output_to_operand_aliasing={{0}: (4, {}), {1}: (5, {})} | custom-call | tf_op jit(solution)/shard_map/weight_grads/pallas_call | solution.py:501
  483.2 7.4 %collective-permute-done.103.refs_4_ = bf16[704,256]{1,0:T(8,128)(2,1)S(1)} collective-permute-done((bf16[704,256]{1,0:T(8,128)(2,1)S(1)}, bf16[704,256]{1,0:T(8,128)(2,1)S(1)}, u32[]{:S(2)}, u32[]{:S(2)}) %collective-permute-start.103) | collective-permute-done | bytes 360480 | tf_op jit(solution)/shard_map/ppermute | solution.py:100
  515.5 6.9 %collective-permute-done.110 = bf16[256,1536]{1,0:T(8,128)(2,1)S(1)} collective-permute-done((bf16[256,1536]{1,0:T(8,128)(2,1)S(1)}, bf16[256,1536]{1,0:T(8,128)(2,1)S(1)}, u32[]{:S(2)}, u32[]{:S(2)}) %collective-permute-start.110) | collective-permute-done | bytes 786464 | tf_op jit(solution)/shard_map/ppermute | solution.py:104
  (573 shorter events, 300.8 us)
Async XLA Ops:
  5.3 20.6 %collective-permute-start.3 = (bf16[256,1536]{1,0:T(8,128)(2,1)S(1)}, bf16[256,1536]{1,0:T(8,128)(2,1)S(1)}, u32[]{:S(2)}, u32[]{:S(2)}) collective-permute-start(bf16[256,1536]{1,0:T(8,128)(2,1)S(1)} %concatenate.129.refs_0_), channel_id=1, source_target_pairs={{16,0},{20,4},{24,8},{28,12},{0,16},{4,20},{8,24},{12,28},{17,1},{... | collective-permute-start | bytes 2359304 | tf_op jit(solution)/shard_map/ppermute | solution.py:100
  9.9 50.4 %collective-permute-start = (bf16[256,1536]{1,0:T(8,128)(2,1)S(1)}, bf16[256,1536]{1,0:T(8,128)(2,1)}, u32[]{:S(2)}, u32[]{:S(2)}) collective-permute-start(bf16[256,1536]{1,0:T(8,128)(2,1)S(1)} %concatenate.129.refs_0_), channel_id=1, source_target_pairs={{4,0},{0,4},{12,8},{8,12},{20,16},{16,20},{28,24},{24,28},{5,1},{1... | collective-permute-start | bytes 2359304 | tf_op jit(solution)/shard_map/ppermute | solution.py:100
  13.9 25.6 %collective-permute-start.9 = (bf16[64,4096]{1,0:T(8,128)(2,1)}, bf16[64,4096]{1,0:T(8,128)(2,1)}, u32[]{:S(2)}, u32[]{:S(2)}) collective-permute-start(bf16[64,4096]{1,0:T(8,128)(2,1)} %get-tuple-element.232.refs_0_.refs_8_), channel_id=1, source_target_pairs={{0,3},{1,0},{2,1},{3,2},{4,7},{5,4},{6,5},{7,6},{8,11},{9,8},{10,9... | collective-permute-start | bytes 1572872 | tf_op jit(solution)/shard_map/ppermute | solution.py:181
  26.0 27.0 %collective-permute-start.6 = (bf16[128,1536]{1,0:T(8,128)(2,1)S(1)}, bf16[128,1536]{1,0:T(8,128)(2,1)S(1)}, u32[]{:S(2)}, u32[]{:S(2)}) collective-permute-start(bf16[128,1536]{1,0:T(8,128)(2,1)S(1)} %slice.489), channel_id=1, source_target_pairs={{8,0},{12,4},{0,8},{4,12},{24,16},{28,20},{16,24},{20,28},{9,1},{1... | collective-permute-start | bytes 1179656 | tf_op jit(solution)/shard_map/ppermute | solution.py:100
  27.9 25.1 %collective-permute-start.5 = (bf16[128,1536]{1,0:T(8,128)(2,1)S(1)}, bf16[128,1536]{1,0:T(8,128)(2,1)S(1)}, u32[]{:S(2)}, u32[]{:S(2)}) collective-permute-start(bf16[128,1536]{1,0:T(8,128)(2,1)S(1)} %slice.488), channel_id=1, source_target_pairs={{16,0},{20,4},{24,8},{28,12},{0,16},{4,20},{8,24},{12,28},{17,1},{... | collective-permute-start | bytes 1179656 | tf_op jit(solution)/shard_map/ppermute | solution.py:100
  30.4 21.9 %collective-permute-start.12 = (bf16[32,4096]{1,0:T(8,128)(2,1)S(1)}, bf16[32,4096]{1,0:T(8,128)(2,1)S(1)}, u32[]{:S(2)}, u32[]{:S(2)}) collective-permute-start(bf16[32,4096]{1,0:T(8,128)(2,1)S(1)} %slice.396), channel_id=1, source_target_pairs={{0,1},{1,2},{2,3},{3,0},{4,5},{5,6},{6,7},{7,4},{8,9},{9,10},{10,1... | collective-permute-start | bytes 786440 | tf_op jit(solution)/shard_map/ppermute | solution.py:181
  94.0 24.4 %collective-permute-start.27 = (bf16[256,2048]{1,0:T(8,128)(2,1)S(1)}, bf16[256,2048]{1,0:T(8,128)(2,1)S(1)}, u32[]{:S(2)}, u32[]{:S(2)}) collective-permute-start(bf16[256,2048]{1,0:T(8,128)(2,1)S(1)} %slice_dynamic-update-slice_fusion.refs_2_.refs_8_), channel_id=1, source_target_pairs={{8,0},{12,4},{0,8},{4,12},{24,16},{28,20},{16,24},{20,28},{9,1},{1... | collective-permute-start | bytes 3145736 | tf_op jit(solution)/shard_map/ppermute | solution.py:100
  106.7 23.3 %collective-permute-start.33 = (bf16[256,2048]{1,0:T(8,128)(2,1)S(1)}, bf16[256,2048]{1,0:T(8,128)(2,1)S(1)}, u32[]{:S(2)}, u32[]{:S(2)}) collective-permute-start(bf16[256,2048]{1,0:T(8,128)(2,1)S(1)} %slice_dynamic-update-slice_fusion.refs_2_.refs_8_), channel_id=1, source_target_pairs={{16,0},{20,4},{24,8},{28,12},{0,16},{4,20},{8,24},{12,28},{17,1},{... | collective-permute-start | bytes 3145736 | tf_op jit(solution)/shard_map/ppermute | solution.py:100
  130.0 21.6 %collective-permute-start.37 = (bf16[256,2048]{1,0:T(8,128)(2,1)S(1)}, bf16[256,2048]{1,0:T(8,128)(2,1)S(1)}, u32[]{:S(2)}, u32[]{:S(2)}) collective-permute-start(bf16[256,2048]{1,0:T(8,128)(2,1)S(1)} %collective-permute-done.33.refs_2_.refs_12_), channel_id=1, source_target_pairs={{4,0},{0,4},{12,8},{8,12},{20,16},{16,20},{28,24},{24,28},{5,1},{1... | collective-permute-start | bytes 3145736 | tf_op jit(solution)/shard_map/ppermute | solution.py:100
  140.9 29.4 %collective-permute-start.31 = (bf16[256,2048]{1,0:T(8,128)(2,1)S(1)}, bf16[256,2048]{1,0:T(8,128)(2,1)S(1)}, u32[]{:S(2)}, u32[]{:S(2)}) collective-permute-start(bf16[256,2048]{1,0:T(8,128)(2,1)S(1)} %constant_dynamic-update-slice_fusion.57.refs_2_.refs_0_), channel_id=1, source_target_pairs={{8,0},{12,4},{0,8},{4,12},{24,16},{28,20},{16,24},{20,28},{9,1},{1... | collective-permute-start | bytes 3145736 | tf_op jit(solution)/shard_map/ppermute | solution.py:100
  148.5 26.0 %collective-permute-start.39 = (bf16[256,2048]{1,0:T(8,128)(2,1)S(1)}, bf16[256,2048]{1,0:T(8,128)(2,1)S(1)}, u32[]{:S(2)}, u32[]{:S(2)}) collective-permute-start(bf16[256,2048]{1,0:T(8,128)(2,1)S(1)} %constant_dynamic-update-slice_fusion.57.refs_2_.refs_0_), channel_id=1, source_target_pairs={{16,0},{20,4},{24,8},{28,12},{0,16},{4,20},{8,24},{12,28},{17,1},{... | collective-permute-start | bytes 3145736 | tf_op jit(solution)/shard_map/ppermute | solution.py:100
  151.7 36.7 %collective-permute-start.45 = (bf16[256,2048]{1,0:T(8,128)(2,1)S(1)}, bf16[256,2048]{1,0:T(8,128)(2,1)}, u32[]{:S(2)}, u32[]{:S(2)}) collective-permute-start(bf16[256,2048]{1,0:T(8,128)(2,1)S(1)} %constant_dynamic-update-slice_fusion.57.refs_2_.refs_0_), channel_id=1, source_target_pairs={{4,0},{0,4},{12,8},{8,12},{20,16},{16,20},{28,24},{24,28},{5,1},{1... | collective-permute-start | bytes 3145736 | tf_op jit(solution)/shard_map/ppermute | solution.py:100
  176.2 26.1 %collective-permute-start.43 = (bf16[256,2048]{1,0:T(8,128)(2,1)S(1)}, bf16[256,2048]{1,0:T(8,128)(2,1)}, u32[]{:S(2)}, u32[]{:S(2)}) collective-permute-start(bf16[256,2048]{1,0:T(8,128)(2,1)S(1)} %collective-permute-done.39.refs_2_.refs_4_), channel_id=1, source_target_pairs={{4,0},{0,4},{12,8},{8,12},{20,16},{16,20},{28,24},{24,28},{5,1},{1... | collective-permute-start | bytes 3145736 | tf_op jit(solution)/shard_map/ppermute | solution.py:100
  273.3 26.6 %collective-permute-start.53 = (bf16[256,2048]{1,0:T(8,128)(2,1)S(1)}, bf16[256,2048]{1,0:T(8,128)(2,1)S(1)}, u32[]{:S(2)}, u32[]{:S(2)}) collective-permute-start(bf16[256,2048]{1,0:T(8,128)(2,1)S(1)} %pad_maximum_fusion.1), channel_id=1, source_target_pairs={{0,16},{4,20},{8,24},{12,28},{16,0},{20,4},{24,8},{28,12},{1,17},{... | collective-permute-start | bytes 3145736 | tf_op jit(solution)/shard_map/ppermute | solution.py:104
  275.2 25.3 %collective-permute-start.52 = (bf16[256,2048]{1,0:T(8,128)(2,1)S(1)}, bf16[256,2048]{1,0:T(8,128)(2,1)S(1)}, u32[]{:S(2)}, u32[]{:S(2)}) collective-permute-start(bf16[256,2048]{1,0:T(8,128)(2,1)S(1)} %pad_maximum_fusion), channel_id=1, source_target_pairs={{0,8},{4,12},{8,0},{12,4},{16,24},{20,28},{24,16},{28,20},{1,9},{5... | collective-permute-start | bytes 3145736 | tf_op jit(solution)/shard_map/ppermute | solution.py:104
  276.8 23.8 %collective-permute-start.51 = (bf16[256,2048]{1,0:T(8,128)(2,1)}, bf16[256,2048]{1,0:T(8,128)(2,1)S(1)}, u32[]{:S(2)}, u32[]{:S(2)}) collective-permute-start(bf16[256,2048]{1,0:T(8,128)(2,1)} %get-tuple-element.332), channel_id=1, source_target_pairs={{0,4},{4,0},{8,12},{12,8},{16,20},{20,16},{24,28},{28,24},{1,5},{5... | collective-permute-start | bytes 3145736 | tf_op jit(solution)/shard_map/ppermute | solution.py:104
  322.4 76.6 %collective-permute-start.58 = (bf16[256,2048]{1,0:T(8,128)(2,1)}, bf16[256,2048]{1,0:T(8,128)(2,1)S(1)}, u32[]{:S(2)}, u32[]{:S(2)}) collective-permute-start(bf16[256,2048]{1,0:T(8,128)(2,1)} %get-tuple-element.350), channel_id=1, source_target_pairs={{0,4},{4,0},{8,12},{12,8},{16,20},{20,16},{24,28},{28,24},{1,5},{5... | collective-permute-start | bytes 3145736 | tf_op jit(solution)/shard_map/ppermute | solution.py:104
  330.8 42.9 %collective-permute-start.65 = (bf16[256,2048]{1,0:T(8,128)(2,1)S(1)}, bf16[256,2048]{1,0:T(8,128)(2,1)S(1)}, u32[]{:S(2)}, u32[]{:S(2)}) collective-permute-start(bf16[256,2048]{1,0:T(8,128)(2,1)S(1)} %pad_maximum_fusion.3), channel_id=1, source_target_pairs={{0,16},{4,20},{8,24},{12,28},{16,0},{20,4},{24,8},{28,12},{1,17},{... | collective-permute-start | bytes 3145736 | tf_op jit(solution)/shard_map/ppermute | solution.py:104
  334.2 40.7 %collective-permute-start.61 = (bf16[256,2048]{1,0:T(8,128)(2,1)S(1)}, bf16[256,2048]{1,0:T(8,128)(2,1)S(1)}, u32[]{:S(2)}, u32[]{:S(2)}) collective-permute-start(bf16[256,2048]{1,0:T(8,128)(2,1)S(1)} %pad_maximum_fusion.2), channel_id=1, source_target_pairs={{0,8},{4,12},{8,0},{12,4},{16,24},{20,28},{24,16},{28,20},{1,9},{5... | collective-permute-start | bytes 3145736 | tf_op jit(solution)/shard_map/ppermute | solution.py:104
  392.7 38.0 %collective-permute-start.84 = (bf16[704,256]{1,0:T(8,128)(2,1)}, bf16[704,256]{1,0:T(8,128)(2,1)S(1)}, u32[]{:S(2)}, u32[]{:S(2)}) collective-permute-start(bf16[704,256]{1,0:T(8,128)(2,1)} %get-tuple-element.404), channel_id=1, source_target_pairs={{0,4},{4,0},{8,12},{12,8},{16,20},{20,16},{24,28},{28,24},{1,5},{5... | collective-permute-start | bytes 1081352 | tf_op jit(solution)/shard_map/ppermute | solution.py:104
  432.8 24.8 %collective-permute-start.93 = (bf16[256,1536]{1,0:T(8,128)(2,1)}, bf16[256,1536]{1,0:T(8,128)(2,1)S(1)}, u32[]{:S(2)}, u32[]{:S(2)}) collective-permute-start(bf16[256,1536]{1,0:T(8,128)(2,1)} %get-tuple-element.424), channel_id=1, source_target_pairs={{0,4},{4,0},{8,12},{12,8},{16,20},{20,16},{24,28},{28,24},{1,5},{5... | collective-permute-start | bytes 2359304 | tf_op jit(solution)/shard_map/ppermute | solution.py:104
  448.5 34.3 %collective-permute-start.98 = (bf16[64,2048]{1,0:T(8,128)(2,1)S(1)}, bf16[64,2048]{1,0:T(8,128)(2,1)S(1)}, u32[]{:S(2)}, u32[]{:S(2)}) collective-permute-start(bf16[64,2048]{1,0:T(8,128)(2,1)S(1)} %pad_maximum_fusion.18), channel_id=1, source_target_pairs={{0,3},{1,0},{2,1},{3,2},{4,7},{5,4},{6,5},{7,6},{8,11},{9,8},{10,9... | collective-permute-start | bytes 786440 | tf_op jit(solution)/shard_map/ppermute | solution.py:181
  448.6 34.2 %collective-permute-start.91 = (bf16[64,2048]{1,0:T(8,128)(2,1)S(1)}, bf16[64,2048]{1,0:T(8,128)(2,1)S(1)}, u32[]{:S(2)}, u32[]{:S(2)}) collective-permute-start(bf16[64,2048]{1,0:T(8,128)(2,1)S(1)} %pad_maximum_fusion.17), channel_id=1, source_target_pairs={{0,1},{1,2},{2,3},{3,0},{4,5},{5,6},{6,7},{7,4},{8,9},{9,10},{10,1... | collective-permute-start | bytes 786440 | tf_op jit(solution)/shard_map/ppermute | solution.py:181
  456.2 24.0 %collective-permute-start.99 = (bf16[704,256]{1,0:T(8,128)(2,1)S(1)}, bf16[704,256]{1,0:T(8,128)(2,1)S(1)}, u32[]{:S(2)}, u32[]{:S(2)}) collective-permute-start(bf16[704,256]{1,0:T(8,128)(2,1)S(1)} %add_convert_fusion.21), channel_id=1, source_target_pairs={{0,2},{1,3},{2,0},{3,1},{4,6},{5,7},{6,4},{7,5},{8,10},{9,11},{10,... | collective-permute-start | bytes 1081352 | tf_op jit(solution)/shard_map/ppermute | solution.py:1782
  (178 other events, 1993.9 us)
